TPU v7x, 32 devices: a whole 2x2x4 slice. The times are simulated.
32 devices in a mesh: row: 8 (over z, y), col: 4 (over x, core).
Axes of the slice: x: 2, y: 2, z: 4, core: 2. Of those that a mesh axis runs over, the one named last changes fastest.
Arguments:
- tokens: bfloat16 [1600, 8192], P('row', 'col')
- ln1_gain: float32 [1600], P('row'), may hold values from 0.25 to 1.75
- ln1_shift: float32 [1600], P('row'), may hold values from -4 to 4
- weight_qkv: bfloat16 [1600, 4800], P('row', 'col'), may hold values from -0.21875 to 0.21875
- bias_qkv: float32 [4800], P('col'), may hold values from -4 to 4
- weight_out: bfloat16 [1600, 1600], P('row', 'col'), may hold values from -0.625 to 0.625
- bias_out: float32 [1600], P('row'), may hold values from -6 to 6
- ln2_gain: float32 [1600], P('row'), may hold values from 0.25 to 1.75
- ln2_shift: float32 [1600], P('row'), may hold values from -4 to 4
- weight_up: bfloat16 [1600, 6400], P('row', 'col'), may hold values from -0.15625 to 0.15625
- bias_up: float32 [6400], P('col'), may hold values from -6 to 6
- weight_down: bfloat16 [1600, 6400], P('row', 'col'), may hold values from -0.109375 to 0.109375
- bias_down: float32 [1600], P('row'), may hold values from -6 to 6
- cotangent: bfloat16 [1600, 8192], P('row', 'col')
Outputs:
- block_output: bfloat16 [1600, 8192], P('row', 'col')
- grad_tokens: float32 [1600, 8192], P('row', 'col')
- grad_ln1_gain: float32 [1600], P('row')
- grad_ln1_shift: float32 [1600], P('row')
- grad_weight_qkv: float32 [1600, 4800], P('row', 'col')
- grad_bias_qkv: float32 [4800], P('col')
- grad_weight_out: float32 [1600, 1600], P('row', 'col')
- grad_bias_out: float32 [1600], P('row')
- grad_ln2_gain: float32 [1600], P('row')
- grad_ln2_shift: float32 [1600], P('row')
- grad_weight_up: float32 [1600, 6400], P('row', 'col')
- grad_bias_up: float32 [6400], P('col')
- grad_weight_down: float32 [1600, 6400], P('row', 'col')
- grad_bias_down: float32 [1600], P('row')
All inputs are finite; a program needn't handle non-finite values.
Results may differ from a plain program's by a relative error of at most 0.012.
The roundings to bfloat16 on the way count: a program that leaves them out, or rounds other values in their place, can miss the bound.
Values may be sent and summed in bfloat16 or wider, within the bound.
A program may use at most 256 MiB of HBM per device.

v0:
```python
import jax
import jax.numpy as jnp
from jax import lax
from jax.sharding import PartitionSpec as P

D = 1600
H = 25
HD = 64
L = 1024
SEQ_ROW = 1


epsilon = 1e-05
excluded = -1e30


def row_totals(first_sum, second_sum):
    return lax.psum((first_sum, second_sum), "row")


def norm_forward(values, norm_gain, norm_shift):
    row_sum, row_squares = row_totals(jnp.sum(values, axis=0), jnp.sum(values * values, axis=0))
    row_mean = row_sum / D
    row_scale = lax.rsqrt(row_squares / D - row_mean * row_mean + epsilon)
    centred = (values - row_mean[None, :]) * row_scale[None, :]
    return (
        (centred * norm_gain[:, None] + norm_shift[:, None]).astype(jnp.bfloat16),
        centred,
        row_scale,
    )


def norm_backward(gradient, centred, row_scale, norm_gain):
    scaled = gradient * norm_gain[:, None]
    first_sum, second_sum = row_totals(jnp.sum(scaled, axis=0), jnp.sum(scaled * centred, axis=0))
    adjusted = scaled - first_sum[None, :] / D - centred * (second_sum[None, :] / D)
    return (
        adjusted * row_scale[None, :],
        jnp.sum(gradient * centred, axis=1),
        jnp.sum(gradient, axis=1),
    )


def spread_cols(values):
    return lax.all_gather(values, "col", axis=1, tiled=True)


def row_terms(gathered, weight):
    return lax.psum_scatter(
        lax.dot_general(
            gathered, weight, (((0,), (0,)), ((), ())), preferred_element_type=jnp.float32
        ),
        "row",
        scatter_dimension=0,
        tiled=True,
    )


def project_rows(gathered, weight):
    return row_terms(gathered, weight)


def share_cols(full_cols):
    return lax.psum_scatter(full_cols, "col", scatter_dimension=1, tiled=True)


def cross_products(values, weight):
    return share_cols(
        lax.dot_general(
            weight,
            lax.all_gather(values, "row", axis=0, tiled=True),
            (((1,), (1,)), ((), ())),
            preferred_element_type=jnp.float32,
        )
    )


def fold_rows(gradient, weight, gathered):

    def accumulate(running, block_rows, offset):
        through = lax.dot_general(
            weight, block_rows, (((1,), (1,)), ((), ())), preferred_element_type=jnp.float32
        )
        weight_grad = jnp.dot(gathered, block_rows, preferred_element_type=jnp.float32)
        return (through, weight_grad)

    initial = (
        jnp.zeros((weight.shape[0], gathered.shape[1]), jnp.float32),
        jnp.zeros(weight.shape, jnp.float32),
    )
    return accumulate(initial, lax.all_gather(gradient, "row", axis=0, tiled=True), jnp.int32(0))


def fold_again(values, gathered):

    def accumulate(running, block_rows, offset):
        return jnp.dot(gathered, block_rows, preferred_element_type=jnp.float32)

    initial = jnp.zeros((gathered.shape[0], values.shape[1]), jnp.float32)
    return accumulate(initial, lax.all_gather(values, "row", axis=0, tiled=True), jnp.int32(0))


def build_slots():
    col_count = lax.axis_size("col")
    unit_count = SEQ_ROW * H
    slot_count = (unit_count + col_count - 1) // col_count
    column_ids = jnp.arange(col_count, dtype=jnp.int32)[:, None]
    slot_ids = jnp.arange(slot_count, dtype=jnp.int32)[None, :]
    numbered = slot_ids * col_count + column_ids
    return jnp.where(numbered < unit_count, numbered, -1)


def slot_matrix(slot_table):
    return (
        slot_table.reshape(-1)[:, None] == jnp.arange(SEQ_ROW * H, dtype=jnp.int32)[None, :]
    ).astype(jnp.bfloat16)


def to_units(values, slot_table):
    channels = values.shape[1] // H
    by_unit = (
        values.reshape(SEQ_ROW, L, channels, H)
        .transpose(0, 3, 1, 2)
        .reshape(SEQ_ROW * H, L * channels)
    )
    outgoing = jnp.dot(slot_matrix(slot_table), by_unit, preferred_element_type=jnp.float32).astype(
        jnp.bfloat16
    )
    outgoing = outgoing.reshape(slot_table.shape[0], slot_table.shape[1], L, channels)
    return lax.all_to_all(outgoing, "col", split_axis=0, concat_axis=3, tiled=True)[0]


def to_tokens(unit_values, slot_table):
    returned = lax.all_to_all(unit_values[None], "col", split_axis=3, concat_axis=0, tiled=True)
    channels = returned.shape[3]
    flat = returned.reshape(slot_table.shape[0] * slot_table.shape[1], L * channels)
    placed = lax.dot_general(
        slot_matrix(slot_table), flat, (((0,), (0,)), ((), ())), preferred_element_type=jnp.float32
    )
    placed = placed.astype(jnp.bfloat16).reshape(SEQ_ROW, H, L, channels)
    return placed.transpose(0, 2, 3, 1).reshape(SEQ_ROW * L, channels * H)


def causal_mask():
    return jnp.arange(L)[:, None] >= jnp.arange(L)[None, :]


def attend_forward(unit_data):
    score_scale = HD ** (-0.5)
    allowed = causal_mask()

    def per_unit(unit_rows):
        query_rows = unit_rows[:, :HD]
        key_rows = unit_rows[:, HD : 2 * HD]
        value_rows = unit_rows[:, 2 * HD :]
        scores = (
            lax.dot_general(
                query_rows, key_rows, (((1,), (1,)), ((), ())), preferred_element_type=jnp.float32
            )
            * score_scale
        )
        scores = jnp.where(allowed, scores, excluded)
        peak = jnp.max(scores, axis=1, keepdims=True)
        weights = jnp.exp(scores - peak)
        row_total = jnp.sum(weights, axis=1, keepdims=True)
        weights_low = (weights / row_total).astype(jnp.bfloat16)
        attended = jnp.dot(weights_low, value_rows, preferred_element_type=jnp.float32).astype(
            jnp.bfloat16
        )
        return (attended, (peak + jnp.log(row_total))[:, 0])

    return lax.map(per_unit, unit_data)


def attend_backward(unit_data, grad_units, log_totals):
    score_scale = HD ** (-0.5)
    allowed = causal_mask()

    def per_unit(inputs):
        unit_rows, grad_rows, log_row = inputs
        query_rows = unit_rows[:, :HD]
        key_rows = unit_rows[:, HD : 2 * HD]
        value_rows = unit_rows[:, 2 * HD :]
        scores = (
            lax.dot_general(
                query_rows, key_rows, (((1,), (1,)), ((), ())), preferred_element_type=jnp.float32
            )
            * score_scale
        )
        scores = jnp.where(allowed, scores, excluded)
        weights = jnp.exp(scores - log_row[:, None])
        weights_low = weights.astype(jnp.bfloat16)
        grad_value = lax.dot_general(
            weights_low, grad_rows, (((0,), (0,)), ((), ())), preferred_element_type=jnp.float32
        )
        grad_weights = lax.dot_general(
            grad_rows, value_rows, (((1,), (1,)), ((), ())), preferred_element_type=jnp.float32
        )
        grad_scores = weights * (
            grad_weights - jnp.sum(weights * grad_weights, axis=1, keepdims=True)
        )
        grad_low = grad_scores.astype(jnp.bfloat16)
        grad_query = jnp.dot(grad_low, key_rows, preferred_element_type=jnp.float32) * score_scale
        grad_key = (
            lax.dot_general(
                grad_low, query_rows, (((0,), (0,)), ((), ())), preferred_element_type=jnp.float32
            )
            * score_scale
        )
        return jnp.concatenate([grad_query, grad_key, grad_value], axis=1).astype(jnp.bfloat16)

    return lax.map(per_unit, (unit_data, grad_units, log_totals))


def body(
    tokens,
    ln1_gain,
    ln1_shift,
    weight_qkv,
    bias_qkv,
    weight_out,
    bias_out,
    ln2_gain,
    ln2_shift,
    weight_up,
    bias_up,
    weight_down,
    bias_down,
    cotangent,
):
    slot_table = build_slots()
    residual_in = tokens.astype(jnp.float32)
    normed_in, centred_in, scale_in = norm_forward(residual_in, ln1_gain, ln1_shift)
    normed_wide = spread_cols(normed_in)
    qkv_rows = (project_rows(normed_wide, weight_qkv) + bias_qkv).astype(jnp.bfloat16)
    unit_data = to_units(qkv_rows, slot_table)
    attended_units, log_totals = attend_forward(unit_data)
    attended_rows = to_tokens(attended_units, slot_table)
    residual_mid = residual_in + cross_products(attended_rows, weight_out) + bias_out[:, None]
    normed_mid, centred_mid, scale_mid = norm_forward(residual_mid, ln2_gain, ln2_shift)
    mid_wide = spread_cols(normed_mid)
    hidden_pre = project_rows(mid_wide, weight_up) + bias_up
    hidden_rows = jax.nn.gelu(hidden_pre, approximate=True).astype(jnp.bfloat16)
    block_output = (
        residual_mid + cross_products(hidden_rows, weight_down) + bias_down[:, None]
    ).astype(jnp.bfloat16)
    grad_wide = spread_cols(cotangent)
    grad_bias_down = jnp.sum(grad_wide, axis=1, dtype=jnp.float32)
    grad_hidden = project_rows(grad_wide, weight_down)
    unused_value, gelu_back = jax.vjp(
        lambda inner: jax.nn.gelu(inner, approximate=True), hidden_pre
    )
    grad_pre = gelu_back(grad_hidden)[0].astype(jnp.bfloat16)
    up_part = jnp.sum(grad_pre, axis=0, dtype=jnp.float32)
    mid_full, grad_weight_up = fold_rows(grad_pre, weight_up, mid_wide)
    grad_normed_mid = share_cols(mid_full)
    grad_norm_mid, gain_two_part, shift_two_part = norm_backward(
        grad_normed_mid, centred_mid, scale_mid, ln2_gain
    )
    grad_residual_mid = cotangent.astype(jnp.float32) + grad_norm_mid
    grad_branch = grad_residual_mid.astype(jnp.bfloat16)
    branch_wide = spread_cols(grad_branch)
    grad_bias_out = jnp.sum(branch_wide, axis=1, dtype=jnp.float32)
    grad_attended = project_rows(branch_wide, weight_out).astype(jnp.bfloat16)
    grad_units = to_units(grad_attended, slot_table)
    grad_unit_qkv = attend_backward(unit_data, grad_units, log_totals)
    grad_qkv_rows = to_tokens(grad_unit_qkv, slot_table)
    qkv_part = jnp.sum(grad_qkv_rows, axis=0, dtype=jnp.float32)
    in_full, grad_weight_qkv = fold_rows(grad_qkv_rows, weight_qkv, normed_wide)
    grad_normed_in = share_cols(in_full)
    grad_norm_in, gain_one_part, shift_one_part = norm_backward(
        grad_normed_in, centred_in, scale_in, ln1_gain
    )
    grad_tokens = grad_residual_mid + grad_norm_in
    grad_weight_down = fold_again(hidden_rows, grad_wide)
    grad_weight_out = fold_again(attended_rows, branch_wide)
    grad_bias_up, grad_bias_qkv = lax.psum((up_part, qkv_part), "row")
    grad_ln1_gain, grad_ln1_shift, grad_ln2_gain, grad_ln2_shift = lax.psum(
        (gain_one_part, shift_one_part, gain_two_part, shift_two_part), "col"
    )
    return (
        block_output,
        grad_tokens,
        grad_ln1_gain,
        grad_ln1_shift,
        grad_weight_qkv,
        grad_bias_qkv,
        grad_weight_out,
        grad_bias_out,
        grad_ln2_gain,
        grad_ln2_shift,
        grad_weight_up,
        grad_bias_up,
        grad_weight_down,
        grad_bias_down,
    )


def solution(mesh):
    in_specs = (
        P("row", "col"),
        P("row"),
        P("row"),
        P("row", "col"),
        P("col"),
        P("row", "col"),
        P("row"),
        P("row"),
        P("row"),
        P("row", "col"),
        P("col"),
        P("row", "col"),
        P("row"),
        P("row", "col"),
    )
    out_specs = (
        P("row", "col"),
        P("row", "col"),
        P("row"),
        P("row"),
        P("row", "col"),
        P("col"),
        P("row", "col"),
        P("row"),
        P("row"),
        P("row"),
        P("row", "col"),
        P("col"),
        P("row", "col"),
        P("row"),
    )
    return jax.shard_map(body, mesh=mesh, in_specs=in_specs, out_specs=out_specs, check_vma=False)
```

profile of v0, /device:TPU:9, one launch (start us, length us, event | category | flops | bytes accessed | tf_op | source)
XLA Modules:
  0.0 4898.5 jit_solution(17613472183118926545)
XLA Ops:
  8.7 27.4 all-reduce.3
  39.3 36.9 all-gather.9.cloned.1.call-done
  76.2 17.4 fusion.69
  93.7 623.5 %reduce-scatter.9.cloned.1.call-done = f32[1024,1200]{0,1:T(8,128)} async-done(((f32[8192,1200]{0,1:T(8,128)}), f32[1024,1200]{0,1:T(8,128)}) %reduce-scatter.9.cloned.1.call-update) | async-done | bytes 4915216 | tf_op jit(solution)/shard_map/reduce_scatter | solution.py:49
  722.5 8.2 copy.41
  730.6 18.4 reshape.182
  749.0 4.6 convolution_convert_fusion.1
  753.6 9.4 reshape.183
  763.0 7.6 copy.42
  770.7 4.7 all-to-all-start
  775.3 31.9 all-to-all-done
  809.1 6.0 copy.44
  815.1 51.8 %while.24 = (s32[]{:T(128)}, bf16[7,1024,64]{1,2,0:T(8,128)(2,1)S(1)}, f32[7,1024]{1,0:T(8,128)S(1)}, bf16[7,1024,192]{2,1,0:T(8,128)(2,1)}, s32[]{:T(128)}, /*index=5*/s32[]{:T(128)}) while((s32[]{:T(128)}, bf16[7,1024,64]{1,2,0:T(8,128)(2,1)S(1)}, f32[7,1024]{1,0:T(8,128)S(1)}, bf16[7,1024,192]{2,1,0:T(8,128)(2,1)}, s32[]{:T(128)}, ...), condition=%wide.region_8.9_spmd.clone, body=%wide.region_5.8_spmd.clone.sunk | while | flops 284228608 | bytes 30974060 | solution.py:172
  867.4 16.7 all_to_all.60
  884.1 5.3 copy.46
  889.4 16.8 reshape.184
  906.7 6.5 reshape.185
  913.2 6.9 copy.47
  921.7 99.6 %all-gather.11.cloned.1.call-done = bf16[8192,400]{0,1:T(8,128)(2,1)} async-done(((bf16[1024,400]{0,1:T(8,128)(2,1)}), bf16[8192,400]{0,1:T(8,128)(2,1)}) %all-gather.11.cloned.1.call-update) | async-done | bytes 6553616 | tf_op jit(solution)/shard_map/all_gather | solution.py:71
  1021.3 7.5 convolution_bitcast_fusion.1
  1029.5 60.1 %reduce-scatter.11.cloned.1.call-done = f32[200,2048]{1,0:T(8,128)} async-done(((f32[200,8192]{1,0:T(8,128)}), f32[200,2048]{1,0:T(8,128)}) %reduce-scatter.11.cloned.1.call-update) | async-done | bytes 1638416 | tf_op jit(solution)/shard_map/reduce_scatter | solution.py:64
  1091.4 27.5 all-reduce.2
  1120.7 23.0 fusion.71
  1143.7 12.3 all-gather.13.cloned.1.call-done
  1156.0 22.9 fusion.70
  1179.1 799.9 %reduce-scatter.17.cloned.1.call-done = f32[1024,1600]{0,1:T(8,128)} async-done(((f32[8192,1600]{0,1:T(8,128)}), f32[1024,1600]{0,1:T(8,128)}) %reduce-scatter.17.cloned.1.call-update) | async-done | bytes 6553616 | tf_op jit(solution)/shard_map/reduce_scatter | solution.py:49
  1979.0 824.9 %reduce-scatter.13.cloned.1.call-done = f32[1024,1600]{0,1:T(8,128)} async-done(((f32[8192,1600]{0,1:T(8,128)}), f32[1024,1600]{0,1:T(8,128)}) %reduce-scatter.13.cloned.1.call-update) | async-done | bytes 6553616 | tf_op jit(solution)/shard_map/reduce_scatter | solution.py:49
  2803.9 10.7 convert_reduce_fusion.2
  2814.7 501.3 %all-gather.19.cloned.1.call-done = bf16[8192,1600]{0,1:T(8,128)(2,1)} async-done(((bf16[1024,1600]{0,1:T(8,128)(2,1)}), bf16[8192,1600]{0,1:T(8,128)(2,1)}) %all-gather.19.cloned.1.call-update) | async-done | bytes 26214416 | tf_op jit(solution)/shard_map/all_gather | solution.py:91
  3316.1 13.3 convolution_bitcast_fusion.2
  3329.4 60.0 %reduce-scatter.19.cloned.1.call-done = f32[200,2048]{1,0:T(8,128)} async-done(((f32[200,8192]{1,0:T(8,128)}), f32[200,2048]{1,0:T(8,128)}) %reduce-scatter.19.cloned.1.call-update) | async-done | bytes 1638416 | tf_op jit(solution)/shard_map/reduce_scatter | solution.py:64
  3392.3 27.2 all-reduce.1
  3422.7 35.8 all-gather.21.cloned.1.call-done
  3458.5 8.5 fusion.72
  3467.1 212.8 %reduce-scatter.21.cloned.1.call-done = f32[1024,400]{0,1:T(8,128)} async-done(((f32[8192,400]{0,1:T(8,128)}), f32[1024,400]{0,1:T(8,128)}) %reduce-scatter.21.cloned.1.call-update) | async-done | bytes 1638416 | tf_op jit(solution)/shard_map/reduce_scatter | solution.py:49
  3681.7 5.4 copy.48
  3687.1 16.6 reshape.188
  3704.2 6.9 reshape.189
  3711.1 6.6 copy.49
  3717.8 4.1 all-to-all-start.2
  3722.1 11.9 all-to-all-done.2
  3734.2 49.8 %while.25 = (s32[]{:T(128)}, bf16[7,1024,192]{1,2,0:T(8,128)(2,1)}, bf16[7,1024,192]{2,1,0:T(8,128)(2,1)}, f32[7,1024]{1,0:T(8,128)S(1)}, bf16[7,1024,64]{1,2,0:T(8,128)(2,1)S(1)}, /*index=5*/s32[]{:T(128)}) while((s32[]{:T(128)}, bf16[7,1024,192]{1,2,0:T(8,128)(2,1)}, bf16[7,1024,192]{2,1,0:T(8,128)(2,1)}, ...), condition=%wide.region_25.26_spmd.clone, body=%wide.region_23.25_spmd.clone.sunk | while | flops 683080704 | bytes 34886228 | solution.py:212
  3783.9 3.3 copy.60
  3787.3 40.5 all_to_all.61
  3827.8 8.3 copy.54
  3836.1 18.5 reshape.190
  3854.6 4.8 convolution_convert_fusion
  3859.4 8.7 reshape.191
  3868.1 8.8 copy.55
  3876.9 4.5 reshape.192
  3882.2 377.2 %all-gather.23.cloned.1.call-done = bf16[8192,1200]{0,1:T(8,128)(2,1)} async-done(((bf16[1024,1200]{0,1:T(8,128)(2,1)}), bf16[8192,1200]{0,1:T(8,128)(2,1)}) %all-gather.23.cloned.1.call-update) | async-done | bytes 19660816 | tf_op jit(solution)/shard_map/all_gather | solution.py:91
  4259.5 13.8 convolution_bitcast_fusion
  4273.4 487.6 %all-gather.15.cloned.1.call-done = bf16[8192,1600]{0,1:T(8,128)(2,1)} async-done(((bf16[1024,1600]{0,1:T(8,128)(2,1)}), bf16[8192,1600]{0,1:T(8,128)(2,1)}) %all-gather.15.cloned.1.call-update) | async-done | bytes 26214416 | tf_op jit(solution)/shard_map/all_gather | solution.py:71
  4761.0 13.8 convolution_bitcast_fusion.3
  4774.9 3.4 convert_reduce_fusion.1
  4778.2 15.1 convolution_bitcast_fusion.4
  4793.3 15.6 fusion.75
  4808.9 3.2 convert_reduce_fusion.3
  4812.1 7.1 fusion.74
  4820.9 11.9 fusion.73
  4835.3 6.0 all-reduce.4
  4841.2 27.6 all-reduce
  4868.8 17.2 reduce-scatter.15.cloned.1.call-done
  4886.1 5.5 fusion.57
  (262 shorter events, 133.9 us)
Async XLA Ops:
  7.2 1148.8 %copy-start = (bf16[200,1600]{1,0:T(8,128)(2,1)S(1)}, bf16[200,1600]{1,0:T(8,128)(2,1)}, u32[]{:S(2)}) copy-start(bf16[200,1600]{1,0:T(8,128)(2,1)} %param.27) | copy-start | bytes 1920004
  7.2 69.0 %copy-start.12 = (bf16[200,1200]{1,0:T(8,128)(2,1)S(1)}, bf16[200,1200]{1,0:T(8,128)(2,1)}, u32[]{:S(2)}) copy-start(bf16[200,1200]{1,0:T(8,128)(2,1)} %param.21) | copy-start | bytes 1440004
  7.2 69.0 %all-gather.9.cloned.1.call-start = ((), (), s32[]{:S(2)}) async-start(), calls=%async_computation.12 | async-start | bytes 4096000 | tf_op jit(solution)/shard_map/all_gather | solution.py:45
  36.2 0.6 copy-start.18
  36.2 0.6 copy-start.20
  39.2 677.9 %reduce-scatter.9.cloned.1.call-start = ((), (), s32[]{:S(2)}) async-start(), calls=%async_computation.13 | async-start | bytes 44236800 | tf_op jit(solution)/shard_map/reduce_scatter | solution.py:49
  93.6 623.6 %copy-start.31 = (f32[1200]{0:T(1024)S(1)}, f32[1200]{0:T(1024)}, u32[]{:S(2)}) copy-start(f32[1200]{0:T(1024)} %param.22) | copy-start | bytes 14404
  770.7 36.5 all-to-all-start
  775.3 246.0 %all-gather.11.cloned.1.call-start = ((), (), s32[]{:S(2)}) async-start(), calls=%async_computation.14 | async-start | bytes 7372800 | tf_op jit(solution)/shard_map/all_gather | solution.py:71
  809.1 6.0 copy-start.9
  817.0 2.0 copy-start.2
  824.4 2.0 copy-start.2
  831.7 2.0 copy-start.2
  839.1 2.0 copy-start.2
  846.5 2.0 copy-start.2
  853.9 2.0 copy-start.2
  861.3 2.0 copy-start.2
  913.2 108.2 %copy-start.10 = (bf16[200,400]{1,0:T(8,128)(2,1)S(1)}, bf16[200,400]{1,0:T(8,128)(2,1)}, u32[]{:S(2)}) copy-start(bf16[200,400]{1,0:T(8,128)(2,1)} %param.23) | copy-start | bytes 480004
  921.3 168.3 %reduce-scatter.11.cloned.1.call-start = ((), (), s32[]{:S(2)}) async-start(), calls=%async_computation.15 | async-start | bytes 8192000 | tf_op jit(solution)/shard_map/reduce_scatter | solution.py:64
  1028.8 60.8 %copy-start.5 = (bf16[200,2048]{1,0:T(8,128)(2,1)S(1)}, bf16[200,2048]{1,0:T(8,128)(2,1)}, u32[]{:S(2)}) copy-start(bf16[200,2048]{1,0:T(8,128)(2,1)} %param.18) | copy-start | bytes 2457604
  1028.8 60.8 %copy-start.34 = (f32[200]{0:T(256)S(1)}, f32[200]{0:T(256)}, u32[]{:S(2)}) copy-start(f32[200]{0:T(256)} %param.24) | copy-start | bytes 2404
  1028.8 90.1 %copy-start.27 = (f32[200]{0:T(256)S(1)}, f32[200]{0:T(256)}, u32[]{:S(2)}) copy-start(f32[200]{0:T(256)} %param.25) | copy-start | bytes 2404
  1028.8 90.1 %copy-start.35 = (f32[200]{0:T(256)S(1)}, f32[200]{0:T(256)}, u32[]{:S(2)}) copy-start(f32[200]{0:T(256)} %param.26) | copy-start | bytes 2404
  1028.8 91.8 %all-gather.17.cloned.1.call-start = ((), (), s32[]{:S(2)}) async-start(), calls=%async_computation.20 | async-start | bytes 4096000 | tf_op jit(solution)/shard_map/all_gather | solution.py:45
  1029.4 126.6 %all-gather.13.cloned.1.call-start = ((), (), s32[]{:S(2)}) async-start(), calls=%async_computation.16 | async-start | bytes 4096000 | tf_op jit(solution)/shard_map/all_gather | solution.py:45
  1091.4 2328.1 %copy-start.3 = (f32[200,2048]{1,0:T(8,128)}, f32[200,2048]{1,0:T(8,128)S(1)}, u32[]{:S(2)}) copy-start(f32[200,2048]{1,0:T(8,128)S(1)} %get-tuple-element.163) | copy-start | bytes 4915204
  1118.9 2300.5 %copy-start.14 = (f32[2048]{0:T(1024)}, f32[2048]{0:T(1024)S(1)}, u32[]{:S(2)}) copy-start(f32[2048]{0:T(1024)S(1)} %get-tuple-element.171) | copy-start | bytes 24580
  1118.9 2300.5 %copy-start.16 = (f32[2048]{0:T(1024)}, f32[2048]{0:T(1024)S(1)}, u32[]{:S(2)}) copy-start(f32[2048]{0:T(1024)S(1)} %get-tuple-element.172) | copy-start | bytes 24580
  1120.2 858.7 %reduce-scatter.17.cloned.1.call-start = ((), (), s32[]{:S(2)}) async-start(), calls=%async_computation.21 | async-start | bytes 58982400 | tf_op jit(solution)/shard_map/reduce_scatter | solution.py:49
  1143.7 1660.3 %reduce-scatter.13.cloned.1.call-start = ((), (), s32[]{:S(2)}) async-start(), calls=%async_computation.17 | async-start | bytes 58982400 | tf_op jit(solution)/shard_map/reduce_scatter | solution.py:49
  1178.9 1625.1 %copy-start.30 = (f32[1600]{0:T(1024)S(1)}, f32[1600]{0:T(1024)}, u32[]{:S(2)}) copy-start(f32[1600]{0:T(1024)} %param.28) | copy-start | bytes 19204
  1178.9 2137.2 %all-gather.19.cloned.1.call-start = ((), (), s32[]{:S(2)}) async-start(), calls=%async_computation.22 | async-start | bytes 29491200 | tf_op jit(solution)/shard_map/all_gather | solution.py:91
  2814.7 574.7 %reduce-scatter.19.cloned.1.call-start = ((), (), s32[]{:S(2)}) async-start(), calls=%async_computation.23 | async-start | bytes 8192000 | tf_op jit(solution)/shard_map/reduce_scatter | solution.py:64
  3329.4 90.1 %copy-start.8 = (bf16[200,2048]{1,0:T(8,128)(2,1)S(1)}, bf16[200,2048]{1,0:T(8,128)(2,1)}, u32[]{:S(2)}) copy-start(bf16[200,2048]{1,0:T(8,128)(2,1)} %param.31) | copy-start | bytes 2457604
  3329.4 129.1 %all-gather.21.cloned.1.call-start = ((), (), s32[]{:S(2)}) async-start(), calls=%async_computation.24 | async-start | bytes 4096000 | tf_op jit(solution)/shard_map/all_gather | solution.py:45
  3419.5 47.6 copy-start.22
  3419.5 47.6 copy-start.24
  3422.5 257.4 %reduce-scatter.21.cloned.1.call-start = ((), (), s32[]{:S(2)}) async-start(), calls=%async_computation.25 | async-start | bytes 14745600 | tf_op jit(solution)/shard_map/reduce_scatter | solution.py:49
  3717.8 16.3 all-to-all-start.2
  3721.9 537.6 %all-gather.23.cloned.1.call-start = ((), (), s32[]{:S(2)}) async-start(), calls=%async_computation.26 | async-start | bytes 22118400 | tf_op jit(solution)/shard_map/all_gather | solution.py:91
  3881.4 378.1 %copy-start.13 = (bf16[200,1200]{1,0:T(8,128)(2,1)S(1)}, bf16[200,1200]{1,0:T(8,128)(2,1)}, u32[]{:S(2)}) copy-start(bf16[200,1200]{1,0:T(8,128)(2,1)} %param.21) | copy-start | bytes 1440004
  3881.4 879.6 %all-gather.15.cloned.1.call-start = ((), (), s32[]{:S(2)}) async-start(), calls=%async_computation.18 | async-start | bytes 29491200 | tf_op jit(solution)/shard_map/all_gather | solution.py:71
  3882.0 950.7 %reduce-scatter.23.cloned.1.call-start = ((), (), s32[]{:S(2)}) async-start(), calls=%async_computation.27 | async-start | bytes 8192000 | tf_op jit(solution)/shard_map/reduce_scatter | solution.py:64
  4273.3 487.7 %copy-start.11 = (bf16[200,1600]{1,0:T(8,128)(2,1)S(1)}, bf16[200,1600]{1,0:T(8,128)(2,1)}, u32[]{:S(2)}) copy-start(bf16[200,1600]{1,0:T(8,128)(2,1)} %param.29) | copy-start | bytes 1920004
  4273.3 612.7 %reduce-scatter.15.cloned.1.call-start = ((), (), s32[]{:S(2)}) async-start(), calls=%async_computation.19 | async-start | bytes 8192000 | tf_op jit(solution)/shard_map/reduce_scatter | solution.py:64
  4774.8 3.4 copy-start.7
  4808.9 10.3 slice-start
  4812.1 7.1 slice-start.1
  4820.7 12.0 copy-start.6
  4820.7 12.0 copy-start.19
  4820.7 12.0 copy-start.21
  4820.8 12.0 copy-start.29
  4820.8 14.5 copy-start.32
  4820.8 14.5 copy-start.33
  4820.8 20.5 copy-start.26
  4820.8 65.2 %copy-start.15 = (f32[2048]{0:T(1024)S(1)}, f32[2048]{0:T(1024)}, u32[]{:S(2)}) copy-start(f32[2048]{0:T(1024)} %copy-done.14) | copy-start | bytes 24580
  4820.8 65.2 %copy-start.17 = (f32[2048]{0:T(1024)S(1)}, f32[2048]{0:T(1024)}, u32[]{:S(2)}) copy-start(f32[2048]{0:T(1024)} %copy-done.16) | copy-start | bytes 24580
  4820.8 65.2 %copy-start.23 = (f32[2048]{0:T(1024)S(1)}, f32[2048]{0:T(1024)}, u32[]{:S(2)}) copy-start(f32[2048]{0:T(1024)} %copy-done.22) | copy-start | bytes 24580
  4820.8 65.2 %copy-start.25 = (f32[2048]{0:T(1024)S(1)}, f32[2048]{0:T(1024)}, u32[]{:S(2)}) copy-start(f32[2048]{0:T(1024)} %copy-done.24) | copy-start | bytes 24580
  4820.8 65.2 %copy-start.28 = (f32[200]{0:T(256)S(1)}, f32[200]{0:T(256)}, u32[]{:S(2)}) copy-start(f32[200]{0:T(256)} %param.25) | copy-start | bytes 2404
  4820.9 65.2 %copy-start.36 = (f32[200]{0:T(256)S(1)}, f32[200]{0:T(256)}, u32[]{:S(2)}) copy-start(f32[200]{0:T(256)} %param.30) | copy-start | bytes 2404
  4832.8 53.3 %copy-start.4 = (f32[200,2048]{1,0:T(8,128)S(1)}, f32[200,2048]{1,0:T(8,128)}, u32[]{:S(2)}) copy-start(f32[200,2048]{1,0:T(8,128)} %copy-done.3) | copy-start | bytes 4915204
  4868.8 22.8 copy-start.1
Sparse Core Ops, SparseCore 0:
  39.3 36.7 all-gather.8
  93.7 623.4 reduce-scatter.8
  921.4 99.8 all-gather.10
  1028.9 60.5 reduce-scatter.10
  1091.0 29.6 all-gather.16
  1122.7 33.2 all-gather.12
  1159.9 819.0 reduce-scatter.16
  1983.4 820.4 reduce-scatter.12
  2814.8 501.2 all-gather.18
  3329.5 59.8 reduce-scatter.18
  3422.6 35.8 all-gather.20
  3467.2 212.6 reduce-scatter.20
  3881.6 377.8 all-gather.22
  4260.9 500.0 all-gather.14
  4763.6 59.8 reduce-scatter.22
  4825.9 60.1 reduce-scatter.14
where the time goes:
time: 4910 us; the launch traced here: 4900 us
  waiting for transfers between devices  4190 us (85%)
  matrix products  235 us (5%)
  local copies, waits for them, and re-layouts  210 us (4%)
  blocking collectives  173 us (4%)
  other arithmetic  60.8 us (1%)
    reduce_scatter x4, waiting for transfers between devices, row_terms(): lax.psum_scatter(lax.dot_general(gathered, weight, (((0,), (0,)), ((), ()...  2460 us
    all_gather x2, waiting for transfers between devices, fold_rows(): lax.all_gather(gradient, 'row', axis=0, tiled=True)  879 us
    all_gather x2, waiting for transfers between devices, cross_products(): lax.all_gather(values, 'row', axis=0, tiled=True)  587 us
    reduce_scatter x4, waiting for transfers between devices, share_cols(): return lax.psum_scatter(full_cols, 'col', scatter_dimension=1, tiled=True)  137 us
    psum x4, blocking collectives, row_totals(): return lax.psum((first_sum, second_sum), 'row')  110 us
  transfers between devices with their start and end apart: 18, of which 17 were waited for; matrix products, arithmetic and copies ran while one was open for 3% of the time, Pallas kernels for 0%

commit v1 on v0

v1 whole, which is shorter than its diff:
```python
import jax
import jax.numpy as jnp
from jax import lax
from jax.sharding import PartitionSpec as P

D = 1600
H = 25
HD = 64
L = 1024
CHANNELS = 3 * HD

epsilon = 1e-05
excluded = -1e30

TN = (((0,), (0,)), ((), ()))
NN = (((1,), (0,)), ((), ()))
NT = (((1,), (1,)), ((), ()))


def product(left, right, dims):
    return lax.dot_general(left, right, dims, preferred_element_type=jnp.float32)


def norm_stats(values):
    mean = jnp.mean(values, axis=0, keepdims=True)
    centred = values - mean
    scale = lax.rsqrt(jnp.mean(centred * centred, axis=0, keepdims=True) + epsilon)
    return centred * scale, scale


def norm_backward(gradient, centred, scale, gain):
    scaled = gradient * gain
    adjusted = (
        scaled
        - jnp.mean(scaled, axis=0, keepdims=True)
        - centred * jnp.mean(scaled * centred, axis=0, keepdims=True)
    )
    return adjusted * scale, jnp.sum(gradient * centred, axis=1), jnp.sum(gradient, axis=1)


def block_order(rows, cols):
    return [(q * cols + c, c * rows + q) for q in range(rows) for c in range(cols)]


def to_blocks(values, rows, cols):
    k, feats, toks = values.shape
    split = values.reshape(k, feats, rows, toks // rows)
    got = lax.all_to_all(split, "row", split_axis=2, concat_axis=1)
    got = got.reshape(k, rows * feats, toks // rows)
    return lax.ppermute(got, ("row", "col"), block_order(rows, cols))


def from_blocks(values, rows, cols):
    back = [(b, a) for a, b in block_order(rows, cols)]
    got = lax.ppermute(values, ("row", "col"), back)
    feats, toks = values.shape
    got = got.reshape(rows, feats // rows, toks)
    got = lax.all_to_all(got, "row", split_axis=0, concat_axis=1)
    return got.reshape(feats // rows, rows * toks)


def regroup_matrix(channels, slots, cols):
    source = jnp.arange(channels * H, dtype=jnp.int32)
    channel, head = source // H, source % H
    target = ((head % cols) * slots + head // cols) * channels + channel
    return (
        target[:, None] == jnp.arange(cols * slots * channels, dtype=jnp.int32)[None, :]
    ).astype(jnp.bfloat16)


def group_heads(weight, matrix, cols):
    moved = product(weight, matrix, NN).astype(jnp.bfloat16)
    moved = moved.reshape(moved.shape[0], cols, -1)
    got = lax.all_to_all(moved, "col", split_axis=1, concat_axis=1, tiled=True)
    return got.reshape(got.shape[0], -1)


def ungroup_heads(gradient, matrix, cols):
    moved = gradient.reshape(gradient.shape[0], cols, -1)
    got = lax.all_to_all(moved, "col", split_axis=1, concat_axis=1, tiled=True)
    return product(got.reshape(got.shape[0], -1), matrix, NT)


def head_rows(values, cols, slots):
    rest = values.shape[1:]
    split = values.reshape(cols, slots, -1, *rest)
    return jnp.moveaxis(split, 0, 1).reshape(slots, -1, *rest)


def flat_rows(values, cols, slots):
    rest = values.shape[2:]
    split = values.reshape(slots, cols, -1, *rest)
    return jnp.moveaxis(split, 0, 1).reshape(-1, *rest)


def attend_forward(heads):
    allowed = jnp.arange(L)[:, None] <= jnp.arange(L)[None, :]
    outs, logs = [], []
    for s in range(heads.shape[0]):
        query, key, value = heads[s, :HD], heads[s, HD : 2 * HD], heads[s, 2 * HD :]
        scores = product(key, query, TN) * HD ** (-0.5)
        scores = jnp.where(allowed, scores, excluded)
        peak = jnp.max(scores, axis=0, keepdims=True)
        weights = jnp.exp(scores - peak)
        total = jnp.sum(weights, axis=0, keepdims=True)
        low = (weights / total).astype(jnp.bfloat16)
        outs.append(product(value, low, NN).astype(jnp.bfloat16))
        logs.append(peak + jnp.log(total))
    return jnp.stack(outs), jnp.stack(logs)


def attend_backward(heads, grads, logs):
    allowed = jnp.arange(L)[:, None] <= jnp.arange(L)[None, :]
    outs = []
    for s in range(heads.shape[0]):
        query, key, value = heads[s, :HD], heads[s, HD : 2 * HD], heads[s, 2 * HD :]
        grad = grads[s]
        scores = product(key, query, TN) * HD ** (-0.5)
        scores = jnp.where(allowed, scores, excluded)
        weights = jnp.exp(scores - logs[s])
        grad_value = product(grad, weights.astype(jnp.bfloat16), NT)
        grad_weights = product(value, grad, TN)
        inner = jnp.sum(weights * grad_weights, axis=0, keepdims=True)
        low = (weights * (grad_weights - inner)).astype(jnp.bfloat16)
        grad_query = product(key, low, NN) * HD ** (-0.5)
        grad_key = product(query, low, NT) * HD ** (-0.5)
        outs.append(jnp.concatenate([grad_query, grad_key, grad_value], axis=0).astype(jnp.bfloat16))
    return jnp.stack(outs)


def spread(values):
    return lax.all_gather(values, "col", axis=1, tiled=True)


def share(values):
    return lax.psum_scatter(
        values.astype(jnp.bfloat16), "col", scatter_dimension=1, tiled=True
    ).astype(jnp.float32)


def whole_weight(weight):
    return lax.all_gather(weight, "row", axis=0, tiled=True)


def share_weight(gradient):
    return lax.psum_scatter(gradient.astype(jnp.bfloat16), "row", scatter_dimension=0, tiled=True)


def body(
    tokens,
    ln1_gain,
    ln1_shift,
    weight_qkv,
    bias_qkv,
    weight_out,
    bias_out,
    ln2_gain,
    ln2_shift,
    weight_up,
    bias_up,
    weight_down,
    bias_down,
    cotangent,
):
    rows, cols = lax.axis_size("row"), lax.axis_size("col")
    row, col = lax.axis_index("row"), lax.axis_index("col")
    slots = (H + cols - 1) // cols
    qkv_channels = CHANNELS // cols
    out_channels = HD // cols

    vectors = lax.all_gather(
        jnp.stack([ln1_gain, ln1_shift, bias_out, ln2_gain, ln2_shift, bias_down]),
        "row",
        axis=1,
        tiled=True,
    )[:, :, None]
    gain_one, shift_one, out_bias, gain_two, shift_two, down_bias = vectors

    biases = lax.all_gather(bias_qkv, "col", axis=0, tiled=True).reshape(CHANNELS, H)
    biases = jnp.pad(biases, ((0, 0), (0, slots * cols - H))).reshape(CHANNELS, slots, cols)
    qkv_bias = lax.dynamic_index_in_dim(biases, col, axis=2, keepdims=False).T[:, :, None]

    qkv_matrix = regroup_matrix(qkv_channels, slots, cols)
    out_matrix = regroup_matrix(out_channels, slots, cols)
    qkv_weight = whole_weight(group_heads(weight_qkv, qkv_matrix, cols))
    out_weight = whole_weight(group_heads(weight_out, out_matrix, cols))
    up_weight = whole_weight(weight_up)
    down_weight = whole_weight(weight_down)

    own = to_blocks(jnp.stack([tokens, cotangent]), rows, cols)
    both = lax.all_gather(own, "col", axis=2, tiled=True)
    residual_own = own[0].astype(jnp.float32)
    cot_own = own[1].astype(jnp.float32)
    cot = both[1]

    normed_in = (norm_stats(both[0].astype(jnp.float32))[0] * gain_one + shift_one).astype(
        jnp.bfloat16
    )
    qkv = product(qkv_weight, normed_in, TN)
    heads = (head_rows(qkv, cols, slots) + qkv_bias).astype(jnp.bfloat16)
    attended, logs = attend_forward(heads)
    attended = flat_rows(attended, cols, slots)
    residual_mid = residual_own + share(product(out_weight, attended, NN)) + out_bias
    centred_mid, scale_mid = norm_stats(residual_mid)
    normed_mid = spread((centred_mid * gain_two + shift_two).astype(jnp.bfloat16))
    hidden_pre = product(up_weight, normed_mid, TN) + bias_up[:, None]
    hidden = jax.nn.gelu(hidden_pre, approximate=True).astype(jnp.bfloat16)
    block_output = (
        residual_mid + share(product(down_weight, hidden, NN)) + down_bias
    ).astype(jnp.bfloat16)
    block_output = from_blocks(block_output, rows, cols)

    grad_hidden = product(down_weight, cot, TN)
    gelu_back = jax.vjp(lambda inner: jax.nn.gelu(inner, approximate=True), hidden_pre)[1]
    grad_pre = gelu_back(grad_hidden)[0].astype(jnp.bfloat16)
    grad_weight_down = share_weight(product(cot, hidden, NT)).astype(jnp.float32)
    grad_normed_mid = share(product(up_weight, grad_pre, NN))
    grad_weight_up = share_weight(product(normed_mid, grad_pre, NT)).astype(jnp.float32)
    up_part = jnp.sum(grad_pre, axis=1, dtype=jnp.float32)
    grad_norm_mid, gain_two_part, shift_two_part = norm_backward(
        grad_normed_mid, centred_mid, scale_mid, gain_two
    )
    grad_residual_mid = cot_own + grad_norm_mid
    grad_branch_own = grad_residual_mid.astype(jnp.bfloat16)
    grad_branch = spread(grad_branch_own)
    grad_attended = product(out_weight, grad_branch, TN).astype(jnp.bfloat16)
    grad_weight_out = ungroup_heads(
        share_weight(product(grad_branch, attended, NT)), out_matrix, cols
    )
    grad_qkv = attend_backward(heads, head_rows(grad_attended, cols, slots), logs)
    grad_qkv = flat_rows(grad_qkv, cols, slots)
    grad_weight_qkv = ungroup_heads(
        share_weight(product(normed_in, grad_qkv, NT)), qkv_matrix, cols
    )
    qkv_part = jnp.sum(grad_qkv, axis=1, dtype=jnp.float32)
    grad_normed_in = share(product(qkv_weight, grad_qkv, NN))
    centred_in, scale_in = norm_stats(residual_own)
    grad_norm_in, gain_one_part, shift_one_part = norm_backward(
        grad_normed_in, centred_in, scale_in, gain_one
    )
    grad_tokens = from_blocks(grad_residual_mid + grad_norm_in, rows, cols)

    features = jnp.stack(
        [
            gain_one_part,
            shift_one_part,
            jnp.sum(grad_branch_own, axis=1, dtype=jnp.float32),
            gain_two_part,
            shift_two_part,
            jnp.sum(cot_own, axis=1),
        ]
    )
    features = lax.psum(features, ("row", "col"))
    features = lax.dynamic_slice_in_dim(features, row * (D // rows), D // rows, axis=1)
    units = lax.psum(jnp.concatenate([up_part, qkv_part]), "row")
    grad_bias_up = units[: up_part.shape[0]]
    spread_bias = lax.all_gather(
        units[up_part.shape[0] :].reshape(cols, slots, qkv_channels), "col", axis=0
    )
    mine = lax.dynamic_index_in_dim(spread_bias, col, axis=1, keepdims=False)
    grad_bias_qkv = mine.transpose(2, 1, 0).reshape(qkv_channels, slots * cols)[:, :H].reshape(-1)
    return (
        block_output,
        grad_tokens,
        features[0],
        features[1],
        grad_weight_qkv,
        grad_bias_qkv,
        grad_weight_out,
        features[2],
        features[3],
        features[4],
        grad_weight_up,
        grad_bias_up,
        grad_weight_down,
        features[5],
    )


def solution(mesh):
    both, row, col = P("row", "col"), P("row"), P("col")
    in_specs = (both, row, row, both, col, both, row, row, row, both, col, both, row, both)
    out_specs = (both, both, row, row, both, col, both, row, row, row, both, col, both, row)
    return jax.shard_map(body, mesh=mesh, in_specs=in_specs, out_specs=out_specs, check_vma=False)
```

time: 4910 us -> 1470 us (0.30)
  waiting for transfers between devices: 4190 us -> 924 us
  local copies, waits for them, and re-layouts: 210 us -> 39.8 us
  matrix products: 235 us -> 147 us
  starting transfers between devices: 10.5 us -> 93.2 us
    reduce_scatter x8 -> x5, waiting for transfers between devices: 2600 us -> 198 us  [the longest x4 103 us: share(): lax.psum_scatter(values.astype(jnp.bfloat16), 'col', scatter_dimension=1,...]
    all_gather x8 -> x7, waiting for transfers between devices: 1550 us -> 233 us  [the longest x4 171 us: whole_weight(): return lax.all_gather(weight, 'row', axis=0, tiled=True)]
    unnamed x16 -> x18, waiting for transfers between devices: 1.29 us -> 448 us
    reshape x14 -> x16, local copies, waits for them, and re-layouts: 125 us -> 9.37 us  [the longest x4 4.13 us: ungroup_heads(): moved = gradient.reshape(gradient.shape[0], cols, -1)]
    dot_general x65 -> x58, matrix products: 235 us -> 147 us  [product(): lax.dot_general(left, right, dims, preferred_element_type=jnp.float32)]
    all_to_all x2 -> x4, starting transfers between devices: 8.76 us -> 81.4 us  [the longest x1 67.4 us: group_heads(): got = lax.all_to_all(moved, 'col', split_axis=1, concat_axis=1, tiled=True)]
    psum x5 -> x2, blocking collectives: 116 us -> 65.7 us  [the longest x1 40.2 us: body(): features = lax.psum(features, ('row', 'col'))]
  transfers between devices with their start and end apart: 18 -> 22, of which waited for: 17 -> 15; matrix products, arithmetic and copies ran while one was open for 3% -> 9% of each run, Pallas kernels for 0% -> 0%
where the time goes in v1:
time: 1470 us; the launch traced here: 1460 us
  waiting for transfers between devices  924 us (63%)
  blocking collectives  197 us (13%)
  matrix products  147 us (10%)
  starting transfers between devices  93.2 us (6%)
  other arithmetic  44.7 us (3%)
  local copies, waits for them, and re-layouts  39.8 us (3%)
  between operations  16.1 us (1%)
    unnamed x18, waiting for transfers between devices  448 us
    all_gather x4, waiting for transfers between devices, whole_weight(): return lax.all_gather(weight, 'row', axis=0, tiled=True)  171 us
    dot_general x58, matrix products, product(): lax.dot_general(left, right, dims, preferred_element_type=jnp.float32)  147 us
    reduce_scatter x4, waiting for transfers between devices, share(): lax.psum_scatter(values.astype(jnp.bfloat16), 'col', scatter_dimension=1,...  103 us
    reduce_scatter x1, waiting for transfers between devices, share_weight(): lax.psum_scatter(gradient.astype(jnp.bfloat16), 'row', scatter_dimension=...  94.7 us
    all_to_all x1, starting transfers between devices, group_heads(): got = lax.all_to_all(moved, 'col', split_axis=1, concat_axis=1, tiled=True)  67.4 us
    all_gather x2, waiting for transfers between devices, spread(): return lax.all_gather(values, 'col', axis=1, tiled=True)  62.3 us
    all_to_all x1, blocking collectives, to_blocks(): got = lax.all_to_all(split, 'row', split_axis=2, concat_axis=1)  60.6 us
  transfers between devices with their start and end apart: 22, of which 15 were waited for; matrix products, arithmetic and copies ran while one was open for 9% of the time, Pallas kernels for 0%

profile of v1, /device:TPU:9, one launch (start us, length us, event | category | flops | bytes accessed | tf_op | source)
XLA Modules:
  0.0 1460.8 jit_solution(7190868534278760962)
XLA Ops:
  8.2 1.5 fusion.46
  10.5 12.2 all_to_all.65
  22.9 1.3 reshape.542
  25.2 60.6 %all_to_all.66 = bf16[2,1,200,8,256]{4,2,0,1,3:T(8,128)(2,1)S(1)} all-to-all(bf16[2,1,200,8,256]{4,2,0,1,3:T(8,128)(2,1)S(1)} %copy.106), channel_id=1, replica_groups=mesh['row'=8,'col'=4] {'row'}, dimensions={3} | all-to-all | bytes 3276800 | tf_op jit(solution)/shard_map/all_to_all | solution.py:48
  86.0 4.3 collective-permute-start
  90.3 36.2 %collective-permute-done = bf16[2,1600,256]{2,1,0:T(8,128)(2,1)S(1)} collective-permute-done((bf16[2,1600,256]{2,1,0:T(8,128)(2,1)S(1)}, bf16[2,1600,256]{2,1,0:T(8,128)(2,1)S(1)}, u32[]{:S(2)}, u32[]{:S(2)}) %collective-permute-start) | collective-permute-done | bytes 1638432 | tf_op jit(solution)/shard_map/ppermute | solution.py:50
  129.0 67.4 %all-to-all-start.1 = ((bf16[200,4,112]{2,0,1:T(8,128)(2,1)}), bf16[200,4,112]{2,0,1:T(8,128)(2,1)S(1)}, u32[]{:S(2)}, u32[]{:S(2)}) async-start(bf16[200,4,112]{2,0,1:T(8,128)(2,1)} %copy.108), calls=%async_computation.1 | async-start | bytes 409600 | tf_op jit(solution)/shard_map/all_to_all | solution.py:74
  198.1 10.8 all-reduce.1
  209.3 24.0 %all-gather = f32[8,200,6]{1,2,0:T(8,128)S(1)} all-gather(f32[1,200,6]{1,2,0:T(8,128)S(1)} %bitcast.520), channel_id=1, replica_groups=mesh['row'=8,'col'=4] {'row'}, dimensions={0}, use_global_device_ids=true | all-gather | bytes 43200 | tf_op jit(solution)/shard_map/all_gather | solution.py:171
  235.1 7.2 copy.112
  242.8 2.7 convert_reduce_fusion
  245.5 3.0 fusion.15
  248.5 7.7 fusion.43
  263.7 1.2 fusion.136
  275.3 13.9 all-gather.9.cloned.1.call-done
  289.2 5.1 convolution_convert_fusion.6
  294.9 37.4 %reduce-scatter.15.cloned.1.call-done = bf16[1600,256]{1,0:T(8,128)(2,1)} async-done(((bf16[1600,1024]{1,0:T(8,128)(2,1)}), bf16[1600,256]{1,0:T(8,128)(2,1)}) %reduce-scatter.15.cloned.1.call-update) | async-done | bytes 819216 | tf_op jit(solution)/shard_map/reduce_scatter | solution.py:136
  332.3 1.5 fusion.220
  333.7 1.6 multiply_reduce_fusion.7
  335.3 3.0 add_convert_fusion.1
  339.2 80.6 %all-gather.17.cloned.1.call-done = bf16[1600,1600]{1,0:T(8,128)(2,1)} async-done(((bf16[200,1600]{1,0:T(8,128)(2,1)}), bf16[1600,1600]{1,0:T(8,128)(2,1)}) %all-gather.17.cloned.1.call-update) | async-done | bytes 5120016 | tf_op jit(solution)/shard_map/all_gather | solution.py:142
  419.7 32.5 %all-gather.15.cloned.1.call-done = bf16[1600,1024]{1,0:T(8,128)(2,1)} async-done(((bf16[1600,256]{1,0:T(8,128)(2,1)}), bf16[1600,1024]{1,0:T(8,128)(2,1)}) %all-gather.15.cloned.1.call-update) | async-done | bytes 3276816 | tf_op jit(solution)/shard_map/all_gather | solution.py:132
  452.3 11.1 fusion.233
  463.4 76.0 %all-gather.19.cloned.1.call-done = bf16[1600,1600]{1,0:T(8,128)(2,1)} async-done(((bf16[200,1600]{1,0:T(8,128)(2,1)}), bf16[1600,1600]{1,0:T(8,128)(2,1)}) %all-gather.19.cloned.1.call-update) | async-done | bytes 5120016 | tf_op jit(solution)/shard_map/all_gather | solution.py:142
  539.4 15.8 %convert_reduce_fusion.1 = (f32[1600]{0:T(1024)}, bf16[1600,1024]{1,0:T(8,128)(2,1)S(1)}) fusion(f32[1024,1600]{0,1:T(8,128)} %fusion.233, f32[1600]{0:T(1024)S(1)} %copy-done.50, bf16[1600,1600]{1,0:T(8,128)(2,1)} %all-gather.19.cloned.1.call-done, bf16[2,1600,1024]{2,1,0:T(8,128)(2,1)} %all-gather.13.cloned.1.call-done), kind=kOutput, calls=%fused_computation.32 | convolution fusion | flops 5280561664 | bytes 18444800 | tf_op jit(solution)/shard_map/dot_general | solution.py:21
  555.3 1.8 copy-done.52
  557.1 7.4 fusion.34
  564.9 38.8 %reduce-scatter.19.cloned.1.call-done = bf16[1600,256]{1,0:T(8,128)(2,1)} async-done(((bf16[1600,1024]{1,0:T(8,128)(2,1)}), bf16[1600,256]{1,0:T(8,128)(2,1)}) %reduce-scatter.19.cloned.1.call-update) | async-done | bytes 819216 | tf_op jit(solution)/shard_map/reduce_scatter | solution.py:136
  603.8 2.5 fusion.96
  606.2 3.0 convert_reduce_fusion.7
  609.8 29.7 %all-gather.21.cloned.1.call-done = bf16[1600,1024]{1,0:T(8,128)(2,1)} async-done(((bf16[1600,256]{1,0:T(8,128)(2,1)}), bf16[1600,1024]{1,0:T(8,128)(2,1)}) %all-gather.21.cloned.1.call-update) | async-done | bytes 3276816 | tf_op jit(solution)/shard_map/all_gather | solution.py:132
  639.5 4.4 convolution_convert_fusion.8
  676.7 1.4 multiply_convert_fusion.1
  679.9 1.5 copy-done.22
  681.4 6.7 convolution_convert_fusion.5
  688.2 11.5 fusion.33
  699.8 5.2 convolution_convert_fusion.7
  705.2 10.2 convolution_convert_fusion.2
  715.9 12.9 convolution_convert_fusion
  728.8 10.3 convolution_convert_fusion.1
  739.2 2.2 fusion.97
  741.4 26.7 %reduce-scatter.17.cloned.1.call-done = bf16[1600,256]{1,0:T(8,128)(2,1)} async-done(((bf16[1600,1024]{1,0:T(8,128)(2,1)}), bf16[1600,256]{1,0:T(8,128)(2,1)}) %reduce-scatter.17.cloned.1.call-update) | async-done | bytes 819216 | tf_op jit(solution)/shard_map/reduce_scatter | solution.py:136
  768.1 4.6 fusion.88
  772.7 3.1 collective-permute-start.1
  775.8 94.7 %reduce-scatter.23.cloned.1.call-done = bf16[200,448]{1,0:T(8,128)(2,1)} async-done(((bf16[1600,448]{1,0:T(8,128)(2,1)}), bf16[200,448]{1,0:T(8,128)(2,1)}) %reduce-scatter.23.cloned.1.call-update) | async-done | bytes 179216 | tf_op jit(solution)/shard_map/reduce_scatter | solution.py:146
  871.7 9.1 all_to_all.67
  880.8 4.2 all-to-all-start.3
  885.0 3.1 collective-permute-start.2
  888.1 191.6 %reduce-scatter.25.cloned.1.call-done = bf16[200,1344]{1,0:T(8,128)(2,1)} async-done(((bf16[1600,1344]{1,0:T(8,128)(2,1)}), bf16[200,1344]{1,0:T(8,128)(2,1)}) %reduce-scatter.25.cloned.1.call-update) | async-done | bytes 537616
  1079.7 2.1 reshape.549
  1082.7 5.2 all-to-all-start.5
  1087.9 9.0 all-to-all-done.5
  1097.8 4.5 all-to-all-start.4
  1102.4 130.8 %reduce-scatter.29.cloned.1.call-done = bf16[200,1600]{1,0:T(8,128)(2,1)} async-done(((bf16[1600,1600]{1,0:T(8,128)(2,1)}), bf16[200,1600]{1,0:T(8,128)(2,1)}) %reduce-scatter.29.cloned.1.call-update) | async-done | bytes 640016
  1233.2 2.2 convert_element_type.362
  1235.4 123.6 %reduce-scatter.27.cloned.1.call-done = bf16[200,1600]{1,0:T(8,128)(2,1)} async-done(((bf16[1600,1600]{1,0:T(8,128)(2,1)}), bf16[200,1600]{1,0:T(8,128)(2,1)}) %reduce-scatter.27.cloned.1.call-update) | async-done | bytes 640016
  1359.1 2.2 convert_element_type.360
  1361.3 2.2 convert_reduce_fusion.2
  1363.7 25.5 %psum.15 = f32[2944]{0:T(1024)S(1)} all-reduce(f32[2944]{0:T(1024)S(1)} %pad_maximum_fusion.8), channel_id=1, replica_groups=mesh['row'=8,'col'=4] {'row'}, use_global_device_ids=true, to_apply=%region_45.46 | all-reduce | flops 2944 | bytes 23552 | tf_op jit(solution)/shard_map/psum | solution.py:255
  1389.9 14.2 all_gather.39
  1406.6 40.2 %psum.14 = f32[6,1600]{1,0:T(8,128)S(1)} all-reduce(f32[6,1600]{1,0:T(8,128)S(1)} %stack.110), channel_id=1, replica_groups=mesh['row'=8,'col'=4] {'row','col'}, use_global_device_ids=true, to_apply=%region_41.42 | all-reduce | flops 9600 | bytes 76800 | tf_op jit(solution)/shard_map/psum | solution.py:253
  1448.4 1.3 copy.135
  1450.2 2.5 fusion
  1452.7 1.4 copy.147
  (297 shorter events, 72.2 us)
Async XLA Ops:
  7.2 227.9 %all-gather.11.cloned.1.call-start = ((), (), s32[]{:S(2)}) async-start(), calls=%async_computation.16 | async-start | bytes 5068800 | tf_op jit(solution)/shard_map/all_gather | solution.py:142
  9.8 14.5 copy-start.24
  9.8 14.7 %copy-start.25 = (bf16[200,2048]{1,0:T(8,128)(2,1)S(1)}, bf16[200,2048]{1,0:T(8,128)(2,1)}, u32[]{:S(2)}) copy-start(bf16[200,2048]{1,0:T(8,128)(2,1)} %param.27) | copy-start | bytes 2457604
  24.2 218.6 %all-gather.13.cloned.1.call-start = ((), (), s32[]{:S(2)}) async-start(), calls=%async_computation.17 | async-start | bytes 8192000 | tf_op jit(solution)/shard_map/all_gather | solution.py:191
  25.2 102.6 %copy-start.49 = (bf16[200,400]{1,0:T(8,128)(2,1)S(1)}, bf16[200,400]{1,0:T(8,128)(2,1)}, u32[]{:S(2)}) copy-start(bf16[200,400]{1,0:T(8,128)(2,1)} %param.19) | copy-start | bytes 480004
  85.8 110.7 %copy-start.51 = (u32[32]{0:T(128)S(1)}, u32[32]{0:T(128)}, u32[]{:S(2)}) copy-start(u32[32]{0:T(128)} %constant.134) | copy-start | bytes 388
  85.8 111.9 %copy-start.35 = (f32[1200]{0:T(1024)S(1)}, f32[1200]{0:T(1024)}, u32[]{:S(2)}) copy-start(f32[1200]{0:T(1024)} %param.18) | copy-start | bytes 14404
  85.8 123.3 %copy-start.42 = (f32[200]{0:T(256)S(1)}, f32[200]{0:T(256)}, u32[]{:S(2)}) copy-start(f32[200]{0:T(256)} %param.15) | copy-start | bytes 2404
  85.8 123.4 %copy-start.43 = (f32[200]{0:T(256)S(1)}, f32[200]{0:T(256)}, u32[]{:S(2)}) copy-start(f32[200]{0:T(256)} %param.16) | copy-start | bytes 2404
  85.8 123.4 %copy-start.44 = (f32[200]{0:T(256)S(1)}, f32[200]{0:T(256)}, u32[]{:S(2)}) copy-start(f32[200]{0:T(256)} %param.20) | copy-start | bytes 2404
  85.8 123.4 %copy-start.45 = (f32[200]{0:T(256)S(1)}, f32[200]{0:T(256)}, u32[]{:S(2)}) copy-start(f32[200]{0:T(256)} %param.21) | copy-start | bytes 2404
  85.9 123.4 %copy-start.46 = (f32[200]{0:T(256)S(1)}, f32[200]{0:T(256)}, u32[]{:S(2)}) copy-start(f32[200]{0:T(256)} %param.22) | copy-start | bytes 2404
  85.9 123.4 %copy-start.47 = (f32[200]{0:T(256)S(1)}, f32[200]{0:T(256)}, u32[]{:S(2)}) copy-start(f32[200]{0:T(256)} %param.26) | copy-start | bytes 2404
  86.0 40.5 %collective-permute-start = (bf16[2,1600,256]{2,1,0:T(8,128)(2,1)S(1)}, bf16[2,1600,256]{2,1,0:T(8,128)(2,1)S(1)}, u32[]{:S(2)}, u32[]{:S(2)}) collective-permute-start(bf16[2,1600,256]{2,1,0:T(8,128)(2,1)S(1)} %bitcast.483), channel_id=1, source_target_pairs={{0,0},{1,8},{2,16},{3,24},{4,1},{5,9},{6,17},{7,25},{8,2},{9,10},{... | collective-permute-start | bytes 4915208 | tf_op jit(solution)/shard_map/ppermute | solution.py:50
  127.8 105.6 %copy-start.32 = (s32[400]{0:T(512)}, s32[400]{0:T(512)S(1)}, u32[]{:S(2)}) copy-start(s32[400]{0:T(512)S(1)} %fusion.208) | copy-start | bytes 4804
  129.0 105.0 %all-to-all-start.1 = ((bf16[200,4,112]{2,0,1:T(8,128)(2,1)}), bf16[200,4,112]{2,0,1:T(8,128)(2,1)S(1)}, u32[]{:S(2)}, u32[]{:S(2)}) async-start(bf16[200,4,112]{2,0,1:T(8,128)(2,1)} %copy.108), calls=%async_computation.1 | async-start | bytes 409600 | tf_op jit(solution)/shard_map/all_to_all | solution.py:74
  196.5 92.7 %all-gather.9.cloned.1.call-start = ((), (), s32[]{:S(2)}) async-start(), calls=%async_computation.15 | async-start | bytes 1843200 | tf_op jit(solution)/shard_map/all_gather | solution.py:142
  234.0 14.5 copy-start.26
  234.0 14.5 copy-start.38
  235.0 97.3 %reduce-scatter.15.cloned.1.call-start = ((), (), s32[]{:S(2)}) async-start(), calls=%async_computation.18 | async-start | bytes 4096000 | tf_op jit(solution)/shard_map/reduce_scatter | solution.py:136
  242.8 5.7 copy-start.21
  245.5 10.8 copy-start.30
  248.5 7.8 copy-start.40
  257.6 16.3 %copy-start.19 = (bf16[7,192,1024]{2,1,0:T(8,128)(2,1)}, bf16[7,192,1024]{2,1,0:T(8,128)(2,1)S(1)}, u32[]{:S(2)}) copy-start(bf16[7,192,1024]{2,1,0:T(8,128)(2,1)S(1)} %fusion.20) | copy-start | bytes 8257540
  258.5 13.0 copy-start.4
  259.4 4.3 copy-start.6
  260.3 5.2 copy-start.8
  261.2 5.8 copy-start.10
  262.1 6.3 copy-start.14
  263.0 6.9 copy-start.16
  275.3 13.9 copy-start.29
  294.2 38.0 %copy-start.3 = (bf16[2,1600,256]{2,1,0:T(8,128)(2,1)S(1)}, bf16[2,1600,256]{2,1,0:T(8,128)(2,1)}, u32[]{:S(2)}) copy-start(bf16[2,1600,256]{2,1,0:T(8,128)(2,1)} %copy-done.2) | copy-start | bytes 4915204
  294.3 125.5 %all-gather.17.cloned.1.call-start = ((), (), s32[]{:S(2)}) async-start(), calls=%async_computation.20 | async-start | bytes 5990400 | tf_op jit(solution)/shard_map/all_gather | solution.py:142
  294.8 157.4 %all-gather.15.cloned.1.call-start = ((), (), s32[]{:S(2)}) async-start(), calls=%async_computation.19 | async-start | bytes 4096000 | tf_op jit(solution)/shard_map/all_gather | solution.py:132
  338.4 201.1 %all-gather.19.cloned.1.call-start = ((), (), s32[]{:S(2)}) async-start(), calls=%async_computation.21 | async-start | bytes 5990400 | tf_op jit(solution)/shard_map/all_gather | solution.py:142
  339.1 200.3 %copy-start.50 = (f32[1600]{0:T(1024)S(1)}, f32[1600]{0:T(1024)}, u32[]{:S(2)}) copy-start(f32[1600]{0:T(1024)} %param.24) | copy-start | bytes 19204
  339.1 264.6 %reduce-scatter.19.cloned.1.call-start = ((), (), s32[]{:S(2)}) async-start(), calls=%async_computation.23 | async-start | bytes 4096000 | tf_op jit(solution)/shard_map/reduce_scatter | solution.py:136
  539.4 17.6 %copy-start.48 = (bf16[1600,1600]{1,0:T(8,128)(2,1)S(1)}, bf16[1600,1600]{1,0:T(8,128)(2,1)}, u32[]{:S(2)}) copy-start(bf16[1600,1600]{1,0:T(8,128)(2,1)} %all-gather.17.cloned.1.call-done) | copy-start | bytes 15360004
  564.5 39.2 %copy-start.18 = (bf16[1600,256]{1,0:T(8,128)(2,1)S(1)}, bf16[1600,256]{1,0:T(8,128)(2,1)}, u32[]{:S(2)}) copy-start(bf16[1600,256]{1,0:T(8,128)(2,1)} %reduce-scatter.15.cloned.1.call-done) | copy-start | bytes 2457604
  564.5 75.0 %all-gather.21.cloned.1.call-start = ((), (), s32[]{:S(2)}) async-start(), calls=%async_computation.24 | async-start | bytes 4096000 | tf_op jit(solution)/shard_map/all_gather | solution.py:132
  609.2 130.0 %reduce-scatter.21.cloned.1.call-start = ((), (), s32[]{:S(2)}) async-start(), calls=%async_computation.25 | async-start | bytes 4096000 | tf_op jit(solution)/shard_map/reduce_scatter | solution.py:136
  639.5 4.5 copy-start.17
  647.8 2.2 copy-start.15
  657.8 2.2 copy-start.9
  678.1 3.3 slice-start
  688.1 80.0 %reduce-scatter.17.cloned.1.call-start = ((), (), s32[]{:S(2)}) async-start(), calls=%async_computation.22 | async-start | bytes 4096000 | tf_op jit(solution)/shard_map/reduce_scatter | solution.py:136
  699.7 5.4 copy-start.27
  699.7 5.4 copy-start.31
  699.7 5.4 copy-start.39
  699.7 5.4 copy-start.41
  699.8 170.8 %reduce-scatter.23.cloned.1.call-start = ((), (), s32[]{:S(2)}) async-start(), calls=%async_computation.26 | async-start | bytes 1843200 | tf_op jit(solution)/shard_map/reduce_scatter | solution.py:146
  705.1 374.7 %reduce-scatter.25.cloned.1.call-start = ((), (), s32[]{:S(2)}) async-start(), calls=%async_computation.27 | async-start | bytes 5068800
  715.4 517.8 %reduce-scatter.29.cloned.1.call-start = ((), (), s32[]{:S(2)}) async-start(), calls=%async_computation.29 | async-start | bytes 5990400
  728.8 630.3 %reduce-scatter.27.cloned.1.call-start = ((), (), s32[]{:S(2)}) async-start(), calls=%async_computation.28 | async-start | bytes 5990400
  739.1 29.0 %copy-start.28 = (f32[1600]{0:T(1024)S(1)}, f32[1600]{0:T(1024)}, u32[]{:S(2)}) copy-start(f32[1600]{0:T(1024)} %get-tuple-element.25) | copy-start | bytes 19204
  772.7 108.0 %collective-permute-start.1 = (bf16[1600,256]{1,0:T(8,128)(2,1)}, bf16[1600,256]{1,0:T(8,128)(2,1)}, u32[]{:S(2)}, u32[]{:S(2)}) collective-permute-start(bf16[1600,256]{1,0:T(8,128)(2,1)} %get-tuple-element.34), channel_id=1, source_target_pairs={{0,0},{8,1},{16,2},{24,3},{1,4},{9,5},{17,6},{25,7},{2,8},{10,9},{... | collective-permute-start | bytes 2457608 | tf_op jit(solution)/shard_map/ppermute | solution.py:55
  880.8 202.0 %all-to-all-start.3 = ((bf16[8,200,1,256]{3,1,2,0:T(8,128)(2,1)}), bf16[8,200,1,256]{3,1,2,0:T(8,128)(2,1)S(1)}, u32[]{:S(2)}, u32[]{:S(2)}) async-start(bf16[8,200,1,256]{3,1,2,0:T(8,128)(2,1)} %bitcast.65), calls=%async_computation.5 | async-start | bytes 1638400 | tf_op jit(solution)/shard_map/all_to_all | solution.py:58
  885.0 202.9 %collective-permute-start.2 = (f32[1600,256]{1,0:T(8,128)}, f32[1600,256]{1,0:T(8,128)}, u32[]{:S(2)}, u32[]{:S(2)}) collective-permute-start(f32[1600,256]{1,0:T(8,128)} %get-tuple-element.33), channel_id=1, source_target_pairs={{0,0},{8,1},{16,2},{24,3},{1,4},{9,5},{17,6},{25,7},{2,8},{10,9},{... | collective-permute-start | bytes 4915208 | tf_op jit(solution)/shard_map/ppermute | solution.py:55
  1082.7 14.2 all-to-all-start.5
  1097.8 354.9 %all-to-all-start.4 = ((f32[8,200,1,256]{3,1,2,0:T(8,128)}), f32[8,200,1,256]{3,1,2,0:T(8,128)S(1)}, u32[]{:S(2)}, u32[]{:S(2)}) async-start(f32[8,200,1,256]{3,1,2,0:T(8,128)} %bitcast.120), calls=%async_computation.8 | async-start | bytes 3276800 | tf_op jit(solution)/shard_map/all_to_all | solution.py:58
  1102.3 261.3 %copy-start.34 = (f32[1600]{0:T(1024)S(1)}, f32[1600]{0:T(1024)}, u32[]{:S(2)}) copy-start(f32[1600]{0:T(1024)} %get-tuple-element.76) | copy-start | bytes 19204
  1102.3 303.0 %copy-start.33 = (s32[400]{0:T(512)S(1)}, s32[400]{0:T(512)}, u32[]{:S(2)}) copy-start(s32[400]{0:T(512)} %copy-done.32) | copy-start | bytes 4804
  1361.3 88.9 %copy-start.37 = (s32[1200]{0:T(1024)S(1)}, s32[1200]{0:T(1024)}, u32[]{:S(2)}) copy-start(s32[1200]{0:T(1024)} %copy-done.36) | copy-start | bytes 14404
  1449.7 4.3 copy-start.1
  (13 other events, 21.4 us)
Sparse Core Ops, SparseCore 0:
  24.3 141.0 all-gather.10
  167.5 75.2 all-gather.12
  245.5 43.6 all-gather.8
  294.4 37.8 reduce-scatter.14
  334.5 85.1 all-gather.16
  421.8 30.4 all-gather.14
  454.7 84.7 all-gather.18
  564.7 39.0 reduce-scatter.18
  609.4 30.1 all-gather.20
  688.2 38.3 reduce-scatter.20
  729.3 38.7 reduce-scatter.16
  771.4 99.0 reduce-scatter.22
  874.4 205.3 reduce-scatter.24
  1083.4 149.7 reduce-scatter.28
  1236.5 122.5 reduce-scatter.26

commit v2 on v1

v2 whole, which is shorter than its diff:
```python
import functools

import jax
import jax.numpy as jnp
from jax import lax
from jax.experimental import pallas as pl
from jax.experimental.pallas import tpu as pltpu
from jax.sharding import PartitionSpec as P

D = 1600
H = 25
HD = 64
L = 1024
CHANNELS = 3 * HD
QB = 256

epsilon = 1e-05
excluded = -1e30

TN = (((0,), (0,)), ((), ()))
NN = (((1,), (0,)), ((), ()))
NT = (((1,), (1,)), ((), ()))
MESH = pl.DeviceIdType.MESH
ANY = pl.BlockSpec(memory_space=pl.ANY)
VMEM = pl.BlockSpec(memory_space=pltpu.VMEM)
LIMIT = 60 * 2**20
f32 = jnp.float32
bf16 = jnp.bfloat16


def product(left, right, dims):
    return lax.dot_general(left, right, dims, preferred_element_type=f32)


def remote(src, dst, send, recv, device):
    return pltpu.make_async_remote_copy(
        src_ref=src,
        dst_ref=dst,
        send_sem=send,
        recv_sem=recv,
        device_id=device,
        device_id_type=MESH,
    )


def meet(devices):
    sem = pltpu.get_barrier_semaphore()
    for device in devices:
        pl.semaphore_signal(sem, inc=1, device_id=device, device_id_type=MESH)
    pl.semaphore_wait(sem, len(devices))


def lanes(index, width):
    return pl.ds(pl.multiple_of(index * width, 128), width)


class Place:
    def __init__(self, rows, cols):
        self.R, self.C, self.A, self.X = rows, cols, rows // 2, cols // 2
        self.r, self.c = lax.axis_index("row"), lax.axis_index("col")
        self.a, self.b = self.r // 2, lax.rem(self.r, 2)
        self.x, self.k = self.c // 2, lax.rem(self.c, 2)
        self.core = (self.r, self.x * 2 + 1 - self.k)
        self.pair = (self.a * 2 + 1 - self.b, self.c)

    def ahead(self, o):
        return lax.rem(self.a + o, self.A)

    def behind(self, o):
        return lax.rem(self.a - o + self.A, self.A)

    def line(self, o):
        return (self.ahead(o) * 2 + self.b, self.c)

    def x_ahead(self, o):
        return lax.rem(self.x + o, self.X)

    def x_behind(self, o):
        return lax.rem(self.x - o + self.X, self.X)

    def side(self, o):
        return (self.r, self.x_ahead(o) * 2 + self.k)

    def col_peers(self):
        return [self.core] + [self.side(o) for o in range(1, self.X)]

    def row_peers(self):
        return [self.pair] + [self.line(o) for o in range(1, self.A)]


class Spread:
    def __init__(self, p, own, full, width, send, recv):
        self.p, self.own, self.full, self.width = p, own, full, width
        self.send, self.recv = send, recv

    def part(self, block):
        return self.full.at[..., lanes(block, self.width)]

    def side_copy(self, o):
        return remote(
            self.own, self.part(self.p.c), self.send.at[o], self.recv.at[o], self.p.side(o)
        )

    def core_copy(self, o):
        p = self.p
        block = p.c if o == 0 else p.x_behind(o) * 2 + p.k
        src = self.own if o == 0 else self.part(block)
        i = p.X + o
        return remote(src, self.part(block), self.send.at[i], self.recv.at[i], p.core)

    def local(self):
        i = 2 * self.p.X
        return pltpu.make_async_copy(self.own, self.part(self.p.c), self.send.at[i])

    def start(self):
        for o in range(1, self.p.X):
            self.side_copy(o).start()
        self.core_copy(0).start()
        self.local().start()

    def forward(self):
        for o in range(1, self.p.X):
            self.side_copy(o).wait_recv()
            self.core_copy(o).start()

    def finish(self):
        for o in range(self.p.X):
            self.core_copy(o).wait()
        for o in range(1, self.p.X):
            self.side_copy(o).wait_send()
        self.local().wait()


def spread_sems(cols):
    return [pltpu.SemaphoreType.DMA((cols + 1,)), pltpu.SemaphoreType.DMA((cols + 1,))]


class Share:
    def __init__(self, p, part, core_in, side_out, side_in, send, recv):
        self.p, self.part, self.core_in = p, part, core_in
        self.side_out, self.side_in, self.send, self.recv = side_out, side_in, send, recv

    def core_copy(self, x):
        p = self.p
        return remote(
            self.part.at[x * 2 + 1 - p.k],
            self.core_in.at[x],
            self.send.at[x],
            self.recv.at[x],
            p.core,
        )

    def side_copy(self, o):
        p = self.p
        i = p.X + o - 1
        return remote(
            self.side_out.at[o - 1],
            self.side_in.at[o - 1],
            self.send.at[i],
            self.recv.at[i],
            p.side(o),
        )

    def start(self):
        for x in range(self.p.X):
            self.core_copy(x).start()

    def middle(self):
        p = self.p
        for x in range(p.X):
            self.core_copy(x).wait_recv()
        for o in range(1, p.X):
            x = p.x_ahead(o)

            def add(d, carry, x=x, o=o):
                total = self.part[x * 2 + p.k, d].astype(f32) + self.core_in[x, d].astype(f32)
                self.side_out[o - 1, d] = total.astype(bf16)
                return carry

            lax.fori_loop(0, p.R, add, 0)
            self.side_copy(o).start()

    def arrive(self):
        for o in range(1, self.p.X):
            self.side_copy(o).wait_recv()

    def total(self, d):
        p = self.p
        result = self.part[p.c, d].astype(f32) + self.core_in[p.x, d].astype(f32)
        for o in range(1, p.X):
            result = result + self.side_in[o - 1, d].astype(f32)
        return result

    def finish(self):
        for x in range(self.p.X):
            self.core_copy(x).wait_send()
        for o in range(1, self.p.X):
            self.side_copy(o).wait_send()


def share_scratch(rows, cols, feats, width):
    half = cols // 2
    return [
        pltpu.VMEM((cols, rows, feats, width), bf16),
        pltpu.VMEM((half, rows, feats, width), bf16),
        pltpu.VMEM((half - 1, rows, feats, width), bf16),
        pltpu.VMEM((half - 1, rows, feats, width), bf16),
        pltpu.SemaphoreType.DMA((cols - 1,)),
        pltpu.SemaphoreType.DMA((cols - 1,)),
    ]


def fill_partial(part, weight, act, cols, rows, width):
    def one(d, carry):
        for j in range(cols):
            part[j, d] = product(
                weight[d], act[:, j * width : (j + 1) * width], NN
            ).astype(bf16)
        return carry

    lax.fori_loop(0, rows, one, 0)


class Reduce:
    def __init__(self, p, left, right, pair_out, pair_in, line_in, sems):
        self.p, self.left, self.right = p, left, right
        self.pair_out, self.pair_in, self.line_in = pair_out, pair_in, line_in
        self.psend, self.precv, self.zsend, self.zrecv = sems

    def chunk(self, d):
        return product(self.left[d], self.right[...], NT)

    def pair_copy(self, i):
        return remote(
            self.pair_out.at[i],
            self.pair_in.at[i],
            self.psend.at[i],
            self.precv.at[i],
            self.p.pair,
        )

    def line_copy(self, o):
        return remote(
            self.pair_in.at[self.p.ahead(o)],
            self.line_in.at[o - 1],
            self.zsend.at[o - 1],
            self.zrecv.at[o - 1],
            self.p.line(o),
        )

    def send_pair(self):
        p = self.p

        def one(o, carry):
            i = p.ahead(o + 1)
            self.pair_out[i] = self.chunk(i * 2 + 1 - p.b).astype(bf16)
            self.pair_copy(i).start()
            return carry

        lax.fori_loop(0, p.A, one, 0)

    def send_line(self):
        p = self.p
        for o in range(1, p.A):
            i = p.ahead(o)
            value = self.chunk(i * 2 + p.b)
            self.pair_copy(i).wait_recv()
            self.pair_in[i] = (value + self.pair_in[i].astype(f32)).astype(bf16)
            self.line_copy(o).start()

    def finish(self, out):
        p = self.p
        value = self.chunk(p.r)
        self.pair_copy(p.a).wait_recv()
        value = value + self.pair_in[p.a].astype(f32)
        for o in range(1, p.A):
            self.line_copy(o).wait_recv()
            value = value + self.line_in[o - 1].astype(f32)
        out[...] = value
        for i in range(p.A):
            self.pair_copy(i).wait_send()
        for o in range(1, p.A):
            self.line_copy(o).wait_send()


def reduce_scratch(rows, feats, width):
    half = rows // 2
    return [
        pltpu.VMEM((half, feats, width), bf16),
        pltpu.VMEM((half, feats, width), bf16),
        pltpu.VMEM((half - 1, feats, width), bf16),
        pltpu.SemaphoreType.DMA((half,)),
        pltpu.SemaphoreType.DMA((half,)),
        pltpu.SemaphoreType.DMA((half - 1,)),
        pltpu.SemaphoreType.DMA((half - 1,)),
    ]


def home(p, q):
    block = p.c * p.R + q
    return (block // p.C, lax.rem(block, p.C))


def own_block(p):
    block = p.r * p.C + p.c
    return block // p.R, lax.rem(block, p.R)


def equal(left, right):
    return jnp.logical_and(left[0] == right[0], left[1] == right[1])


def exchange_copies(p, src, dst, send, recv):
    out = []
    for o in range(1, p.C):
        to = lax.rem(p.c + o, p.C)
        out.append(remote(src.at[to], dst.at[p.c], send.at[o], recv.at[o], (p.r, to)))
    return out


def all_col(p):
    return [(p.r, lax.rem(p.c + o, p.C)) for o in range(1, p.C)]


def all_row(p):
    return [(lax.rem(p.r + o, p.R), p.c) for o in range(1, p.R)]


def enter_kernel(
    rows, cols, tokcot, wq, wo, bias, vec, both, own, wq_o, wo_o, bias_o, vec_o,
    send, recv, local, csend, crecv, ssend, srecv, vsend, vrecv,
):
    p = Place(rows, cols)
    me = (p.r, p.c)
    width = own.shape[-1]
    source_col, _ = own_block(p)
    sources = [(q, source_col) for q in range(rows)]
    targets = [home(p, q) for q in range(rows)]
    meet(sources + targets + all_col(p) + all_row(p))

    swaps = []
    for i, (src, dst) in enumerate(((wq, wq_o), (wo, wo_o), (bias, bias_o))):
        swaps += exchange_copies(p, src, dst, csend.at[i], crecv.at[i])
    for copy in swaps:
        copy.start()
    keeps = [
        pltpu.make_async_copy(src.at[p.c], dst.at[p.c], local.at[i])
        for i, (src, dst) in enumerate(((wq, wq_o), (wo, wo_o), (bias, bias_o)))
    ]
    keeps.append(pltpu.make_async_copy(vec, vec_o.at[p.r], local.at[3]))
    for copy in keeps:
        copy.start()

    def outgoing(q):
        return remote(
            tokcot.at[:, :, q * width : (q + 1) * width],
            own.at[:, p.r],
            send.at[q],
            recv.at[p.r],
            targets[q],
        )

    def staying(q):
        return pltpu.make_async_copy(
            tokcot.at[:, :, q * width : (q + 1) * width], own.at[:, p.r], local.at[4]
        )

    for q in range(rows):
        here = equal(targets[q], me)

        @pl.when(here)
        def _():
            staying(q).start()

        @pl.when(jnp.logical_not(here))
        def _():
            outgoing(q).start()

    vecs = [
        remote(vec, vec_o.at[p.r], vsend.at[o], vrecv.at[o], peer)
        for o, peer in enumerate(all_row(p))
    ]
    for copy in vecs:
        copy.start()

    for q in range(rows):
        here = equal(sources[q], me)

        @pl.when(here)
        def _():
            staying(0).wait()

        @pl.when(jnp.logical_not(here))
        def _():
            remote(
                tokcot.at[:, :, 0:width], own.at[:, q], send.at[0], recv.at[q], sources[q]
            ).wait_recv()

    gather = Spread(p, own, both, width, ssend, srecv)
    gather.start()
    gather.forward()
    for copy in swaps + vecs:
        copy.wait()
    for copy in keeps:
        copy.wait()
    gather.finish()
    for q in range(rows):

        @pl.when(jnp.logical_not(equal(targets[q], me)))
        def _():
            outgoing(q).wait_send()


def leave_kernel(
    rows, cols, blocks, gq, go, feat, units, res, gq_o, go_o, feat_o, units_o,
    feat_in, feat_sum, send, recv, local, csend, crecv, fsend, frecv, usend, urecv,
):
    p = Place(rows, cols)
    me = (p.r, p.c)
    width = blocks.shape[-1]
    target_col, place = own_block(p)
    targets = [(q, target_col) for q in range(rows)]
    sources = [home(p, q) for q in range(rows)]
    meet(sources + targets + all_col(p) + all_row(p))

    feats, unit_copies = [], []
    for o in range(1, rows):
        to = lax.rem(p.r + o, rows)
        feats.append(
            remote(feat.at[to], feat_in.at[o], fsend.at[o], frecv.at[o], (to, p.c))
        )
        unit_copies.append(
            remote(units, units_o.at[p.r], usend.at[o], urecv.at[o], (to, p.c))
        )
    for copy in feats + unit_copies:
        copy.start()
    swaps = []
    for i, (src, dst) in enumerate(((gq, gq_o), (go, go_o))):
        swaps += exchange_copies(p, src, dst, csend.at[i], crecv.at[i])
    for copy in swaps:
        copy.start()
    keeps = [
        pltpu.make_async_copy(src.at[p.c], dst.at[p.c], local.at[i])
        for i, (src, dst) in enumerate(((gq, gq_o), (go, go_o)))
    ]
    keeps.append(pltpu.make_async_copy(units, units_o.at[p.r], local.at[2]))
    for copy in keeps:
        copy.start()

    def slot(q):
        return res.at[:, :, lanes(q, width)]

    def outgoing(q):
        return remote(blocks.at[:, q], slot(place), send.at[q], recv.at[place], targets[q])

    def staying(q):
        return pltpu.make_async_copy(blocks.at[:, q], slot(place), local.at[3])

    for q in range(rows):
        here = equal(targets[q], me)

        @pl.when(here)
        def _():
            staying(q).start()

        @pl.when(jnp.logical_not(here))
        def _():
            outgoing(q).start()

    total = feat[p.r]
    for o, copy in enumerate(feats):
        copy.wait_recv()
        total = total + feat_in[o + 1]
    feat_sum[...] = total
    feat_o[p.c] = total
    sums = [
        remote(feat_sum, feat_o.at[p.c], csend.at[2, o + 1], crecv.at[2, o + 1], peer)
        for o, peer in enumerate(all_col(p))
    ]
    for copy in sums:
        copy.start()

    for q in range(rows):
        here = equal(sources[q], me)

        @pl.when(here)
        def _():
            staying(0).wait()

        @pl.when(jnp.logical_not(here))
        def _():
            remote(
                blocks.at[:, 0], slot(q), send.at[0], recv.at[q], sources[q]
            ).wait_recv()

    for copy in swaps + unit_copies + sums:
        copy.wait()
    for copy in feats:
        copy.wait_send()
    for copy in keeps:
        copy.wait()
    for q in range(rows):

        @pl.when(jnp.logical_not(equal(targets[q], me)))
        def _():
            outgoing(q).wait_send()


def masked_scores(key, query, first):
    scores = product(key, query, TN) * HD ** (-0.5)
    keys = lax.broadcasted_iota(jnp.int32, scores.shape, 0)
    queries = lax.broadcasted_iota(jnp.int32, scores.shape, 1) + first
    return jnp.where(keys <= queries, scores, excluded)


def attend_kernel(qkv, out, logs):
    for first in range(0, L, QB):
        last = first + QB
        scores = masked_scores(qkv[HD : 2 * HD, :last], qkv[:HD, first:last], first)
        peak = jnp.max(scores, axis=0, keepdims=True)
        weights = jnp.exp(scores - peak)
        total = jnp.sum(weights, axis=0, keepdims=True)
        low = (weights * (1.0 / total)).astype(bf16)
        out[:, first:last] = product(qkv[2 * HD :, :last], low, NN).astype(bf16)
        logs[0, :, first:last] = peak + jnp.log(total)


def attend(qkv):
    slots = qkv.shape[0] // CHANNELS
    return pl.pallas_call(
        attend_kernel,
        grid=(slots,),
        out_shape=[
            jax.ShapeDtypeStruct((slots * HD, L), bf16),
            jax.ShapeDtypeStruct((slots, 1, L), f32),
        ],
        in_specs=[pl.BlockSpec((CHANNELS, L), lambda s: (s, 0))],
        out_specs=[
            pl.BlockSpec((HD, L), lambda s: (s, 0)),
            pl.BlockSpec((1, 1, L), lambda s: (s, 0, 0)),
        ],
        compiler_params=pltpu.CompilerParams(vmem_limit_bytes=LIMIT),
        cost_estimate=pl.CostEstimate(
            flops=slots * 4 * HD * L * L, bytes_accessed=4 * 2**20, transcendentals=slots * L * L
        ),
    )(qkv)


def attend_back(qkv, grad, logs, out, dkey, dval):
    query, key, value = qkv[:HD], qkv[HD : 2 * HD], qkv[2 * HD :]
    dkey[...] = jnp.zeros_like(dkey)
    dval[...] = jnp.zeros_like(dval)
    for first in range(0, L, QB):
        last = first + QB
        scores = masked_scores(key[:, :last], query[:, first:last], first)
        weights = jnp.exp(scores - logs[:, first:last])
        back = grad[:, first:last]
        dval[:, :last] += product(back, weights.astype(bf16), NT)
        grad_weights = product(value[:, :last], back, TN)
        inner = jnp.sum(weights * grad_weights, axis=0, keepdims=True)
        low = (weights * (grad_weights - inner)).astype(bf16)
        out(0, first, last, product(key[:, :last], low, NN) * HD ** (-0.5))
        dkey[:, :last] += product(query[:, first:last], low, NT)
    out(HD, 0, L, dkey[...] * HD ** (-0.5))
    out(2 * HD, 0, L, dval[...])


def middle_kernel(rows, cols, weight, att, own, vec, resid, full, normed, *scratch):
    p = Place(rows, cols)
    share = Share(p, *scratch[:6])
    width = own.shape[-1]
    gather = Spread(p, normed, full, width, *scratch[6:8])
    meet(p.col_peers())
    fill_partial(share.part, weight, att, cols, rows, width)
    share.start()
    share.middle()
    share.arrive()

    def first(d, total):
        value = own[d].astype(f32) + share.total(d) + vec[d, :, 2:3]
        resid[d] = value
        return total + jnp.sum(value, axis=0, keepdims=True)

    zero = jnp.zeros((1, width), f32)
    mean = lax.fori_loop(0, rows, first, zero) / D

    def second(d, total):
        value = resid[d] - mean
        return total + jnp.sum(value * value, axis=0, keepdims=True)

    scale = lax.rsqrt(lax.fori_loop(0, rows, second, zero) / D + epsilon)

    def third(d, carry):
        value = (resid[d] - mean) * scale
        normed[d] = (value * vec[d, :, 3:4] + vec[d, :, 4:5]).astype(bf16)
        return carry

    lax.fori_loop(0, rows, third, 0)
    gather.start()
    gather.forward()
    share.finish()
    gather.finish()


def norm_back(rows, width, incoming, values, gain, store, parts):
    zero = jnp.zeros((1, width), f32)

    def sums(d, total):
        return total + jnp.sum(values(d), axis=0, keepdims=True)

    mean = lax.fori_loop(0, rows, sums, zero) / D

    def squares(d, total):
        value = values(d) - mean
        return total + jnp.sum(value * value, axis=0, keepdims=True)

    scale = lax.rsqrt(lax.fori_loop(0, rows, squares, zero) / D + epsilon)

    def moments(d, totals):
        centred = (values(d) - mean) * scale
        back = incoming(d)
        parts(d, jnp.sum(back * centred, axis=1, keepdims=True), jnp.sum(back, axis=1, keepdims=True))
        scaled = back * gain(d)
        return (
            totals[0] + jnp.sum(scaled, axis=0, keepdims=True),
            totals[1] + jnp.sum(scaled * centred, axis=0, keepdims=True),
        )

    first, second = lax.fori_loop(0, rows, moments, (zero, zero))

    def last(d, carry):
        centred = (values(d) - mean) * scale
        scaled = incoming(d) * gain(d)
        store(d, scale * (scaled - first / D - centred * (second / D)))
        return carry

    lax.fori_loop(0, rows, last, 0)


def back_one_kernel(
    rows, cols, cot, cot_own, hidden, grad_pre, w_up, w_down, resid, vec,
    grad_down, grad_mid, branch, output, parts, branch_own, *scratch,
):
    p = Place(rows, cols)
    width = resid.shape[-1]
    share = Share(p, *scratch[:6])
    gather = Spread(p, branch_own, branch, width, *scratch[6:8])
    down = Reduce(p, cot, hidden, *scratch[8:11], scratch[11:15])
    share_out = Share(p, *scratch[15:21])
    meet(p.col_peers() + p.row_peers())
    fill_partial(share.part, w_up, grad_pre, cols, rows, width)
    share.start()
    down.send_pair()
    share.middle()
    fill_partial(share_out.part, w_down, hidden, cols, rows, width)
    share_out.start()
    share.arrive()

    def incoming(d):
        return share.total(d)

    def store(d, value):
        total = cot_own[d].astype(f32) + value
        grad_mid[d] = total
        low = total.astype(bf16)
        branch_own[d] = low
        parts[d, :, 2:3] = jnp.sum(low.astype(f32), axis=1, keepdims=True)
        parts[d, :, 3:4] = jnp.sum(cot_own[d].astype(f32), axis=1, keepdims=True)

    def put(d, gain, shift):
        parts[d, :, 0:1] = gain
        parts[d, :, 1:2] = shift

    norm_back(
        rows, width, incoming, lambda d: resid[d], lambda d: vec[d, :, 3:4], store, put
    )
    gather.start()
    share_out.middle()
    down.send_line()
    gather.forward()
    share_out.arrive()

    def result(d, carry):
        output[d] = (resid[d] + share_out.total(d) + vec[d, :, 5:6]).astype(bf16)
        return carry

    lax.fori_loop(0, rows, result, 0)
    down.finish(grad_down)
    share.finish()
    share_out.finish()
    gather.finish()


def back_two_kernel(
    rows, cols, normed_mid, grad_pre, branch, att, w_out, qkv, logs, normed_in, w_qkv,
    own, grad_mid, vec,
    grad_up, grad_out, grad_qkv_w, grad_tok, parts, grad_qkv, grad_att, dkey, dval, *scratch,
):
    p = Place(rows, cols)
    width = own.shape[-1]
    slots = logs.shape[0]
    share = Share(p, *scratch[:6])
    up = Reduce(p, normed_mid, grad_pre, *scratch[6:9], scratch[9:13])
    out = Reduce(p, branch, att, *scratch[13:16], scratch[16:20])
    wide = Reduce(p, normed_in, grad_qkv, *scratch[20:23], scratch[23:27])
    meet(p.col_peers() + p.row_peers())
    up.send_pair()
    for s in range(slots):
        total = product(w_out[0, :, s * HD : (s + 1) * HD], branch[0], TN)
        for d in range(1, rows):
            total = total + product(w_out[d, :, s * HD : (s + 1) * HD], branch[d], TN)
        grad_att[s * HD : (s + 1) * HD] = total.astype(bf16)
    out.send_pair()
    up.send_line()
    out.send_line()

    def head(s, carry):
        base = pl.multiple_of(s * CHANNELS, 64)

        def store(row, first, last, value):
            grad_qkv[pl.ds(base + row, HD), first:last] = value.astype(bf16)

        attend_back(
            qkv[pl.ds(base, CHANNELS)],
            grad_att[pl.ds(pl.multiple_of(s * HD, 64), HD)],
            logs[s],
            store,
            dkey,
            dval,
        )
        return carry

    lax.fori_loop(0, slots, head, 0)
    wide.send_pair()
    fill_partial(share.part, w_qkv, grad_qkv, cols, rows, width)
    share.start()
    wide.send_line()
    share.middle()
    up.finish(grad_up)
    out.finish(grad_out)
    share.arrive()

    def store_tokens(d, value):
        grad_tok[d] = (grad_mid[d] + value).astype(bf16)

    def put(d, gain, shift):
        parts[d, :, 0:1] = gain
        parts[d, :, 1:2] = shift

    norm_back(
        rows,
        width,
        lambda d: share.total(d),
        lambda d: own[d].astype(f32),
        lambda d: vec[d, :, 0:1],
        store_tokens,
        put,
    )
    wide.finish(grad_qkv_w)
    share.finish()


def call(kernel, outs, scratch, args, collective, spec=VMEM, out_specs=None):
    return pl.pallas_call(
        kernel,
        out_shape=[jax.ShapeDtypeStruct(s, t) for s, t in outs],
        in_specs=[spec] * len(args),
        out_specs=[spec] * len(outs) if out_specs is None else out_specs,
        scratch_shapes=scratch,
        compiler_params=pltpu.CompilerParams(
            collective_id=collective, has_side_effects=True, vmem_limit_bytes=LIMIT
        ),
    )(*args)


def one_hot(target, size):
    return (target[:, None] == jnp.arange(size, dtype=jnp.int32)[None, :]).astype(bf16)


def split_matrix(channels, slots, cols):
    source = jnp.arange(channels * H, dtype=jnp.int32)
    channel, head = source // H, source % H
    return one_hot(
        ((head % cols) * slots + head // cols) * channels + channel, cols * slots * channels
    )


def join_matrix(channels, slots, cols):
    source = jnp.arange(cols * slots * channels, dtype=jnp.int32)
    col, slot, channel = source // (slots * channels), source // channels % slots, source % channels
    return one_hot((slot * cols + col) * channels + channel, cols * slots * channels)


def to_owners(weight, matrix, cols):
    moved = product(weight, matrix, NN).astype(bf16)
    return moved.reshape(moved.shape[0], cols, -1).transpose(1, 0, 2)


def joined(blocks, matrix):
    flat = blocks.transpose(1, 0, 2).reshape(blocks.shape[1], -1)
    return product(flat, matrix, NN).astype(bf16)


def from_joined(gradient, matrix, cols):
    moved = product(gradient.astype(bf16), matrix, NT).astype(bf16)
    return moved.reshape(moved.shape[0], cols, -1).transpose(1, 0, 2)


def from_owners(blocks, matrix):
    flat = blocks.transpose(1, 0, 2).reshape(blocks.shape[1], -1)
    return product(flat, matrix, NT)


def whole_weight(weight):
    return lax.all_gather(weight, "row", axis=0, tiled=True)


def body(
    tokens, ln1_gain, ln1_shift, weight_qkv, bias_qkv, weight_out, bias_out, ln2_gain,
    ln2_shift, weight_up, bias_up, weight_down, bias_down, cotangent,
):
    rows, cols = lax.axis_size("row"), lax.axis_size("col")
    slots = (H + cols - 1) // cols
    ch, och = CHANNELS // cols, HD // cols
    feats = D // rows
    width = L // cols
    ffc = weight_up.shape[1]
    dma = pltpu.SemaphoreType.DMA

    qkv_split, out_split = split_matrix(ch, slots, cols), split_matrix(och, slots, cols)
    qkv_join, out_join = join_matrix(ch, slots, cols), join_matrix(och, slots, cols)
    wq = to_owners(weight_qkv, qkv_split, cols)
    wo = to_owners(weight_out, out_split, cols)
    bias = jnp.pad(bias_qkv.reshape(ch, H), ((0, 0), (0, slots * cols - H)))
    bias = bias.reshape(ch, slots, cols).transpose(2, 1, 0)
    zero = jnp.zeros_like(ln1_gain)
    vec = jnp.stack(
        [ln1_gain, ln1_shift, bias_out, ln2_gain, ln2_shift, bias_down, zero, zero]
    )
    both, own, wq, wo, bias, vec = call(
        functools.partial(enter_kernel, rows, cols),
        [
            ((2, rows, feats, L), bf16),
            ((2, rows, feats, width), bf16),
            (wq.shape, bf16),
            (wo.shape, bf16),
            (bias.shape, f32),
            ((rows,) + vec.shape, f32),
        ],
        [dma((rows,)), dma((rows,)), dma((5,)), dma((3, cols)), dma((3, cols))]
        + spread_sems(cols)
        + [dma((rows,)), dma((rows,))],
        (jnp.stack([tokens, cotangent]), wq, wo, bias, vec),
        1,
        ANY,
    )
    vec = vec.transpose(0, 2, 1)
    w_up = whole_weight(weight_up)
    w_qkv = whole_weight(joined(wq, qkv_join))
    w_out = whole_weight(joined(wo, out_join))
    w_down = whole_weight(weight_down)
    qkv_bias = bias.transpose(1, 0, 2).reshape(slots * CHANNELS, 1)

    chunked = lambda array: array.reshape(rows, feats, array.shape[-1])
    flat = lambda array: array.reshape(D, array.shape[-1])

    values = flat(both[0]).astype(f32)
    mean = jnp.mean(values, axis=0, keepdims=True)
    centred = values - mean
    scale = lax.rsqrt(jnp.mean(centred * centred, axis=0, keepdims=True) + epsilon)
    normed_in = (
        centred * scale * flat(vec[:, :, 0:1]) + flat(vec[:, :, 1:2])
    ).astype(bf16)
    qkv = (product(w_qkv, normed_in, TN) + qkv_bias).astype(bf16)
    att, logs = attend(qkv)

    resid, normed_mid = call(
        functools.partial(middle_kernel, rows, cols),
        [((rows, feats, width), f32), ((rows, feats, L), bf16)],
        [pltpu.VMEM((rows, feats, width), bf16)]
        + share_scratch(rows, cols, feats, width)
        + spread_sems(cols),
        (chunked(w_out), att, own[0], vec),
        2,
    )
    hidden_pre = product(w_up, flat(normed_mid), TN) + bias_up[:, None]
    hidden = jax.nn.gelu(hidden_pre, approximate=True).astype(bf16)
    grad_hidden = product(w_down, flat(both[1]), TN)
    gelu_back = jax.vjp(lambda inner: jax.nn.gelu(inner, approximate=True), hidden_pre)[1]
    grad_pre = gelu_back(grad_hidden)[0].astype(bf16)
    up_part = jnp.sum(grad_pre, axis=1, dtype=f32)

    grad_weight_down, grad_mid, branch, output, parts_two = call(
        functools.partial(back_one_kernel, rows, cols),
        [
            ((feats, ffc), f32),
            ((rows, feats, width), f32),
            ((rows, feats, L), bf16),
            ((rows, feats, width), bf16),
            ((rows, feats, 4), f32),
        ],
        [pltpu.VMEM((rows, feats, width), bf16)]
        + share_scratch(rows, cols, feats, width)
        + spread_sems(cols)
        + reduce_scratch(rows, feats, ffc)
        + share_scratch(rows, cols, feats, width),
        (both[1], own[1], hidden, grad_pre, chunked(w_up), chunked(w_down), resid, vec),
        3,
    )
    grad_weight_up, grad_out, grad_qkv_w, grad_tok, parts_one, grad_qkv = call(
        functools.partial(back_two_kernel, rows, cols),
        [
            ((feats, ffc), f32),
            ((feats, slots * HD), f32),
            ((feats, slots * CHANNELS), f32),
            ((rows, feats, width), bf16),
            ((rows, feats, 2), f32),
            ((slots * CHANNELS, L), bf16),
        ],
        [
            pltpu.VMEM((slots * HD, L), bf16),
            pltpu.VMEM((HD, L), f32),
            pltpu.VMEM((HD, L), f32),
        ]
        + share_scratch(rows, cols, feats, width)
        + reduce_scratch(rows, feats, ffc)
        + reduce_scratch(rows, feats, slots * HD)
        + reduce_scratch(rows, feats, slots * CHANNELS),
        (
            normed_mid, grad_pre, branch, att, chunked(w_out), qkv, logs,
            chunked(normed_in), chunked(w_qkv), own[0], grad_mid, vec,
        ),
        4,
    )
    qkv_part = jnp.sum(grad_qkv, axis=1, dtype=f32)

    feat = jnp.concatenate([parts_one, parts_two, jnp.zeros((rows, feats, 2), f32)], axis=2)
    feat = feat.transpose(0, 2, 1)
    units = jnp.concatenate([up_part, qkv_part])[None, :]
    gq = from_joined(grad_qkv_w, qkv_join, cols)
    go = from_joined(grad_out, out_join, cols)
    res, gq, go, feat, units = call(
        functools.partial(leave_kernel, rows, cols),
        [
            ((2, feats, rows * width), bf16),
            (gq.shape, bf16),
            (go.shape, bf16),
            ((cols,) + feat.shape[1:], f32),
            ((rows,) + units.shape, f32),
        ],
        [
            pltpu.VMEM(feat.shape, f32),
            pltpu.VMEM(feat.shape[1:], f32),
            dma((rows,)), dma((rows,)), dma((4,)), dma((3, cols)), dma((3, cols)),
            dma((rows,)), dma((rows,)), dma((rows,)), dma((rows,)),
        ],
        (jnp.stack([output, grad_tok]), gq, go, feat, units),
        5,
    )
    feat = jnp.sum(feat, axis=0)
    units = jnp.sum(units, axis=0)[0]
    grad_weight_qkv = from_owners(gq, qkv_split)
    grad_weight_out = from_owners(go, out_split)
    grads = lax.all_gather(units[ffc:].reshape(slots, cols, ch), "col", axis=0)
    mine = lax.dynamic_index_in_dim(grads, lax.axis_index("col"), axis=2, keepdims=False)
    grad_bias_qkv = mine.transpose(2, 1, 0).reshape(ch, slots * cols)[:, :H].reshape(-1)
    return (
        res[0],
        res[1].astype(f32),
        feat[0],
        feat[1],
        grad_weight_qkv,
        grad_bias_qkv,
        grad_weight_out,
        feat[4],
        feat[2],
        feat[3],
        grad_weight_up,
        units[:ffc],
        grad_weight_down,
        feat[5],
    )


def solution(mesh):
    both, row, col = P("row", "col"), P("row"), P("col")
    in_specs = (both, row, row, both, col, both, row, row, row, both, col, both, row, both)
    out_specs = (both, both, row, row, both, col, both, row, row, row, both, col, both, row)
    return jax.shard_map(body, mesh=mesh, in_specs=in_specs, out_specs=out_specs, check_vma=False)
```

time: 1470 us -> 850 us (0.58)
  waiting for transfers between devices: 924 us -> 204 us
  Pallas kernels: 0 us -> 508 us
  blocking collectives: 197 us -> 10.8 us
  starting transfers between devices: 93.2 us -> 0.16 us
  matrix products: 147 us -> 54 us
  other arithmetic: 44.7 us -> 20.2 us
    pallas_call x0 -> x6, Pallas kernels: none -> 508 us  [the longest x5 491 us: call(): pl.pallas_call(kernel, out_shape=[jax.ShapeDtypeStruct(s, t) for s, t in...]
    unnamed x18 -> x4, waiting for transfers between devices: 448 us -> 1.24 us
    reduce_scatter x5 -> x0, waiting for transfers between devices: 198 us -> none  [the longest x4 103 us: share(): lax.psum_scatter(values.astype(jnp.bfloat16), 'col', scatter_dimension=1,...]
    dot_general x58 -> x11, matrix products: 147 us -> 54 us  [product(): return lax.dot_general(left, right, dims, preferred_element_type=f32)]
    all_to_all x3 -> x0, blocking collectives: 81.9 us -> none  [the longest x1 60.6 us: to_blocks(): got = lax.all_to_all(split, 'row', split_axis=2, concat_axis=1)]
    all_to_all x4 -> x0, starting transfers between devices: 81.4 us -> none  [the longest x1 67.4 us: group_heads(): got = lax.all_to_all(moved, 'col', split_axis=1, concat_axis=1, tiled=True)]
    psum x2 -> x0, blocking collectives: 65.7 us -> none  [the longest x1 40.2 us: body(): features = lax.psum(features, ('row', 'col'))]
    all_gather x3 -> x0, waiting for transfers between devices: 62.7 us -> none  [the longest x2 62.3 us: spread(): return lax.all_gather(values, 'col', axis=1, tiled=True)]
  transfers between devices with their start and end apart: 22 -> 4, of which waited for: 15 -> 4; matrix products, arithmetic and copies ran while one was open for 9% -> 5% of each run, Pallas kernels for 0% -> 9%
where the time goes in v2:
time: 850 us; the launch traced here: 841 us
  Pallas kernels  508 us (60%)
  waiting for transfers between devices  204 us (24%)
  matrix products  54 us (6%)
  local copies, waits for them, and re-layouts  28.8 us (3%)
  other arithmetic  20.2 us (2%)
  between operations  14.7 us (2%)
  blocking collectives  10.8 us (1%)
    pallas_call x5, Pallas kernels, call(): pl.pallas_call(kernel, out_shape=[jax.ShapeDtypeStruct(s, t) for s, t in...  491 us
    all_gather x4, waiting for transfers between devices, whole_weight(): return lax.all_gather(weight, 'row', axis=0, tiled=True)  203 us
    dot_general x11, matrix products, product(): return lax.dot_general(left, right, dims, preferred_element_type=f32)  54 us
    pallas_call x1, Pallas kernels, attend(): pl.pallas_call(attend_kernel, grid=(slots,), out_shape=[jax.ShapeDtypeStr...  17.7 us
  transfers between devices with their start and end apart: 4, of which 4 were waited for; matrix products, arithmetic and copies ran while one was open for 5% of the time, Pallas kernels for 9%

profile of v2, /device:TPU:9, one launch (start us, length us, event | category | flops | bytes accessed | tf_op | source)
XLA Modules:
  0.0 841.2 jit_solution(8829891482540038219)
XLA Ops:
  7.3 0.9 reshape.305
  8.4 0.6 copy.89
  9.0 1.3 fusion.31
  10.3 0.2 reshape.304
  10.5 0.7 copy.88
  11.3 1.5 fusion.30
  12.8 0.6 reshape.303
  13.4 0.9 copy.86
  14.3 1.3 pad_maximum_fusion.tokcot
  15.7 0.6 stack.52.vec
  16.3 102.2 %shard_map.245 = (bf16[2,8,200,1024]{3,2,1,0:T(8,128)(2,1)}, bf16[2,8,200,256]{3,2,1,0:T(8,128)(2,1)}, bf16[4,200,336]{2,1,0:T(8,128)(2,1)}, bf16[4,200,112]{2,1...) custom-call(bf16[2,200,2048]{2,1,0:T(8,128)(2,1)} %pad_maximum_fusion.tokcot, ...), custom_call_target="tpu_custom_call" | custom-call | tf_op jit(solution)/shard_map/pallas_call | solution.py:764
  118.5 1.4 copy.67
  119.9 0.4 reshape.309
  120.3 2.6 fusion.28
  123.1 0.2 reshape.307
  123.3 1.1 convolution_convert_fusion.1
  124.5 0.7 all-gather.9.cloned.1.call-update
  125.2 0.5 all-gather.11.cloned.1.call-update
  125.9 1.2 copy.68
  127.0 2.3 slice_reduce_fusion.1
  129.6 2.7 convert_reduce_fusion.2
  132.3 2.8 multiply_reduce_fusion
  135.2 1.3 slice_bitcast_fusion.2
  136.4 3.7 slice_bitcast_fusion.3
  140.1 2.7 fusion.14.normed_in
  142.8 2.6 fusion.22
  145.4 78.4 %all-gather.7.cloned.1.call-done = bf16[1600,1344]{1,0:T(8,128)(2,1)} async-done(((bf16[200,1344]{1,0:T(8,128)(2,1)}), bf16[1600,1344]{1,0:T(8,128)(2,1)}) %all-gather.7.cloned.1.call-update) | async-done | bytes 4300816 | tf_op jit(solution)/shard_map/all_gather | solution.py:815
  223.8 9.4 %add_convert_fusion.qkv = bf16[1344,1024]{1,0:T(8,128)(2,1)} fusion(bf16[1600,1344]{1,0:T(8,128)(2,1)} %all-gather.7.cloned.1.call-done, bf16[1600,1024]{1,0:T(8,128)(2,1)} %fusion.22, f32[1344]{0:T(1024)S(1)} %add.285), kind=kOutput, calls=%fused_computation.35 | convolution fusion | flops 4406771712 | bytes 10335488 | tf_op jit(solution)/shard_map/dot_general | solution.py:32
  233.2 17.7 %shard_map.246 = (bf16[448,1024]{1,0:T(8,128)(2,1)}, f32[7,1,1024]{2,1,0:T(1,128)}) custom-call(bf16[1344,1024]{1,0:T(8,128)(2,1)} %add_convert_fusion.qkv), custom_call_target="tpu_custom_call" | custom-call | flops 1879048192 | bytes 4194304 | tf_op jit(solution)/shard_map/pallas_call | solution.py:530
  250.9 20.0 %all-gather.5.cloned.1.call-done = bf16[1600,448]{1,0:T(8,128)(2,1)} async-done(((bf16[200,448]{1,0:T(8,128)(2,1)}), bf16[1600,448]{1,0:T(8,128)(2,1)}) %all-gather.5.cloned.1.call-update) | async-done | bytes 1433616 | tf_op jit(solution)/shard_map/all_gather | solution.py:815
  270.9 56.0 %shard_map.247 = (f32[8,200,256]{2,1,0:T(8,128)}, bf16[8,200,1024]{2,1,0:T(8,128)(2,1)}) custom-call(bf16[8,200,448]{2,1,0:T(8,128)(2,1)} %bitcast.134, bf16[448,1024]{1,0:T(8,128)(2,1)} %get-tuple-element.46.att, bf16[8,200,256]{2,1,0:T(8,128)(2,1)} %get-tuple-element.73.own, f32[8,200,8]{2,1,0:T(8,128)} %bitcast.131), custom_call_target="tpu_custom_call" | custom-call | tf_op jit(solution)/shard_map/pallas_call | solution.py:764
  326.9 30.5 %all-gather.9.cloned.1.call-done = bf16[1600,1600]{1,0:T(8,128)(2,1)} async-done(((bf16[200,1600]{1,0:T(8,128)(2,1)}), bf16[1600,1600]{1,0:T(8,128)(2,1)}) %all-gather.9.cloned.1.call-update) | async-done | bytes 5120016 | tf_op jit(solution)/shard_map/all_gather | solution.py:815
  357.4 13.4 %fusion.18 = (bf16[1600,1024]{1,0:T(8,128)(2,1)}, f32[1024,1600]{0,1:T(8,128)}) fusion(f32[1600]{0:T(1024)S(1)} %copy-done.19, bf16[1600,1024]{1,0:T(8,128)(2,1)} %bitcast.139, bf16[1600,1600]{1,0:T(8,128)(2,1)} %all-gather.9.cloned.1.call-done), kind=kOutput, calls=%fused_computation.26 | convolution fusion | flops 5259264000 | bytes 18233600 | tf_op jit(solution)/shard_map/dot_general | solution.py:32
  370.8 74.1 %all-gather.11.cloned.1.call-done = bf16[1600,1600]{1,0:T(8,128)(2,1)} async-done(((bf16[200,1600]{1,0:T(8,128)(2,1)}), bf16[1600,1600]{1,0:T(8,128)(2,1)}) %all-gather.11.cloned.1.call-update) | async-done | bytes 5120016 | tf_op jit(solution)/shard_map/all_gather | solution.py:815
  444.9 16.6 %convert_reduce_fusion = (f32[1600]{0:T(1024)S(1)}, bf16[1600,1024]{1,0:T(8,128)(2,1)}) fusion(f32[1024,1600]{0,1:T(8,128)} %get-tuple-element.81, f32[1600]{0:T(1024)S(1)} %copy-done.19, bf16[1600,1024]{1,0:T(8,128)(2,1)} %bitcast.140, bf16[1600,1600]{1,0:T(8,128)(2,1)} %all-gather.11.cloned.1.call-done), kind=kOutput, calls=%fused_computation.32 | convolution fusion | flops 5280561664 | bytes 18240000 | tf_op jit(solution)/shard_map/dot_general | solution.py:32
  461.6 110.7 %shard_map.248 = (f32[200,1600]{1,0:T(8,128)}, f32[8,200,256]{2,1,0:T(8,128)}, bf16[8,200,1024]{2,1,0:T(8,128)(2,1)}, bf16[8,200,256]{2,1,0:T(8,128)(2,1)}, f32[8,200,4]{2,1,0:T(8,128)}) custom-call(bf16[8,200,1024]{2,1,0:T(8,128)(2,1)} %get-tuple-element.68.cot, bf16[8,200,256]{2,1,0:T(8,128)(2,1)} %get-tuple-element.72.cot_own, ...), custom_call_target="tpu_custom_call" | custom-call | tf_op jit(solution)/shard_map/pallas_call | solution.py:764
  572.3 176.3 %shard_map.249 = (f32[200,1600]{1,0:T(8,128)}, f32[200,448]{1,0:T(8,128)}, f32[200,1344]{1,0:T(8,128)}, bf16[8,200,256]{2,1,0:T(8,128)(2,1)}, f32[8,200,2]{2,1,0:T(8,128)}, /*index=5*/bf16[1344,1024]{1,0:T(8,128)(2,1)}) custom-call(bf16[8,200,1024]{2,1,0:T(8,128)(2,1)} %get-tuple-element.47.normed_mid, bf16[1600,1024]{1,0:T(8,128)(2,1)} %get-tuple-element.83.grad_pre, ...), custom_call_target="tpu_custom_call" | custom-call | tf_op jit(solution)/shard_map/pallas_call | solution.py:764
  748.6 2.3 convert_reduce_fusion.1
  751.0 0.6 broadcast_in_dim.5.units
  751.7 1.5 copy.72
  753.1 1.5 copy.73
  754.6 1.5 convolution_convert_fusion
  756.2 0.7 copy.87
  757.0 2.9 fusion.29
  759.9 0.6 reshape.314
  760.5 0.9 copy.85
  761.4 1.3 pad_maximum_fusion.1.blocks
  762.7 0.7 maximum_bitcast_fusion.feat
  763.4 45.4 %shard_map.250 = (bf16[2,200,2048]{2,1,0:T(8,128)(2,1)}, bf16[4,200,336]{2,1,0:T(8,128)(2,1)}, bf16[4,200,112]{2,1,0:T(8,128)(2,1)}, f32[4,8,200]{2,1,0:T(8,128)}, f32[8,1,2944]{2,1,0:T(1,128)}) custom-call(bf16[2,8,200,256]{3,2,1,0:T(8,128)(2,1)} %pad_maximum_fusion.1.blocks, bf16[4,200,336]{2,1,0:T(8,128)(2,1)} %bitcast.141, ...), custom_call_target="tpu_custom_call" | custom-call | tf_op jit(solution)/shard_map/pallas_call | solution.py:764
  808.8 1.1 reduce_sum.61
  809.9 0.6 slice_reduce_fusion.2
  810.6 0.8 reduce_sum.60
  811.4 0.6 fusion.96
  812.1 10.8 %all_gather.19 = f32[4,7,4,48]{3,2,1,0:T(4,128)S(1)} all-gather(f32[1,7,4,48]{3,2,1,0:T(4,128)S(1)} %all_gather_reshape.3), channel_id=1, replica_groups=mesh['row'=8,'col'=4] {'col'}, dimensions={0}, use_global_device_ids=true | all-gather | bytes 26880 | tf_op jit(solution)/shard_map/all_gather | solution.py:964
  823.0 0.7 reshape.318
  823.8 1.0 copy.77
  824.8 0.2 reshape.319
  825.0 1.2 fusion.32
  826.1 1.3 copy.74
  827.5 0.4 reshape.316
  827.9 2.5 fusion.2
  830.4 1.6 bitcast_convert_fusion
  832.1 1.1 copy.93
  833.1 1.1 copy.94
  (77 shorter events, 1.4 us)
Async XLA Ops:
  7.2 4.0 copy-start
  7.2 7.1 copy-start.6
  7.2 7.1 copy-start.7
  7.2 216.6 %all-gather.7.cloned.1.call-start = ((), (), s32[]{:S(2)}) async-start(), calls=%async_computation.1 | async-start | bytes 5068800 | tf_op jit(solution)/shard_map/all_gather | solution.py:815
  11.2 4.4 copy-start.13
  11.2 4.4 copy-start.14
  11.2 4.4 copy-start.15
  11.2 4.4 copy-start.16
  11.2 4.4 copy-start.17
  11.2 4.4 copy-start.18
  118.5 4.5 copy-start.10
  118.5 7.2 copy-start.12
  118.5 7.3 copy-start.11
  123.0 147.9 %all-gather.5.cloned.1.call-start = ((), (), s32[]{:S(2)}) async-start(), calls=%async_computation | async-start | bytes 1843200 | tf_op jit(solution)/shard_map/all_gather | solution.py:815
  124.4 232.9 %all-gather.9.cloned.1.call-start = ((), (), s32[]{:S(2)}) async-start(), calls=%async_computation.2 | async-start | bytes 5990400 | tf_op jit(solution)/shard_map/all_gather | solution.py:815
  125.2 11.3 %slice-start = ((s8[6553600]{0:T(1024)(128)(4,1)}), s8[2359296]{0:T(1024)(128)(4,1)S(1)}, s32[]{:S(2)}) async-start(s8[6553600]{0:T(1024)(128)(4,1)} %bitcast.128), calls=%async_computation.4 | async-start | bytes 4718592
  125.2 319.7 %all-gather.11.cloned.1.call-start = ((), (), s32[]{:S(2)}) async-start(), calls=%async_computation.3 | async-start | bytes 5990400 | tf_op jit(solution)/shard_map/all_gather | solution.py:815
  129.5 5.7 copy-start.2
  129.6 6.8 slice-start.1
  233.2 124.2 %copy-start.19 = (f32[1600]{0:T(1024)S(1)}, f32[1600]{0:T(1024)}, u32[]{:S(2)}) copy-start(f32[1600]{0:T(1024)} %param.24) | copy-start | bytes 19204
  748.6 12.8 %copy-start.8 = (bf16[8,200,256]{2,1,0:T(8,128)(2,1)S(1)}, bf16[8,200,256]{2,1,0:T(8,128)(2,1)}, u32[]{:S(2)}) copy-start(bf16[8,200,256]{2,1,0:T(8,128)(2,1)} %get-tuple-element.49) | copy-start | bytes 2457604
  748.6 12.8 %copy-start.9 = (bf16[8,200,256]{2,1,0:T(8,128)(2,1)S(1)}, bf16[8,200,256]{2,1,0:T(8,128)(2,1)}, u32[]{:S(2)}) copy-start(bf16[8,200,256]{2,1,0:T(8,128)(2,1)} %get-tuple-element.53) | copy-start | bytes 2457604
  808.8 21.6 %copy-start.3 = (bf16[2,200,2048]{2,1,0:T(8,128)(2,1)S(1)}, bf16[2,200,2048]{2,1,0:T(8,128)(2,1)}, u32[]{:S(2)}) copy-start(bf16[2,200,2048]{2,1,0:T(8,128)(2,1)} %get-tuple-element.59) | copy-start | bytes 4915204
  827.5 6.7 copy-start.1
  827.9 4.1 copy-start.5
  827.9 5.2 copy-start.4
Sparse Core Ops, SparseCore 0:
  123.1 100.6 all-gather.6
  226.6 44.2 all-gather.4
  273.1 84.2 all-gather.8
  359.4 85.4 all-gather.10

commit v3 on v2

v3 whole, which is shorter than its diff:
```python
import functools

import jax
import jax.numpy as jnp
from jax import lax
from jax.experimental import pallas as pl
from jax.experimental.pallas import tpu as pltpu
from jax.sharding import PartitionSpec as P

D = 1600
H = 25
HD = 64
L = 1024
CHANNELS = 3 * HD
QB = 256

epsilon = 1e-05
excluded = -1e30

TN = (((0,), (0,)), ((), ()))
NN = (((1,), (0,)), ((), ()))
NT = (((1,), (1,)), ((), ()))
MESH = pl.DeviceIdType.MESH
ANY = pl.BlockSpec(memory_space=pl.ANY)
VMEM = pl.BlockSpec(memory_space=pltpu.VMEM)
LIMIT = 62 * 2**20
f32 = jnp.float32
bf16 = jnp.bfloat16


def product(left, right, dims):
    return lax.dot_general(left, right, dims, preferred_element_type=f32)


def remote(src, dst, send, recv, device):
    return pltpu.make_async_remote_copy(
        src_ref=src,
        dst_ref=dst,
        send_sem=send,
        recv_sem=recv,
        device_id=device,
        device_id_type=MESH,
    )


def meet(devices):
    sem = pltpu.get_barrier_semaphore()
    for device in devices:
        pl.semaphore_signal(sem, inc=1, device_id=device, device_id_type=MESH)
    pl.semaphore_wait(sem, len(devices))


def lanes(index, width):
    return pl.ds(pl.multiple_of(index * width, 128), width)


class Place:
    def __init__(self, rows, cols):
        self.R, self.C, self.A, self.X = rows, cols, rows // 2, cols // 2
        self.r, self.c = lax.axis_index("row"), lax.axis_index("col")
        self.a, self.b = self.r // 2, lax.rem(self.r, 2)
        self.x, self.k = self.c // 2, lax.rem(self.c, 2)
        self.core = (self.r, self.x * 2 + 1 - self.k)
        self.pair = (self.a * 2 + 1 - self.b, self.c)
        self.pos = jnp.where(self.b == 0, self.a, rows - 1 - self.a)
        self.around = [(self.row_at(1), self.c), (self.row_at(-1), self.c)]

    def row_at(self, o):
        at = lax.rem(self.pos + o + self.R, self.R)
        return jnp.where(at < self.A, at * 2, (self.R - 1 - at) * 2 + 1)

    def ahead(self, o):
        return lax.rem(self.a + o, self.A)

    def behind(self, o):
        return lax.rem(self.a - o + self.A, self.A)

    def line(self, o):
        return (self.ahead(o) * 2 + self.b, self.c)

    def x_ahead(self, o):
        return lax.rem(self.x + o, self.X)

    def x_behind(self, o):
        return lax.rem(self.x - o + self.X, self.X)

    def side(self, o):
        return (self.r, self.x_ahead(o) * 2 + self.k)

    def col_peers(self):
        return [self.core] + [self.side(o) for o in range(1, self.X)]

    def row_peers(self):
        return [self.pair] + [self.line(o) for o in range(1, self.A)]


class Spread:
    def __init__(self, p, own, full, width, send, recv):
        self.p, self.own, self.full, self.width = p, own, full, width
        self.send, self.recv = send, recv

    def part(self, block):
        return self.full.at[..., lanes(block, self.width)]

    def side_copy(self, o):
        return remote(
            self.own, self.part(self.p.c), self.send.at[o], self.recv.at[o], self.p.side(o)
        )

    def core_copy(self, o):
        p = self.p
        block = p.c if o == 0 else p.x_behind(o) * 2 + p.k
        src = self.own if o == 0 else self.part(block)
        i = p.X + o
        return remote(src, self.part(block), self.send.at[i], self.recv.at[i], p.core)

    def local(self):
        i = 2 * self.p.X
        return pltpu.make_async_copy(self.own, self.part(self.p.c), self.send.at[i])

    def start(self):
        for o in range(1, self.p.X):
            self.side_copy(o).start()
        self.core_copy(0).start()
        self.local().start()

    def forward(self):
        for o in range(1, self.p.X):
            self.side_copy(o).wait_recv()
            self.core_copy(o).start()

    def finish(self):
        for o in range(self.p.X):
            self.core_copy(o).wait()
        for o in range(1, self.p.X):
            self.side_copy(o).wait_send()
        self.local().wait()


def spread_sems(cols):
    return [pltpu.SemaphoreType.DMA((cols + 1,)), pltpu.SemaphoreType.DMA((cols + 1,))]


class Share:
    def __init__(self, p, part, core_in, side_out, side_in, send, recv):
        self.p, self.part, self.core_in = p, part, core_in
        self.side_out, self.side_in, self.send, self.recv = side_out, side_in, send, recv

    def core_copy(self, x):
        p = self.p
        return remote(
            self.part.at[x * 2 + 1 - p.k],
            self.core_in.at[x],
            self.send.at[x],
            self.recv.at[x],
            p.core,
        )

    def side_copy(self, o):
        p = self.p
        i = p.X + o - 1
        return remote(
            self.side_out.at[o - 1],
            self.side_in.at[o - 1],
            self.send.at[i],
            self.recv.at[i],
            p.side(o),
        )

    def start(self):
        for x in range(self.p.X):
            self.core_copy(x).start()

    def middle(self):
        p = self.p
        for x in range(p.X):
            self.core_copy(x).wait_recv()
        for o in range(1, p.X):
            x = p.x_ahead(o)

            def add(d, carry, x=x, o=o):
                total = self.part[x * 2 + p.k, d].astype(f32) + self.core_in[x, d].astype(f32)
                self.side_out[o - 1, d] = total.astype(bf16)
                return carry

            lax.fori_loop(0, p.R, add, 0)
            self.side_copy(o).start()

    def arrive(self):
        for o in range(1, self.p.X):
            self.side_copy(o).wait_recv()

    def total(self, d):
        p = self.p
        result = self.part[p.c, d].astype(f32) + self.core_in[p.x, d].astype(f32)
        for o in range(1, p.X):
            result = result + self.side_in[o - 1, d].astype(f32)
        return result

    def finish(self):
        for x in range(self.p.X):
            self.core_copy(x).wait_send()
        for o in range(1, self.p.X):
            self.side_copy(o).wait_send()


def share_scratch(rows, cols, feats, width):
    half = cols // 2
    return [
        pltpu.VMEM((cols, rows, feats, width), bf16),
        pltpu.VMEM((half, rows, feats, width), bf16),
        pltpu.VMEM((half - 1, rows, feats, width), bf16),
        pltpu.VMEM((half - 1, rows, feats, width), bf16),
        pltpu.SemaphoreType.DMA((cols - 1,)),
        pltpu.SemaphoreType.DMA((cols - 1,)),
    ]


def fill_partial(part, weight, act, cols, rows, width):
    def one(d, carry):
        for j in range(cols):
            part[j, d] = product(
                weight[d], act[:, j * width : (j + 1) * width], NN
            ).astype(bf16)
        return carry

    lax.fori_loop(0, rows, one, 0)


def middle(size, extra):
    return min((size // 256 + extra) * 128, (size - 1) // 128 * 128)


class Reduce:
    def __init__(self, p, left, right, scratch, cut):
        self.p, self.left, self.right = p, left, right
        self.slots, self.send, self.recv = scratch
        self.parts = (slice(0, cut), slice(cut, self.slots.shape[-1]))

    def copy(self, way, t):
        part = self.parts[way]
        i = way * self.p.R + t
        return remote(
            self.slots.at[t, :, part],
            self.slots.at[t + 1, :, part],
            self.send.at[i],
            self.recv.at[i],
            self.p.around[way],
        )

    def step(self, t):
        p = self.p
        for way in range(2):
            part = self.parts[way]
            row = p.row_at(-1 - t if way == 0 else 1 + t)
            value = product(self.left[row], self.right[part], NT)
            if t > 0:
                self.copy(way, t - 1).wait_recv()
                value = value + self.slots[t, :, part].astype(f32)
            if t < p.R - 1:
                self.slots[t, :, part] = value.astype(bf16)
                self.copy(way, t).start()
            else:
                self.out[:, part] = value.astype(self.out.dtype)

    def into(self, out):
        self.out = out
        return self

    def finish(self):
        for way in range(2):
            for t in range(self.p.R - 1):
                self.copy(way, t).wait_send()


def reduce_scratch(rows, feats, size):
    return [
        pltpu.VMEM((rows, feats, size), bf16),
        pltpu.SemaphoreType.DMA((2 * rows,)),
        pltpu.SemaphoreType.DMA((2 * rows,)),
    ]


def steps(rows, *rings):
    return [(ring, t) for t in range(rows) for ring in rings]


def serve(queue, t):
    while queue and queue[0][1] <= t:
        ring, at = queue.pop(0)
        ring.step(at)


def home(p, q):
    block = p.c * p.R + q
    return (block // p.C, lax.rem(block, p.C))


def own_block(p):
    block = p.r * p.C + p.c
    return block // p.R, lax.rem(block, p.R)


def equal(left, right):
    return jnp.logical_and(left[0] == right[0], left[1] == right[1])


def exchange_copies(p, src, dst, send, recv):
    out = []
    for o in range(1, p.C):
        to = lax.rem(p.c + o, p.C)
        out.append(remote(src.at[to], dst.at[p.c], send.at[o], recv.at[o], (p.r, to)))
    return out


def all_col(p):
    return [(p.r, lax.rem(p.c + o, p.C)) for o in range(1, p.C)]


def all_row(p):
    return [(lax.rem(p.r + o, p.R), p.c) for o in range(1, p.R)]


class Back:
    def __init__(self, p, src, dst, sems):
        self.p, self.src, self.dst = p, src, dst
        self.send, self.recv = sems
        self.width = src.shape[-1]
        self.col, self.place = own_block(p)

    def slot(self, q):
        return self.dst.at[:, lanes(q, self.width)]

    def outgoing(self, q):
        return remote(
            self.src.at[q],
            self.slot(self.place),
            self.send.at[q],
            self.recv.at[self.place],
            (q, self.col),
        )

    def staying(self, q):
        return pltpu.make_async_copy(
            self.src.at[q], self.slot(self.place), self.send.at[self.p.R]
        )

    def start(self):
        p = self.p
        for q in range(p.R):
            here = equal((q, self.col), (p.r, p.c))

            @pl.when(here)
            def _():
                self.staying(q).start()

            @pl.when(jnp.logical_not(here))
            def _():
                self.outgoing(q).start()

    def finish(self):
        p = self.p
        for q in range(p.R):
            source = home(p, q)
            here = equal(source, (p.r, p.c))

            @pl.when(here)
            def _():
                self.staying(0).wait()

            @pl.when(jnp.logical_not(here))
            def _():
                remote(
                    self.src.at[0], self.slot(q), self.send.at[0], self.recv.at[q], source
                ).wait_recv()

        for q in range(p.R):

            @pl.when(jnp.logical_not(equal((q, self.col), (p.r, p.c))))
            def _():
                self.outgoing(q).wait_send()


def masked_scores(key, query, first):
    scores = product(key, query, TN) * HD ** (-0.5)
    keys = lax.broadcasted_iota(jnp.int32, scores.shape, 0)
    queries = lax.broadcasted_iota(jnp.int32, scores.shape, 1) + first
    return jnp.where(keys <= queries, scores, excluded)


def attend_back(qkv, grad, logs, out, dkey, dval):
    query, key, value = qkv[:HD], qkv[HD : 2 * HD], qkv[2 * HD :]
    dkey[...] = jnp.zeros_like(dkey)
    dval[...] = jnp.zeros_like(dval)
    for first in range(0, L, QB):
        last = first + QB
        scores = masked_scores(key[:, :last], query[:, first:last], first)
        weights = jnp.exp(scores - logs[:, first:last])
        back = grad[:, first:last]
        dval[:, :last] += product(back, weights.astype(bf16), NT)
        grad_weights = product(value[:, :last], back, TN)
        inner = jnp.sum(weights * grad_weights, axis=0, keepdims=True)
        low = (weights * (grad_weights - inner)).astype(bf16)
        out(0, first, last, product(key[:, :last], low, NN) * HD ** (-0.5))
        dkey[:, :last] += product(query[:, first:last], low, NT)
    out(HD, 0, L, dkey[...] * HD ** (-0.5))
    out(2 * HD, 0, L, dval[...])


def norm_back(rows, width, incoming, values, gain, store, parts):
    zero = jnp.zeros((1, width), f32)

    def sums(d, total):
        return total + jnp.sum(values(d), axis=0, keepdims=True)

    mean = lax.fori_loop(0, rows, sums, zero) / D

    def squares(d, total):
        value = values(d) - mean
        return total + jnp.sum(value * value, axis=0, keepdims=True)

    scale = lax.rsqrt(lax.fori_loop(0, rows, squares, zero) / D + epsilon)

    def moments(d, totals):
        centred = (values(d) - mean) * scale
        back = incoming(d)
        parts(d, jnp.sum(back * centred, axis=1, keepdims=True), jnp.sum(back, axis=1, keepdims=True))
        scaled = back * gain(d)
        return (
            totals[0] + jnp.sum(scaled, axis=0, keepdims=True),
            totals[1] + jnp.sum(scaled * centred, axis=0, keepdims=True),
        )

    first, second = lax.fori_loop(0, rows, moments, (zero, zero))

    def last(d, carry):
        centred = (values(d) - mean) * scale
        scaled = incoming(d) * gain(d)
        store(d, scale * (scaled - first / D - centred * (second / D)))
        return carry

    lax.fori_loop(0, rows, last, 0)


class Ring:
    def __init__(self, p, own, full, sems, cut):
        self.p, self.own, self.full = p, own, full
        self.send, self.recv = sems
        self.parts = (slice(0, cut), slice(cut, own.shape[1]))

    def copy(self, way, t):
        p = self.p
        row = p.row_at(-t if way == 0 else t)
        part = self.parts[way]
        i = way * p.R + t
        return remote(
            self.own.at[:, part] if t == 0 else self.full.at[row, :, part],
            self.full.at[row, :, part],
            self.send.at[i],
            self.recv.at[i],
            p.around[way],
        )

    def local(self):
        return pltpu.make_async_copy(
            self.own, self.full.at[self.p.r], self.send.at[self.p.R - 1]
        )

    def step(self, t):
        if t == 0:
            self.local().start()
        for way in range(2):
            if t > 0:
                self.copy(way, t - 1).wait_recv()
            if t < self.p.R - 1:
                self.copy(way, t).start()
        if t == self.p.R - 1:
            self.local().wait()

    def finish(self):
        for way in range(2):
            for t in range(self.p.R - 1):
                self.copy(way, t).wait_send()


class Redistribute:
    def __init__(self, p, src, own, sems):
        self.p, self.src, self.own = p, src, own
        self.send, self.recv = sems
        self.width = own.shape[-1]
        self.col, _ = own_block(p)

    def outgoing(self, q, target):
        return remote(
            self.src.at[:, q * self.width : (q + 1) * self.width],
            self.own.at[self.p.r],
            self.send.at[q],
            self.recv.at[self.p.r],
            target,
        )

    def staying(self, q):
        return pltpu.make_async_copy(
            self.src.at[:, q * self.width : (q + 1) * self.width],
            self.own.at[self.p.r],
            self.send.at[self.p.R],
        )

    def start(self):
        p = self.p
        for q in range(p.R):
            target = home(p, q)
            here = equal(target, (p.r, p.c))

            @pl.when(here)
            def _():
                self.staying(q).start()

            @pl.when(jnp.logical_not(here))
            def _():
                self.outgoing(q, target).start()

    def arrive(self):
        p = self.p
        for q in range(p.R):
            here = equal((q, self.col), (p.r, p.c))

            @pl.when(here)
            def _():
                self.staying(0).wait()

            @pl.when(jnp.logical_not(here))
            def _():
                remote(
                    self.src.at[:, 0 : self.width],
                    self.own.at[q],
                    self.send.at[0],
                    self.recv.at[q],
                    (q, self.col),
                ).wait_recv()

    def finish(self):
        p = self.p
        for q in range(p.R):
            target = home(p, q)

            @pl.when(jnp.logical_not(equal(target, (p.r, p.c))))
            def _():
                self.outgoing(q, target).wait_send()


def norm_scale(rows, width, values):
    zero = jnp.zeros((1, width), f32)

    def sums(d, total):
        return total + jnp.sum(values(d), axis=0, keepdims=True)

    mean = lax.fori_loop(0, rows, sums, zero) / D

    def squares(d, total):
        value = values(d) - mean
        return total + jnp.sum(value * value, axis=0, keepdims=True)

    return mean, lax.rsqrt(lax.fori_loop(0, rows, squares, zero) / D + epsilon)


def tiled(size, tile, one):
    count = size // tile

    def step(i, carry):
        one(pl.multiple_of(i * tile, tile), tile)
        return carry

    lax.fori_loop(0, count, step, 0)
    if size % tile:
        one(count * tile, size % tile)


def summed(weight, act, rows, first, size):
    total = product(weight[0, :, pl.ds(first, size)], act[0], TN)
    for d in range(1, rows):
        total = total + product(weight[d, :, pl.ds(first, size)], act[d], TN)
    return total


def forward_kernel(
    rows, cols,
    tok, cot, wq, wo, bias, vec, wu, wd, bias_up,
    wq_f, wo_f, wu_f, wd_f, n1_f, qkv_f, att_f, logs_f, resid_f, n2_f, hidden_f, gp_f,
    cot_f, tok_own_f, cot_own_f, vec_f,
    qfull, ofull, ufull, dfull, qown, oown, qin, oin, bin_, qbias, vin, vecs,
    xfull, n1, qkv, att, logs, resid, normed, n2, hidden, gp, cfull, tok_own, cot_own,
    part, core_in, side_out, side_in, share_s, share_r,
    qs, qr, os_, or_, us, ur, ds0, dr0, ts, tr, cs, cr,
    xs, xr, ys, yr, ns, nr, es, er, vs, vr, loc,
):
    p = Place(rows, cols)
    width = tok_own.shape[-1]
    slots = logs.shape[0]
    ch = CHANNELS // cols
    ffc = hidden.shape[0]
    red_tok = Redistribute(p, tok, tok_own, (ts, tr))
    red_cot = Redistribute(p, cot, cot_own, (cs, cr))
    sources = [(q, red_tok.col) for q in range(rows)]
    targets = [home(p, q) for q in range(rows)]
    meet(sources + targets + all_col(p) + all_row(p))

    groups = ((wq, qin), (wo, oin), (bias, bin_))
    swaps = []
    for i, (src, dst) in enumerate(groups):
        swaps.append(exchange_copies(p, src, dst, es.at[i], er.at[i]))
    for copies in swaps:
        for copy in copies:
            copy.start()
    keeps = [
        pltpu.make_async_copy(src.at[p.c], dst.at[p.c], loc.at[i])
        for i, (src, dst) in enumerate(groups)
    ]
    keeps.append(pltpu.make_async_copy(vec, vin.at[p.r], loc.at[3]))
    for copy in keeps:
        copy.start()
    red_tok.start()
    vec_copies = [
        remote(vec, vin.at[p.r], vs.at[o], vr.at[o], peer)
        for o, peer in enumerate(all_row(p))
    ]
    for copy in vec_copies:
        copy.start()

    for copies, keep in zip(swaps, keeps):
        for copy in copies:
            copy.wait_recv()
        keep.wait()
    och = HD // cols
    for j in range(cols):
        for s in range(slots):
            base = s * CHANNELS + j * ch
            qown[:, base : base + ch] = qin[j, :, s * ch : (s + 1) * ch]
            qbias[:, base : base + ch] = bin_[j, :, s * ch : (s + 1) * ch]
            base = s * HD + j * och
            oown[:, base : base + och] = oin[j, :, s * och : (s + 1) * och]
    ring_q = Ring(p, qown, qfull, (qs, qr), middle(slots * CHANNELS, 0))
    ring_o = Ring(p, oown, ofull, (os_, or_), middle(slots * HD, 1))
    ring_u = Ring(p, wu, ufull, (us, ur), middle(ffc, 0))
    ring_d = Ring(p, wd, dfull, (ds0, dr0), middle(ffc, 1))
    early = steps(rows, ring_q, ring_o)
    late = steps(rows, ring_u, ring_d)
    serve(early, 0)
    red_tok.arrive()
    spread_x = Spread(p, tok_own, xfull, width, xs, xr)
    spread_x.start()
    serve(early, rows * 1 // 8)
    for copy in vec_copies:
        copy.wait_recv()
    keeps[3].wait()
    eye = (
        lax.broadcasted_iota(jnp.int32, (8, 8), 0) == lax.broadcasted_iota(jnp.int32, (8, 8), 1)
    ).astype(f32)
    for d in range(rows):
        vecs[d] = lax.dot_general(
            vin[d], eye, TN, precision=lax.Precision.HIGHEST, preferred_element_type=f32
        )
    spread_x.forward()
    serve(early, rows * 2 // 8)
    spread_x.finish()
    outs = []

    def keep_out(src, dst):
        copy = pltpu.make_async_copy(src, dst, loc.at[4 + len(outs)])
        copy.start()
        outs.append(copy)

    keep_out(tok_own, tok_own_f)
    keep_out(vecs, vec_f)
    mean, scale = norm_scale(rows, L, lambda d: xfull[d].astype(f32))
    serve(early, rows * 3 // 8)

    def normal(d, carry):
        value = (xfull[d].astype(f32) - mean) * scale
        n1[d] = (value * vecs[d, :, 0:1] + vecs[d, :, 1:2]).astype(bf16)
        return carry

    lax.fori_loop(0, rows, normal, 0)
    keep_out(n1, n1_f)

    serve(early, rows - 2)
    serve(late, 0)
    red_cot.start()
    serve(early, rows)
    keep_out(qfull, wq_f)
    keep_out(ofull, wo_f)
    ones = jnp.ones((8, L), bf16)

    def project(first, size):
        total = product(qbias[:, pl.ds(first, size)], ones, TN)
        total = total + summed(qfull, n1, rows, first, size)
        qkv[pl.ds(first, size)] = total.astype(bf16)

    tiled(slots * CHANNELS, 384, project)
    keep_out(qkv, qkv_f)

    def head(s, carry):
        base = s * CHANNELS
        rows_of = lambda part: pl.ds(pl.multiple_of(base + part * HD, HD), HD)
        query, key, value = qkv[rows_of(0)], qkv[rows_of(1)], qkv[rows_of(2)]
        for first in range(0, L, QB):
            last = first + QB
            scores = masked_scores(key[:, :last], query[:, first:last], first)
            peak = jnp.max(scores, axis=0, keepdims=True)
            weights = jnp.exp(scores - peak)
            total = jnp.sum(weights, axis=0, keepdims=True)
            low = (weights * (1.0 / total)).astype(bf16)
            att[pl.ds(pl.multiple_of(s * HD, HD), HD), first:last] = product(
                value[:, :last], low, NN
            ).astype(bf16)
            logs[s, :, first:last] = peak + jnp.log(total)
        return carry

    half = slots * 5 // 7
    lax.fori_loop(0, half, head, 0)
    serve(late, rows * 1 // 8)
    lax.fori_loop(half, slots, head, 0)
    keep_out(att, att_f)
    keep_out(logs, logs_f)

    share = Share(p, part, core_in, side_out, side_in, share_s, share_r)
    fill_partial(part, ofull, att, cols, rows, width)
    share.start()
    share.middle()
    serve(late, rows * 2 // 8)
    share.arrive()

    def first_pass(d, total):
        value = tok_own[d].astype(f32) + share.total(d) + vecs[d, :, 2:3]
        resid[d] = value
        return total

    lax.fori_loop(0, rows, first_pass, 0)
    keep_out(resid, resid_f)
    mean, scale = norm_scale(rows, width, lambda d: resid[d])

    def third(d, carry):
        value = (resid[d] - mean) * scale
        normed[d] = (value * vecs[d, :, 3:4] + vecs[d, :, 4:5]).astype(bf16)
        return carry

    lax.fori_loop(0, rows, third, 0)
    spread_n = Spread(p, normed, n2, width, ns, nr)
    spread_n.start()
    serve(late, rows * 3 // 8)
    red_cot.arrive()
    spread_n.forward()
    spread_c = Spread(p, cot_own, cfull, width, ys, yr)
    spread_c.start()
    serve(late, rows * 4 // 8)
    spread_n.finish()
    keep_out(n2, n2_f)
    keep_out(cot_own, cot_own_f)
    serve(late, rows * 5 // 8)
    spread_c.forward()
    serve(late, rows * 6 // 8)
    spread_c.finish()
    keep_out(cfull, cot_f)
    serve(late, rows)
    keep_out(ufull, wu_f)

    def up(first, size):
        value = summed(ufull, n2, rows, first, size) + bias_up[pl.ds(first, size)]
        cube = 0.7978845608 * (value + 0.044715 * value * value * value)
        bend = jnp.tanh(cube)
        hidden[pl.ds(first, size)] = (0.5 * value * (1.0 + bend)).astype(bf16)
        slope = 0.7978845608 * (1.0 + 3.0 * 0.044715 * value * value)
        gp[pl.ds(first, size)] = (
            0.5 * (1.0 + bend) + 0.5 * value * (1.0 - bend * bend) * slope
        ).astype(bf16)

    tiled(ffc, 256, up)
    keep_out(hidden, hidden_f)

    def down(first, size):
        value = summed(dfull, cfull, rows, first, size)
        value = (value * gp[pl.ds(first, size)].astype(f32)).astype(bf16)
        gp[pl.ds(first, size)] = value

    tiled(ffc, 256, down)
    keep_out(gp, gp_f)
    keep_out(dfull, wd_f)
    for copies in swaps:
        for copy in copies:
            copy.wait_send()
    for copy in vec_copies:
        copy.wait_send()
    for ring in (ring_q, ring_o, ring_u, ring_d):
        ring.finish()
    red_tok.finish()
    red_cot.finish()
    share.finish()
    for copy in outs:
        copy.wait()


def forward(rows, cols, args, shapes):
    feats, width, slots, ffc = shapes
    dma = pltpu.SemaphoreType.DMA
    big = lambda n, t=bf16: pltpu.VMEM((rows, feats, n), t)
    qn, on = slots * CHANNELS, slots * HD
    ch, och = CHANNELS // cols, HD // cols
    outs = [
        ((rows, feats, qn), bf16),
        ((rows, feats, on), bf16),
        ((rows, feats, ffc), bf16),
        ((rows, feats, ffc), bf16),
        ((rows, feats, L), bf16),
        ((qn, L), bf16),
        ((on, L), bf16),
        ((slots, 1, L), f32),
        ((rows, feats, width), f32),
        ((rows, feats, L), bf16),
        ((ffc, L), bf16),
        ((ffc, L), bf16),
        ((rows, feats, L), bf16),
        ((rows, feats, width), bf16),
        ((rows, feats, width), bf16),
        ((rows, feats, 8), f32),
    ]
    scratch = [
        big(qn), big(on), big(ffc), big(ffc),
        pltpu.VMEM((feats, qn), bf16), pltpu.VMEM((feats, on), bf16),
        pltpu.VMEM((cols, feats, slots * ch), bf16),
        pltpu.VMEM((cols, feats, slots * och), bf16),
        pltpu.VMEM((cols, 8, slots * ch), bf16),
        pltpu.VMEM((8, qn), bf16),
        pltpu.VMEM((rows, 8, feats), f32),
        big(8, f32),
        big(L), big(L),
        pltpu.VMEM((qn, L), bf16), pltpu.VMEM((on, L), bf16), pltpu.VMEM((slots, 1, L), f32),
        big(width, f32), big(width), big(L),
        pltpu.VMEM((ffc, L), bf16), pltpu.VMEM((ffc, L), bf16),
        big(L), big(width), big(width),
    ]
    scratch += share_scratch(rows, cols, feats, width)
    scratch += [dma((2 * rows,))] * 8
    scratch += [dma((rows + 1,)), dma((rows,))] * 2
    scratch += spread_sems(cols) * 3
    scratch += [dma((3, cols)), dma((3, cols)), dma((rows,)), dma((rows,)), dma((24,))]
    return call(
        functools.partial(forward_kernel, rows, cols),
        outs,
        scratch,
        args,
        1,
        ANY,
        in_specs=[ANY] * 8 + [VMEM],
        out_specs=[ANY] * 16,
    )


def back_one_kernel(
    rows, cols, ready, w_up, grad_pre, cot, hidden, cot_own, resid, vec, w_down, normed_mid,
    grad_down, grad_up, grad_mid, branch, part_out, parts, branch_own, *scratch,
):
    p = Place(rows, cols)
    width = resid.shape[-1]
    half = grad_up.shape[1]
    share = Share(p, *scratch[:6])
    gather = Spread(p, branch_own, branch, width, *scratch[6:8])
    down = Reduce(p, cot, hidden, scratch[8:11], middle(hidden.shape[0], 0)).into(grad_down)
    up = Reduce(
        p, normed_mid, grad_pre.at[pl.ds(0, half)], scratch[11:14], middle(half, 0)
    ).into(grad_up)
    queue = steps(rows, down, up)
    at = lambda t: rows * t // 8
    meet(p.col_peers() + p.row_peers())
    ready("w_up", "grad_pre")
    fill_partial(share.part, w_up, grad_pre, cols, rows, width)
    share.start()
    ready("cot", "hidden", "normed_mid")
    serve(queue, 0)
    share.middle()
    serve(queue, at(1))
    ready("cot_own", "resid", "vec", "w_down")
    serve(queue, at(2))
    share.arrive()

    def store(d, value):
        total = cot_own[d].astype(f32) + value
        grad_mid[d] = total
        low = total.astype(bf16)
        branch_own[d] = low
        parts[d, :, 4:5] = jnp.sum(low.astype(f32), axis=1, keepdims=True)
        parts[d, :, 5:6] = jnp.sum(cot_own[d].astype(f32), axis=1, keepdims=True)

    parts[...] = jnp.zeros_like(parts)

    def put(d, gain, shift):
        parts[d, :, 2:3] = gain
        parts[d, :, 3:4] = shift

    norm_back(
        rows,
        width,
        lambda d: share.total(d),
        lambda d: resid[d],
        lambda d: vec[d, :, 3:4],
        store,
        put,
    )
    gather.start()
    serve(queue, at(3))
    fill_partial(part_out, w_down, hidden, cols, rows, width)
    serve(queue, at(4))
    gather.forward()
    serve(queue, rows)
    down.finish()
    up.finish()
    share.finish()
    gather.finish()


def back_two_kernel(
    rows, cols, ready, part_out, normed_mid, grad_pre, w_out, branch, att, qkv, logs, resid,
    vec, normed_in, w_qkv, own, late_mid, parts,
    grad_up, wq_o, wo_o, bias_o, units_o, feat_o, res_out, res_tok,
    grad_tok, grad_qkv, grad_att, dkey, dval, lead_sum, rest_sum, out_sum, gq, go, gb,
    units, units_in, qkv_in, output, feat, feat_in, feat_sum, feat_cols,
    bs, br, ts, tr, es, er, fs, fr, us, ur, ws, wr, loc, *scratch,
):
    p = Place(rows, cols)
    width = own.shape[-1]
    slots = logs.shape[0]
    ch, och = CHANNELS // cols, HD // cols
    ffc = grad_pre.shape[0]
    half = grad_up.shape[1]
    qn = slots * CHANNELS
    share = Share(p, *scratch[:6])
    lead = slots * 4 // 7
    up = Reduce(
        p, normed_mid, grad_pre.at[pl.ds(ffc - half, half)], scratch[6:9], middle(half, 0)
    ).into(grad_up)
    out = Reduce(p, branch, att, scratch[9:12], middle(slots * HD, 1)).into(out_sum)
    wide = [
        Reduce(
            p,
            normed_in,
            grad_qkv.at[pl.ds(first * CHANNELS, count * CHANNELS)],
            scratch[i : i + 3],
            middle(count * CHANNELS, 0),
        ).into(total)
        for first, count, i, total in (
            (0, lead, 12, lead_sum),
            (lead, slots - lead, 15, rest_sum),
        )
    ]
    early = steps(rows, up, out)
    late = steps(rows, *wide)
    at = lambda t: rows * t // 8
    share_out = Share(p, scratch[0], scratch[18], scratch[2], *scratch[19:22])
    part_copy = pltpu.make_async_copy(part_out, scratch[0], loc.at[3])
    grad_mid = resid
    mid_copy = pltpu.make_async_copy(late_mid, grad_mid, loc.at[4])
    part_copy.start()
    back_out = Back(p, output, res_out, (bs, br))
    back_tok = Back(p, grad_tok, res_tok, (ts, tr))
    sources = [(q, back_out.col) for q in range(rows)]
    targets = [home(p, q) for q in range(rows)]
    meet(sources + targets + all_col(p) + all_row(p))
    part_copy.wait()
    share_out.start()
    ready("normed_mid", "grad_pre", "branch", "att")
    serve(early, 0)
    share_out.middle()
    ready("w_out", "qkv", "logs")
    for s in range(slots):
        total = product(w_out[0, :, s * HD : (s + 1) * HD], branch[0], TN)
        for d in range(1, rows):
            total = total + product(w_out[d, :, s * HD : (s + 1) * HD], branch[d], TN)
        grad_att[s * HD : (s + 1) * HD] = total.astype(bf16)

    def head(s, carry):
        base = pl.multiple_of(s * CHANNELS, 64)

        def store(row, first, last, value):
            grad_qkv[pl.ds(base + row, HD), first:last] = value.astype(bf16)

        attend_back(
            qkv[pl.ds(base, CHANNELS)],
            grad_att[pl.ds(pl.multiple_of(s * HD, 64), HD)],
            logs[s],
            store,
            dkey,
            dval,
        )
        return carry

    serve(early, at(1))
    lax.fori_loop(0, lead // 2, head, 0)
    serve(early, at(2))
    lax.fori_loop(lead // 2, lead, head, 0)
    serve(early, at(3))
    ready("normed_in")
    wide[0].step(0)
    ready("resid", "vec")
    share_out.arrive()

    def result(d, carry):
        output[d] = (resid[d] + share_out.total(d) + vec[d, :, 5:6]).astype(bf16)
        return carry

    lax.fori_loop(0, rows, result, 0)
    back_out.start()
    share_out.finish()
    mid_copy.start()
    late.pop(0)
    lax.fori_loop(lead, slots, head, 0)
    serve(early, at(4))
    serve(late, 0)
    ready("w_qkv", "own", "parts")
    mid_copy.wait()
    fill_partial(share.part, w_qkv, grad_qkv, cols, rows, width)
    share.start()
    serve(early, at(5))
    serve(late, at(1))
    ones = jnp.ones((8, L), bf16)
    units[:, :ffc] = product(ones, grad_pre[...], NT)[0:1]
    units[:, ffc:] = product(ones, grad_qkv[...], NT)[0:1]
    row_units = []
    for o, peer in enumerate(all_row(p)):
        row_units.append(remote(units, units_in.at[o + 1], us.at[o], ur.at[o], peer))
    for copy in row_units:
        copy.start()
    share.middle()
    serve(early, at(6))
    serve(late, at(2))
    serve(early, rows)
    for j in range(cols):
        for s in range(slots):
            base = s * HD + j * och
            go[j, :, s * och : (s + 1) * och] = out_sum[:, base : base + och]
    swap_o = exchange_copies(p, go, wo_o, es.at[0], er.at[0])
    for copy in swap_o:
        copy.start()
    serve(late, at(3))
    share.arrive()

    def store_tokens(d, value):
        grad_tok[d] = (grad_mid[d] + value).astype(bf16)

    def put(d, gain, shift):
        parts[d, :, 0:1] = gain
        parts[d, :, 1:2] = shift

    norm_back(
        rows,
        width,
        lambda d: share.total(d),
        lambda d: own[d].astype(f32),
        lambda d: vec[d, :, 0:1],
        store_tokens,
        put,
    )
    back_tok.start()
    serve(late, at(4))
    eye = (
        lax.broadcasted_iota(jnp.int32, (8, 8), 0) == lax.broadcasted_iota(jnp.int32, (8, 8), 1)
    ).astype(f32)
    for d in range(rows):
        feat[d] = lax.dot_general(
            eye, parts[d], NT, precision=lax.Precision.HIGHEST, preferred_element_type=f32
        )
    feats = []
    for o in range(1, rows):
        to = lax.rem(p.r + o, rows)
        feats.append(remote(feat.at[to], feat_in.at[o], fs.at[o], fr.at[o], (to, p.c)))
    for copy in feats:
        copy.start()
    serve(late, at(5))
    total = units[...]
    for o, copy in enumerate(row_units):
        copy.wait_recv()
        total = total + units_in[o + 1]
    units_o[...] = total[:, :ffc]
    qkv_in[...] = total[:, ffc:]
    for j in range(cols):
        for s in range(slots):
            base = s * CHANNELS + j * ch
            gb[j, :, s * ch : (s + 1) * ch] = qkv_in[:, base : base + ch]
    swap_b = exchange_copies(p, gb, bias_o, es.at[1], er.at[1])
    for copy in swap_b:
        copy.start()
    serve(late, at(6))
    total = feat[p.r]
    for o, copy in enumerate(feats):
        copy.wait_recv()
        total = total + feat_in[o + 1]
    feat_sum[...] = total
    sums = [
        remote(feat_sum, feat_cols.at[o + 1], ws.at[o], wr.at[o], peer)
        for o, peer in enumerate(all_col(p))
    ]
    for copy in sums:
        copy.start()
    serve(late, rows)
    for j in range(cols):
        for s in range(slots):
            base = (s if s < lead else s - lead) * CHANNELS + j * ch
            source = lead_sum if s < lead else rest_sum
            gq[j, :, s * ch : (s + 1) * ch] = source[:, base : base + ch]
    for ring in [up, out] + wide:
        ring.finish()
    swap_q = exchange_copies(p, gq, wq_o, es.at[2], er.at[2])
    for copy in swap_q:
        copy.start()
    keeps = [
        pltpu.make_async_copy(src.at[p.c], dst.at[p.c], loc.at[i])
        for i, (src, dst) in enumerate(((gq, wq_o), (go, wo_o), (gb, bias_o)))
    ]
    for copy in keeps:
        copy.start()
    for o, copy in enumerate(sums):
        copy.wait_recv()
        total = total + feat_cols[o + 1]
    feat_o[...] = total
    share.finish()
    back_out.finish()
    back_tok.finish()
    for copy in swap_o + swap_b + swap_q:
        copy.wait()
    for copy in keeps:
        copy.wait()
    for copy in row_units + feats + sums:
        copy.wait_send()


RAW = ("part_out", "late_mid")
INPUTS = {
    back_one_kernel: (
        "w_up", "grad_pre", "cot", "hidden", "cot_own", "resid", "vec", "w_down", "normed_mid",
    ),
    back_two_kernel: (
        "part_out", "normed_mid", "grad_pre", "w_out", "branch", "att", "qkv", "logs", "resid",
        "vec", "normed_in", "w_qkv", "own", "late_mid", "parts",
    ),
}


def call(kernel, outs, scratch, args, collective, spec=VMEM, in_specs=None, out_specs=None):
    return pl.pallas_call(
        kernel,
        out_shape=[jax.ShapeDtypeStruct(s, t) for s, t in outs],
        in_specs=[spec] * len(args) if in_specs is None else in_specs,
        out_specs=[spec] * len(outs) if out_specs is None else out_specs,
        scratch_shapes=scratch,
        compiler_params=pltpu.CompilerParams(
            collective_id=collective, has_side_effects=True, vmem_limit_bytes=LIMIT
        ),
    )(*args)


def staged(kernel, count, *refs):
    rows, cols, outs = count
    names = INPUTS[kernel]
    ins = len(names)
    rest = list(refs[ins + outs :])
    buffers = [refs[i] if name in RAW else rest.pop(0) for i, name in enumerate(names)]
    sem = rest.pop(0)
    copies = {
        name: pltpu.make_async_copy(refs[i], buffers[i], sem.at[i])
        for i, name in enumerate(names)
        if name not in RAW
    }
    for name in copies:
        copies[name].start()

    def ready(*names):
        for name in names:
            copies[name].wait()

    kernel(rows, cols, ready, *buffers, *refs[ins : ins + outs], *rest)


def call_staged(kernel, rows, cols, outs, scratch, args, collective):
    return call(
        functools.partial(staged, kernel, (rows, cols, len(outs))),
        outs,
        [
            pltpu.VMEM(arg.shape, arg.dtype)
            for name, arg in zip(INPUTS[kernel], args)
            if name not in RAW
        ]
        + [pltpu.SemaphoreType.DMA((len(args),))]
        + scratch,
        args,
        collective,
        in_specs=[ANY] * len(args),
    )


def one_hot(target, size):
    return (target[:, None] == jnp.arange(size, dtype=jnp.int32)[None, :]).astype(bf16)


def split_matrix(channels, slots, cols):
    source = jnp.arange(channels * H, dtype=jnp.int32)
    channel, head = source // H, source % H
    return one_hot(
        ((head % cols) * slots + head // cols) * channels + channel, cols * slots * channels
    )


def to_owners(weight, matrix, cols):
    moved = product(weight, matrix, NN).astype(bf16)
    return moved.reshape(moved.shape[0], cols, -1).transpose(1, 0, 2)


def from_owners(blocks, matrix):
    flat = blocks.transpose(1, 0, 2).reshape(blocks.shape[1], -1)
    return product(flat, matrix, NT)


def body(
    tokens, ln1_gain, ln1_shift, weight_qkv, bias_qkv, weight_out, bias_out, ln2_gain,
    ln2_shift, weight_up, bias_up, weight_down, bias_down, cotangent,
):
    rows, cols = lax.axis_size("row"), lax.axis_size("col")
    slots = (H + cols - 1) // cols
    ch, och = CHANNELS // cols, HD // cols
    feats = D // rows
    width = L // cols
    ffc = weight_up.shape[1]
    dma = pltpu.SemaphoreType.DMA

    qkv_split, out_split = split_matrix(ch, slots, cols), split_matrix(och, slots, cols)
    wq = to_owners(weight_qkv, qkv_split, cols)
    wo = to_owners(weight_out, out_split, cols)
    bias = jnp.pad(bias_qkv.reshape(ch, H), ((0, 0), (0, slots * cols - H)))
    bias = bias.reshape(ch, slots, cols).transpose(2, 1, 0).reshape(cols, 1, slots * ch)
    terms = []
    for _ in range(3):
        terms.append(lax.reduce_precision(bias, 8, 7))
        bias = bias - terms[-1]
    bias = jnp.concatenate(terms + [jnp.zeros_like(bias)] * 5, axis=1).astype(bf16)
    zero = jnp.zeros_like(ln1_gain)
    vec = jnp.stack(
        [ln1_gain, ln1_shift, bias_out, ln2_gain, ln2_shift, bias_down, zero, zero]
    )
    (
        w_qkv, w_out, w_up, w_down, normed_in, qkv, att, logs, resid, normed_mid, hidden,
        grad_pre, cot, tok_own, cot_own, vec,
    ) = forward(
        rows,
        cols,
        (tokens, cotangent, wq, wo, bias, vec, weight_up, weight_down, bias_up[:, None]),
        (feats, width, slots, ffc),
    )
    half = ffc // 2 // 128 * 128
    grad_weight_down, grad_up_one, grad_mid, branch, part_out, parts = call_staged(
        back_one_kernel,
        rows,
        cols,
        [
            ((feats, ffc), f32),
            ((feats, half), f32),
            ((rows, feats, width), f32),
            ((rows, feats, L), bf16),
            ((cols, rows, feats, width), bf16),
            ((rows, feats, 8), f32),
        ],
        [pltpu.VMEM((rows, feats, width), bf16)]
        + share_scratch(rows, cols, feats, width)
        + spread_sems(cols)
        + reduce_scratch(rows, feats, ffc)
        + reduce_scratch(rows, feats, half),
        (w_up, grad_pre, cot, hidden, cot_own, resid, vec, w_down, normed_mid),
        3,
    )
    qn, on = slots * CHANNELS, slots * HD
    vm = pltpu.VMEM
    lead = slots * 4 // 7 * CHANNELS
    (
        grad_up_two, gq, go, gb, grad_bias_up, feat, res_out, res_tok
    ) = call_staged(
        back_two_kernel,
        rows,
        cols,
        [
            ((feats, ffc - half), f32),
            ((cols, feats, slots * ch), bf16),
            ((cols, feats, slots * och), bf16),
            ((cols, 1, slots * ch), f32),
            ((1, ffc), f32),
            ((8, feats), f32),
            ((feats, rows * width), bf16),
            ((feats, rows * width), bf16),
        ],
        [
            vm((rows, feats, width), bf16),
            vm((qn, L), bf16),
            vm((on, L), bf16),
            vm((HD, L), f32),
            vm((HD, L), f32),
            vm((feats, lead), bf16),
            vm((feats, qn - lead), bf16),
            vm((feats, on), bf16),
            vm((cols, feats, slots * ch), bf16),
            vm((cols, feats, slots * och), bf16),
            vm((cols, 1, slots * ch), f32),
            vm((1, ffc + qn), f32),
            vm((rows, 1, ffc + qn), f32),
            vm((1, qn), f32),
            vm((rows, feats, width), bf16),
            vm((rows, 8, feats), f32),
            vm((rows, 8, feats), f32),
            vm((8, feats), f32),
            vm((cols, 8, feats), f32),
        ]
        + [dma((rows + 1,)), dma((rows,))] * 2
        + [dma((3, cols)), dma((3, cols))]
        + [dma((rows,))] * 4
        + [dma((cols,))] * 2
        + [dma((5,))]
        + share_scratch(rows, cols, feats, width)
        + reduce_scratch(rows, feats, ffc - half)
        + reduce_scratch(rows, feats, on)
        + reduce_scratch(rows, feats, lead)
        + reduce_scratch(rows, feats, qn - lead)
        + [share_scratch(rows, cols, feats, width)[i] for i in (1, 3, 4, 5)],
        (
            part_out, normed_mid, grad_pre, w_out, branch, att, qkv, logs, resid,
            vec, normed_in, w_qkv, tok_own, grad_mid, parts,
        ),
        4,
    )
    grad_weight_up = jnp.concatenate([grad_up_one, grad_up_two], axis=1)
    grad_weight_qkv = from_owners(gq, qkv_split)
    grad_weight_out = from_owners(go, out_split)
    grad_bias_qkv = gb.reshape(cols, slots, ch).transpose(2, 1, 0)
    grad_bias_qkv = grad_bias_qkv.reshape(ch, slots * cols)[:, :H].reshape(-1)
    return (
        res_out,
        res_tok.astype(f32),
        feat[0],
        feat[1],
        grad_weight_qkv,
        grad_bias_qkv,
        grad_weight_out,
        feat[4],
        feat[2],
        feat[3],
        grad_weight_up,
        grad_bias_up[0],
        grad_weight_down,
        feat[5],
    )


def solution(mesh):
    both, row, col = P("row", "col"), P("row"), P("col")
    in_specs = (both, row, row, both, col, both, row, row, row, both, col, both, row, both)
    out_specs = (both, both, row, row, both, col, both, row, row, row, both, col, both, row)
    return jax.shard_map(body, mesh=mesh, in_specs=in_specs, out_specs=out_specs, check_vma=False)
```

time: 850 us -> 558 us (0.66)
  waiting for transfers between devices: 204 us -> 0 us
  matrix products: 54 us -> 6.5 us
  Pallas kernels: 508 us -> 526 us
  local copies, waits for them, and re-layouts: 28.8 us -> 13.4 us
  other arithmetic: 20.2 us -> 5.28 us
  between operations: 14.7 us -> 1.33 us
  blocking collectives: 10.8 us -> 0 us
    all_gather x4 -> x0, waiting for transfers between devices: 203 us -> none  [whole_weight(): return lax.all_gather(weight, 'row', axis=0, tiled=True)]
    dot_general x11 -> x4, matrix products: 54 us -> 6.5 us  [product(): return lax.dot_general(left, right, dims, preferred_element_type=f32)]
    pallas_call x5 -> x3, Pallas kernels: 491 us -> 526 us  [call(): pl.pallas_call(kernel, out_shape=[jax.ShapeDtypeStruct(s, t) for s, t in...]
    pallas_call x1 -> x0, Pallas kernels: 17.7 us -> none  [attend(): pl.pallas_call(attend_kernel, grid=(slots,), out_shape=[jax.ShapeDtypeStr...]
    all_gather x1 -> x0, blocking collectives: 10.8 us -> none  [body(): grads = lax.all_gather(units[ffc:].reshape(slots, cols, ch), 'col', axis=0)]
    reduce_sum x5 -> x0, other arithmetic: 9.74 us -> none  [the longest x1 2.84 us: body(): jnp.mean(centred * centred, axis=0, keepdims=True) + epsilon]
  transfers between devices with their start and end apart: 4 -> 0, of which waited for: 4 -> 0; matrix products, arithmetic and copies ran while one was open for 5% -> 0% of each run, Pallas kernels for 9% -> 0%
where the time goes in v3:
time: 558 us; the launch traced here: 552 us
  Pallas kernels  526 us (94%)
  local copies, waits for them, and re-layouts  13.4 us (2%)
  matrix products  6.5 us (1%)
    pallas_call x3, Pallas kernels, call(): pl.pallas_call(kernel, out_shape=[jax.ShapeDtypeStruct(s, t) for s, t in...  526 us

profile of v3, /device:TPU:9, one launch (start us, length us, event | category | flops | bytes accessed | tf_op | source)
XLA Modules:
  0.0 552.4 jit_solution(9110123055260584385)
XLA Ops:
  0.6 0.0 copy-start
  0.7 0.1 pad.10.clone
  0.8 1.4 stack.31.vec
  2.2 0.8 reshape.202
  3.0 0.1 copy.51
  3.2 0.1 reshape.204
  3.3 0.7 maximum_maximum_fusion.bias
  4.0 1.3 fusion.6
  5.3 0.2 reshape.201
  5.5 0.7 copy.61
  6.2 0.0 copy-done
  6.2 0.0 copy-start.7
  6.2 1.5 fusion.5
  7.7 0.6 reshape.200
  8.3 0.9 copy.60
  9.2 0.0 copy-done.7
  9.2 1.2 broadcast_in_dim.3.bias_up
  10.4 268.3 %shard_map.245 = (bf16[8,200,1344]{2,1,0:T(8,128)(2,1)}, bf16[8,200,448]{2,1,0:T(8,128)(2,1)}, bf16[8,200,1600]{2,1,0:T(8,128)(2,1)}, bf16[8,200,1600]{2,1,0:T(8...) custom-call(bf16[200,2048]{1,0:T(8,128)(2,1)} %tok.1, ...), custom_call_target="tpu_custom_call" | custom-call | tf_op jit(solution)/shard_map/pallas_call | solution.py:1147
  278.8 92.9 %shard_map.246 = (f32[200,1600]{1,0:T(8,128)}, f32[200,768]{1,0:T(8,128)}, f32[8,200,256]{2,1,0:T(8,128)}, bf16[8,200,1024]{2,1,0:T(8,128)(2,1)}, bf16[4,8,200,2...) custom-call(bf16[8,200,1600]{2,1,0:T(8,128)(2,1)} %get-tuple-element.44.refs_0_, ...), custom_call_target="tpu_custom_call" | custom-call | tf_op jit(solution)/shard_map/pallas_call | solution.py:1147
  371.6 164.6 %shard_map.247 = (f32[200,832]{1,0:T(8,128)}, bf16[4,200,336]{2,1,0:T(8,128)(2,1)}, bf16[4,200,112]{2,1,0:T(8,128)(2,1)}, f32[4,1,336]{2,1,0:T(1,128)}, f32[1,16...) custom-call(bf16[4,8,200,256]{3,2,1,0:T(8,128)(2,1)} %get-tuple-element.53.refs_0_, ...), custom_call_target="tpu_custom_call" | custom-call | tf_op jit(solution)/shard_map/pallas_call | solution.py:1147
  536.3 0.7 reduce
  537.0 1.3 reduce.1
  538.3 1.5 fusion.43
  539.8 0.1 reshape.206
  539.9 0.1 copy.49
  540.0 0.7 reshape.208
  540.7 1.0 copy.50
  541.8 0.2 reshape.209
  541.9 1.2 fusion.7
  543.1 1.3 copy.47
  544.4 0.0 copy-start.5
  544.4 0.0 copy-start.6
  544.5 0.4 reshape.205
  544.9 0.0 copy-start.4
  544.9 2.5 fusion
  547.4 0.0 copy-done.5
  547.4 0.0 copy-done.6
  547.4 0.0 copy-start.3
  547.4 0.0 copy-start.2
  547.4 1.2 pad_maximum_fusion
  548.6 0.0 copy-done.4
  548.6 0.0 copy-start.1
  548.6 1.3 convert_element_type.24
  549.9 0.0 copy-done.3
  549.9 0.9 copy.64
  550.8 0.0 copy-done.2
  550.8 1.1 copy.65
  551.9 0.0 copy-done.1
  (13 shorter events, 0.1 us)
Async XLA Ops:
  0.6 5.5 %copy-start = (bf16[200,1200]{1,0:T(8,128)(2,1)S(1)}, bf16[200,1200]{1,0:T(8,128)(2,1)}, u32[]{:S(2)}) copy-start(bf16[200,1200]{1,0:T(8,128)(2,1)} %param.17) | copy-start | bytes 1440004
  6.2 3.1 copy-start.7
  544.4 3.0 copy-start.5
  544.4 3.0 copy-start.6
  544.9 3.7 copy-start.4
  547.4 2.5 copy-start.3
  547.4 3.4 copy-start.2
  548.6 3.3 copy-start.1

commit v4 on v3

--- a/solution.py
+++ b/solution.py
@@ -216,7 +216,7 @@
     ]
 
 
-def fill_partial(part, weight, act, cols, rows, width):
+def fill_partial(part, weight, act, cols, rows, width, between=lambda: None):
     def one(d, carry):
         for j in range(cols):
             part[j, d] = product(
@@ -224,7 +224,9 @@
             ).astype(bf16)
         return carry
 
-    lax.fori_loop(0, rows, one, 0)
+    lax.fori_loop(0, rows // 2, one, 0)
+    between()
+    lax.fori_loop(rows // 2, rows, one, 0)
 
 
 def middle(size, extra):
@@ -289,6 +291,12 @@
     while queue and queue[0][1] <= t:
         ring, at = queue.pop(0)
         ring.step(at)
+
+
+def take(queue, count):
+    for ring, at in queue[:count]:
+        ring.step(at)
+    del queue[:count]
 
 
 def home(p, q):
@@ -660,8 +668,9 @@
         vecs[d] = lax.dot_general(
             vin[d], eye, TN, precision=lax.Precision.HIGHEST, preferred_element_type=f32
         )
+    serve(early, rows * 2 // 8)
+    serve(early, rows * 3 // 8)
     spread_x.forward()
-    serve(early, rows * 2 // 8)
     spread_x.finish()
     outs = []
 
@@ -673,7 +682,7 @@
     keep_out(tok_own, tok_own_f)
     keep_out(vecs, vec_f)
     mean, scale = norm_scale(rows, L, lambda d: xfull[d].astype(f32))
-    serve(early, rows * 3 // 8)
+    serve(early, rows * 4 // 8)
 
     def normal(d, carry):
         value = (xfull[d].astype(f32) - mean) * scale
@@ -684,8 +693,8 @@
     keep_out(n1, n1_f)
 
     serve(early, rows - 2)
+    red_cot.start()
     serve(late, 0)
-    red_cot.start()
     serve(early, rows)
     keep_out(qfull, wq_f)
     keep_out(ofull, wo_f)
@@ -718,16 +727,25 @@
 
     half = slots * 5 // 7
     lax.fori_loop(0, half, head, 0)
-    serve(late, rows * 1 // 8)
+    red_cot.arrive()
+    spread_c = Spread(p, cot_own, cfull, width, ys, yr)
+    spread_c.start()
     lax.fori_loop(half, slots, head, 0)
+    take(late, 1)
     keep_out(att, att_f)
     keep_out(logs, logs_f)
 
     share = Share(p, part, core_in, side_out, side_in, share_s, share_r)
     fill_partial(part, ofull, att, cols, rows, width)
     share.start()
+    take(late, 1)
     share.middle()
-    serve(late, rows * 2 // 8)
+    spread_c.forward()
+    take(late, 1)
+    keep_out(cot_own, cot_own_f)
+    spread_c.finish()
+    keep_out(cfull, cot_f)
+    take(late, 2)
     share.arrive()
 
     def first_pass(d, total):
@@ -747,21 +765,11 @@
     lax.fori_loop(0, rows, third, 0)
     spread_n = Spread(p, normed, n2, width, ns, nr)
     spread_n.start()
-    serve(late, rows * 3 // 8)
-    red_cot.arrive()
+    take(late, 3)
     spread_n.forward()
-    spread_c = Spread(p, cot_own, cfull, width, ys, yr)
-    spread_c.start()
-    serve(late, rows * 4 // 8)
     spread_n.finish()
     keep_out(n2, n2_f)
-    keep_out(cot_own, cot_own_f)
-    serve(late, rows * 5 // 8)
-    spread_c.forward()
-    serve(late, rows * 6 // 8)
-    spread_c.finish()
-    keep_out(cfull, cot_f)
-    serve(late, rows)
+    take(late, len(late) - 1)
     keep_out(ufull, wu_f)
 
     def up(first, size):
@@ -775,6 +783,8 @@
         ).astype(bf16)
 
     tiled(ffc, 256, up)
+    take(late, 1)
+    keep_out(dfull, wd_f)
     keep_out(hidden, hidden_f)
 
     def down(first, size):
@@ -784,7 +794,6 @@
 
     tiled(ffc, 256, down)
     keep_out(gp, gp_f)
-    keep_out(dfull, wd_f)
     for copies in swaps:
         for copy in copies:
             copy.wait_send()
@@ -856,8 +865,8 @@
 
 
 def back_one_kernel(
-    rows, cols, ready, w_up, grad_pre, cot, hidden, cot_own, resid, vec, w_down, normed_mid,
-    grad_down, grad_up, grad_mid, branch, part_out, parts, branch_own, *scratch,
+    rows, cols, ready, cot, hidden, normed_mid, grad_pre, w_up, cot_own, resid, vec, w_down,
+    grad_down, grad_up, grad_mid, branch, output, parts, branch_own, *scratch,
 ):
     p = Place(rows, cols)
     width = resid.shape[-1]
@@ -868,18 +877,22 @@
     up = Reduce(
         p, normed_mid, grad_pre.at[pl.ds(0, half)], scratch[11:14], middle(half, 0)
     ).into(grad_up)
+    share_out = Share(p, scratch[0], scratch[14], scratch[2], *scratch[15:18])
     queue = steps(rows, down, up)
     at = lambda t: rows * t // 8
     meet(p.col_peers() + p.row_peers())
-    ready("w_up", "grad_pre")
-    fill_partial(share.part, w_up, grad_pre, cols, rows, width)
+    ready("cot", "hidden", "normed_mid", "grad_pre")
+    take(queue, 2)
+    ready("w_up")
+    fill_partial(
+        share.part, w_up, grad_pre, cols, rows, width, lambda: take(queue, 1)
+    )
     share.start()
-    ready("cot", "hidden", "normed_mid")
-    serve(queue, 0)
+    take(queue, 1)
     share.middle()
-    serve(queue, at(1))
     ready("cot_own", "resid", "vec", "w_down")
     serve(queue, at(2))
+    serve(queue, at(3))
     share.arrive()
 
     def store(d, value):
@@ -906,23 +919,33 @@
         put,
     )
     gather.start()
-    serve(queue, at(3))
-    fill_partial(part_out, w_down, hidden, cols, rows, width)
+    share.finish()
     serve(queue, at(4))
+    fill_partial(share_out.part, w_down, hidden, cols, rows, width)
+    share_out.start()
+    serve(queue, at(5))
+    share_out.middle()
     gather.forward()
     serve(queue, rows)
+    share_out.arrive()
+
+    def result(d, carry):
+        output[d] = (resid[d] + share_out.total(d) + vec[d, :, 5:6]).astype(bf16)
+        return carry
+
+    lax.fori_loop(0, rows, result, 0)
     down.finish()
     up.finish()
-    share.finish()
+    share_out.finish()
     gather.finish()
 
 
 def back_two_kernel(
-    rows, cols, ready, part_out, normed_mid, grad_pre, w_out, branch, att, qkv, logs, resid,
-    vec, normed_in, w_qkv, own, late_mid, parts,
+    rows, cols, ready, output, normed_mid, grad_pre, w_out, branch, att, qkv, logs,
+    vec, normed_in, w_qkv, own, grad_mid, parts,
     grad_up, wq_o, wo_o, bias_o, units_o, feat_o, res_out, res_tok,
     grad_tok, grad_qkv, grad_att, dkey, dval, lead_sum, rest_sum, out_sum, gq, go, gb,
-    units, units_in, qkv_in, output, feat, feat_in, feat_sum, feat_cols,
+    units, units_in, qkv_in, feat, feat_in, feat_sum, feat_cols,
     bs, br, ts, tr, es, er, fs, fr, us, ur, ws, wr, loc, *scratch,
 ):
     p = Place(rows, cols)
@@ -954,21 +977,14 @@
     early = steps(rows, up, out)
     late = steps(rows, *wide)
     at = lambda t: rows * t // 8
-    share_out = Share(p, scratch[0], scratch[18], scratch[2], *scratch[19:22])
-    part_copy = pltpu.make_async_copy(part_out, scratch[0], loc.at[3])
-    grad_mid = resid
-    mid_copy = pltpu.make_async_copy(late_mid, grad_mid, loc.at[4])
-    part_copy.start()
     back_out = Back(p, output, res_out, (bs, br))
     back_tok = Back(p, grad_tok, res_tok, (ts, tr))
     sources = [(q, back_out.col) for q in range(rows)]
     targets = [home(p, q) for q in range(rows)]
     meet(sources + targets + all_col(p) + all_row(p))
-    part_copy.wait()
-    share_out.start()
+    back_out.start()
     ready("normed_mid", "grad_pre", "branch", "att")
     serve(early, 0)
-    share_out.middle()
     ready("w_out", "qkv", "logs")
     for s in range(slots):
         total = product(w_out[0, :, s * HD : (s + 1) * HD], branch[0], TN)
@@ -992,34 +1008,29 @@
         )
         return carry
 
+    third = lead * 3 // 4
+    lax.fori_loop(0, third, head, 0)
     serve(early, at(1))
-    lax.fori_loop(0, lead // 2, head, 0)
+    lax.fori_loop(third, lead, head, 0)
+    ready("normed_in")
+    take(late, 1)
     serve(early, at(2))
-    lax.fori_loop(lead // 2, lead, head, 0)
+    most = lead + (slots - lead) // 2
+    lax.fori_loop(lead, most, head, 0)
     serve(early, at(3))
-    ready("normed_in")
-    wide[0].step(0)
-    ready("resid", "vec")
-    share_out.arrive()
-
-    def result(d, carry):
-        output[d] = (resid[d] + share_out.total(d) + vec[d, :, 5:6]).astype(bf16)
-        return carry
-
-    lax.fori_loop(0, rows, result, 0)
-    back_out.start()
-    share_out.finish()
-    mid_copy.start()
-    late.pop(0)
-    lax.fori_loop(lead, slots, head, 0)
+    lax.fori_loop(most, slots, head, 0)
     serve(early, at(4))
-    serve(late, 0)
-    ready("w_qkv", "own", "parts")
-    mid_copy.wait()
-    fill_partial(share.part, w_qkv, grad_qkv, cols, rows, width)
+    take(late, 1)
+    ready("w_qkv", "own", "parts", "vec", "grad_mid")
+    fill_partial(
+        share.part, w_qkv, grad_qkv, cols, rows, width, lambda: serve(early, at(5))
+    )
     share.start()
-    serve(early, at(5))
-    serve(late, at(1))
+    serve(early, at(6))
+    take(late, 1)
+    share.middle()
+    serve(early, rows)
+    take(late, 1)
     ones = jnp.ones((8, L), bf16)
     units[:, :ffc] = product(ones, grad_pre[...], NT)[0:1]
     units[:, ffc:] = product(ones, grad_qkv[...], NT)[0:1]
@@ -1028,10 +1039,8 @@
         row_units.append(remote(units, units_in.at[o + 1], us.at[o], ur.at[o], peer))
     for copy in row_units:
         copy.start()
-    share.middle()
-    serve(early, at(6))
     serve(late, at(2))
-    serve(early, rows)
+    serve(late, at(3))
     for j in range(cols):
         for s in range(slots):
             base = s * HD + j * och
@@ -1039,7 +1048,7 @@
     swap_o = exchange_copies(p, go, wo_o, es.at[0], er.at[0])
     for copy in swap_o:
         copy.start()
-    serve(late, at(3))
+    serve(late, at(4))
     share.arrive()
 
     def store_tokens(d, value):
@@ -1058,8 +1067,6 @@
         store_tokens,
         put,
     )
-    back_tok.start()
-    serve(late, at(4))
     eye = (
         lax.broadcasted_iota(jnp.int32, (8, 8), 0) == lax.broadcasted_iota(jnp.int32, (8, 8), 1)
     ).astype(f32)
@@ -1074,6 +1081,8 @@
     for copy in feats:
         copy.start()
     serve(late, at(5))
+    serve(late, rows - 2)
+    back_tok.start()
     total = units[...]
     for o, copy in enumerate(row_units):
         copy.wait_recv()
@@ -1087,7 +1096,6 @@
     swap_b = exchange_copies(p, gb, bias_o, es.at[1], er.at[1])
     for copy in swap_b:
         copy.start()
-    serve(late, at(6))
     total = feat[p.r]
     for o, copy in enumerate(feats):
         copy.wait_recv()
@@ -1131,14 +1139,14 @@
         copy.wait_send()
 
 
-RAW = ("part_out", "late_mid")
+RAW = ("output",)
 INPUTS = {
     back_one_kernel: (
-        "w_up", "grad_pre", "cot", "hidden", "cot_own", "resid", "vec", "w_down", "normed_mid",
+        "cot", "hidden", "normed_mid", "grad_pre", "w_up", "cot_own", "resid", "vec", "w_down",
     ),
     back_two_kernel: (
-        "part_out", "normed_mid", "grad_pre", "w_out", "branch", "att", "qkv", "logs", "resid",
-        "vec", "normed_in", "w_qkv", "own", "late_mid", "parts",
+        "output", "normed_mid", "grad_pre", "w_out", "branch", "att", "qkv", "logs",
+        "vec", "normed_in", "w_qkv", "own", "grad_mid", "parts",
     ),
 }
 
@@ -1253,7 +1261,7 @@
         (feats, width, slots, ffc),
     )
     half = ffc // 2 // 128 * 128
-    grad_weight_down, grad_up_one, grad_mid, branch, part_out, parts = call_staged(
+    grad_weight_down, grad_up_one, grad_mid, branch, output, parts = call_staged(
         back_one_kernel,
         rows,
         cols,
@@ -1262,15 +1270,16 @@
             ((feats, half), f32),
             ((rows, feats, width), f32),
             ((rows, feats, L), bf16),
-            ((cols, rows, feats, width), bf16),
+            ((rows, feats, width), bf16),
             ((rows, feats, 8), f32),
         ],
         [pltpu.VMEM((rows, feats, width), bf16)]
         + share_scratch(rows, cols, feats, width)
         + spread_sems(cols)
         + reduce_scratch(rows, feats, ffc)
-        + reduce_scratch(rows, feats, half),
-        (w_up, grad_pre, cot, hidden, cot_own, resid, vec, w_down, normed_mid),
+        + reduce_scratch(rows, feats, half)
+        + [share_scratch(rows, cols, feats, width)[i] for i in (1, 3, 4, 5)],
+        (cot, hidden, normed_mid, grad_pre, w_up, cot_own, resid, vec, w_down),
         3,
     )
     qn, on = slots * CHANNELS, slots * HD
@@ -1307,7 +1316,6 @@
             vm((1, ffc + qn), f32),
             vm((rows, 1, ffc + qn), f32),
             vm((1, qn), f32),
-            vm((rows, feats, width), bf16),
             vm((rows, 8, feats), f32),
             vm((rows, 8, feats), f32),
             vm((8, feats), f32),
@@ -1317,15 +1325,14 @@
         + [dma((3, cols)), dma((3, cols))]
         + [dma((rows,))] * 4
         + [dma((cols,))] * 2
-        + [dma((5,))]
+        + [dma((3,))]
         + share_scratch(rows, cols, feats, width)
         + reduce_scratch(rows, feats, ffc - half)
         + reduce_scratch(rows, feats, on)
         + reduce_scratch(rows, feats, lead)
-        + reduce_scratch(rows, feats, qn - lead)
-        + [share_scratch(rows, cols, feats, width)[i] for i in (1, 3, 4, 5)],
+        + reduce_scratch(rows, feats, qn - lead),
         (
-            part_out, normed_mid, grad_pre, w_out, branch, att, qkv, logs, resid,
+            output, normed_mid, grad_pre, w_out, branch, att, qkv, logs,
             vec, normed_in, w_qkv, tok_own, grad_mid, parts,
         ),
         4,

time: 558 us -> 521 us (0.934)
  Pallas kernels: 526 us -> 491 us
    pallas_call x3, Pallas kernels: 526 us -> 491 us  [call(): pl.pallas_call(kernel, out_shape=[jax.ShapeDtypeStruct(s, t) for s, t in...]
where the time goes in v4:
time: 521 us; the launch traced here: 517 us
  Pallas kernels  491 us (94%)
  local copies, waits for them, and re-layouts  12.7 us (2%)
  matrix products  6.5 us (1%)
  other arithmetic  5.36 us (1%)
    pallas_call x3, Pallas kernels, call(): pl.pallas_call(kernel, out_shape=[jax.ShapeDtypeStruct(s, t) for s, t in...  491 us

profile of v4, /device:TPU:9, one launch (start us, length us, event | category | flops | bytes accessed | tf_op | source)
XLA Modules:
  0.0 517.0 jit_solution(1937758329623706770)
XLA Ops:
  0.6 0.0 copy-start
  0.7 0.1 pad.10.clone
  0.8 1.4 stack.31.vec
  2.2 0.8 reshape.202
  3.0 0.1 copy.51
  3.2 0.1 reshape.204
  3.3 0.7 maximum_maximum_fusion.bias
  4.0 1.3 fusion.6
  5.3 0.2 reshape.201
  5.5 0.7 copy.61
  6.2 0.0 copy-done
  6.2 1.5 fusion.5
  7.7 0.0 copy-start.8
  7.7 0.6 reshape.200
  8.3 0.9 copy.60
  9.2 0.0 copy-done.8
  9.2 1.2 broadcast_in_dim.3.bias_up
  10.4 258.6 %shard_map.245 = (bf16[8,200,1344]{2,1,0:T(8,128)(2,1)}, bf16[8,200,448]{2,1,0:T(8,128)(2,1)}, bf16[8,200,1600]{2,1,0:T(8,128)(2,1)}, bf16[8,200,1600]{2,1,0:T(8...) custom-call(bf16[200,2048]{1,0:T(8,128)(2,1)} %tok.1, ...), custom_call_target="tpu_custom_call" | custom-call | tf_op jit(solution)/shard_map/pallas_call | solution.py:1155
  269.0 87.5 %shard_map.246 = (f32[200,1600]{1,0:T(8,128)}, f32[200,768]{1,0:T(8,128)}, f32[8,200,256]{2,1,0:T(8,128)}, bf16[8,200,1024]{2,1,0:T(8,128)(2,1)}, bf16[8,200,256]{2,1,0:T(8,128)(2,1)}, /*index=5*/f32[8,200,8]{2,1,0:T(8,128)}) custom-call(bf16[8,200,1024]{2,1,0:T(8,128)(2,1)} %get-tuple-element.44.refs_0_, bf16[1600,1024]{1,0:T(8,128)(2,1)} %get-tuple-element.45.refs_1_, ...), custom_call_target="tpu_custom_call" | custom-call | tf_op jit(solution)/shard_map/pallas_call | solution.py:1155
  356.5 145.0 %shard_map.247 = (f32[200,832]{1,0:T(8,128)}, bf16[4,200,336]{2,1,0:T(8,128)(2,1)}, bf16[4,200,112]{2,1,0:T(8,128)(2,1)}, f32[4,1,336]{2,1,0:T(1,128)}, f32[1,16...) custom-call(bf16[8,200,256]{2,1,0:T(8,128)(2,1)} %get-tuple-element.53.refs_0_, ...), custom_call_target="tpu_custom_call" | custom-call | tf_op jit(solution)/shard_map/pallas_call | solution.py:1155
  501.6 0.0 copy-start.7
  501.6 0.8 reduce
  502.4 1.3 reduce.1
  503.7 1.5 fusion.43
  505.2 0.1 reshape.206
  505.3 0.1 copy.49
  505.4 0.7 reshape.208
  506.1 1.0 copy.50
  507.1 0.2 reshape.209
  507.3 1.2 fusion.7
  508.5 0.0 copy-done.7
  508.5 0.2 copy.47
  508.7 0.4 reshape.205
  509.2 0.0 copy-start.5
  509.2 0.0 copy-start.6
  509.2 2.5 fusion
  511.7 0.0 copy-done.5
  511.7 0.0 copy-done.6
  511.7 0.0 copy-start.4
  511.7 1.2 pad_maximum_fusion
  512.8 0.3 copy-done.4
  513.2 0.0 copy-start.3
  513.2 0.0 copy-start.2
  513.2 1.4 convert_element_type.24
  514.5 0.0 copy-done.3
  514.5 0.0 copy-start.1
  514.5 0.9 copy.64
  515.4 0.0 copy-done.2
  515.4 1.1 copy.65
  516.5 0.0 copy-done.1
  (13 shorter events, 0.1 us)
Async XLA Ops:
  0.6 5.5 %copy-start = (bf16[200,1200]{1,0:T(8,128)(2,1)S(1)}, bf16[200,1200]{1,0:T(8,128)(2,1)}, u32[]{:S(2)}) copy-start(bf16[200,1200]{1,0:T(8,128)(2,1)} %param.17) | copy-start | bytes 1440004
  7.7 1.5 copy-start.8
  501.6 6.9 %copy-start.7 = (bf16[4,200,336]{2,1,0:T(8,128)(2,1)S(1)}, bf16[4,200,336]{2,1,0:T(8,128)(2,1)}, u32[]{:S(2)}) copy-start(bf16[4,200,336]{2,1,0:T(8,128)(2,1)} %get-tuple-element.67) | copy-start | bytes 1612804
  509.2 2.5 copy-start.5
  509.2 2.5 copy-start.6
  511.7 1.5 copy-start.4
  513.2 1.4 copy-start.3
  513.2 2.3 copy-start.2
  514.5 2.0 copy-start.1

commit v5 on v4

--- a/solution.py
+++ b/solution.py
@@ -300,13 +300,17 @@
 
 
 def home(p, q):
-    block = p.c * p.R + q
-    return (block // p.C, lax.rem(block, p.C))
+    half = p.X // 2
+    place = (q // p.C * half + p.x // 2) * 2 + p.k
+    return (place * 2 + lax.rem(p.k + p.x, 2), lax.rem(q, p.C))
 
 
 def own_block(p):
-    block = p.r * p.C + p.c
-    return block // p.R, lax.rem(block, p.R)
+    half = p.X // 2
+    k = lax.rem(p.a, 2)
+    pair = p.a // 2
+    x = lax.rem(pair, half) * 2 + lax.rem(p.b + k, 2)
+    return x * 2 + k, pair // half * p.C + p.c
 
 
 def equal(left, right):
@@ -596,7 +600,7 @@
     tok, cot, wq, wo, bias, vec, wu, wd, bias_up,
     wq_f, wo_f, wu_f, wd_f, n1_f, qkv_f, att_f, logs_f, resid_f, n2_f, hidden_f, gp_f,
     cot_f, tok_own_f, cot_own_f, vec_f,
-    qfull, ofull, ufull, dfull, qown, oown, qin, oin, bin_, qbias, vin, vecs,
+    qfull, ofull, ufull, dfull, qown, oown, qout, oout, qin, oin, bin_, qbias, vin, vecs,
     xfull, n1, qkv, att, logs, resid, normed, n2, hidden, gp, cfull, tok_own, cot_own,
     part, core_in, side_out, side_in, share_s, share_r,
     qs, qr, os_, or_, us, ur, ds0, dr0, ts, tr, cs, cr,
@@ -612,8 +616,12 @@
     sources = [(q, red_tok.col) for q in range(rows)]
     targets = [home(p, q) for q in range(rows)]
     meet(sources + targets + all_col(p) + all_row(p))
-
-    groups = ((wq, qin), (wo, oin), (bias, bin_))
+    red_tok.start()
+    for src, dst in ((wq, qout), (wo, oout)):
+        block = dst.shape[-1]
+        for j in range(cols):
+            dst[j] = src[:, j * block : (j + 1) * block]
+    groups = ((qout, qin), (oout, oin), (bias, bin_))
     swaps = []
     for i, (src, dst) in enumerate(groups):
         swaps.append(exchange_copies(p, src, dst, es.at[i], er.at[i]))
@@ -627,7 +635,6 @@
     keeps.append(pltpu.make_async_copy(vec, vin.at[p.r], loc.at[3]))
     for copy in keeps:
         copy.start()
-    red_tok.start()
     vec_copies = [
         remote(vec, vin.at[p.r], vs.at[o], vr.at[o], peer)
         for o, peer in enumerate(all_row(p))
@@ -837,6 +844,8 @@
         pltpu.VMEM((feats, qn), bf16), pltpu.VMEM((feats, on), bf16),
         pltpu.VMEM((cols, feats, slots * ch), bf16),
         pltpu.VMEM((cols, feats, slots * och), bf16),
+        pltpu.VMEM((cols, feats, slots * ch), bf16),
+        pltpu.VMEM((cols, feats, slots * och), bf16),
         pltpu.VMEM((cols, 8, slots * ch), bf16),
         pltpu.VMEM((8, qn), bf16),
         pltpu.VMEM((rows, 8, feats), f32),
@@ -859,7 +868,7 @@
         args,
         1,
         ANY,
-        in_specs=[ANY] * 8 + [VMEM],
+        in_specs=[ANY, ANY, VMEM, VMEM, ANY, ANY, ANY, ANY, VMEM],
         out_specs=[ANY] * 16,
     )
 
@@ -941,10 +950,10 @@
 
 
 def back_two_kernel(
-    rows, cols, ready, output, normed_mid, grad_pre, w_out, branch, att, qkv, logs,
+    rows, cols, ready, output, up_one, normed_mid, grad_pre, w_out, branch, att, qkv, logs,
     vec, normed_in, w_qkv, own, grad_mid, parts,
-    grad_up, wq_o, wo_o, bias_o, units_o, feat_o, res_out, res_tok,
-    grad_tok, grad_qkv, grad_att, dkey, dval, lead_sum, rest_sum, out_sum, gq, go, gb,
+    grad_up_all, wq_o, wo_o, bias_o, units_o, feat_o, res_out, res_f32,
+    grad_up, res_tok, grad_tok, grad_qkv, grad_att, dkey, dval, lead_sum, rest_sum, out_sum, gq, go, gb,
     units, units_in, qkv_in, feat, feat_in, feat_sum, feat_cols,
     bs, br, ts, tr, es, er, fs, fr, us, ur, ws, wr, loc, *scratch,
 ):
@@ -983,6 +992,10 @@
     targets = [home(p, q) for q in range(rows)]
     meet(sources + targets + all_col(p) + all_row(p))
     back_out.start()
+    one_copy = pltpu.make_async_copy(
+        up_one, grad_up_all.at[:, : ffc - half], loc.at[3]
+    )
+    one_copy.start()
     ready("normed_mid", "grad_pre", "branch", "att")
     serve(early, 0)
     ready("w_out", "qkv", "logs")
@@ -1118,6 +1131,10 @@
     swap_q = exchange_copies(p, gq, wq_o, es.at[2], er.at[2])
     for copy in swap_q:
         copy.start()
+    two_copy = pltpu.make_async_copy(
+        grad_up, grad_up_all.at[:, ffc - half :], loc.at[4]
+    )
+    two_copy.start()
     keeps = [
         pltpu.make_async_copy(src.at[p.c], dst.at[p.c], loc.at[i])
         for i, (src, dst) in enumerate(((gq, wq_o), (go, wo_o), (gb, bias_o)))
@@ -1131,6 +1148,9 @@
     share.finish()
     back_out.finish()
     back_tok.finish()
+    res_f32[...] = res_tok[...].astype(f32)
+    one_copy.wait()
+    two_copy.wait()
     for copy in swap_o + swap_b + swap_q:
         copy.wait()
     for copy in keeps:
@@ -1139,13 +1159,13 @@
         copy.wait_send()
 
 
-RAW = ("output",)
+RAW = ("output", "up_one")
 INPUTS = {
     back_one_kernel: (
         "cot", "hidden", "normed_mid", "grad_pre", "w_up", "cot_own", "resid", "vec", "w_down",
     ),
     back_two_kernel: (
-        "output", "normed_mid", "grad_pre", "w_out", "branch", "att", "qkv", "logs",
+        "output", "up_one", "normed_mid", "grad_pre", "w_out", "branch", "att", "qkv", "logs",
         "vec", "normed_in", "w_qkv", "own", "grad_mid", "parts",
     ),
 }
@@ -1186,7 +1206,7 @@
     kernel(rows, cols, ready, *buffers, *refs[ins : ins + outs], *rest)
 
 
-def call_staged(kernel, rows, cols, outs, scratch, args, collective):
+def call_staged(kernel, rows, cols, outs, scratch, args, collective, out_specs=None):
     return call(
         functools.partial(staged, kernel, (rows, cols, len(outs))),
         outs,
@@ -1200,6 +1220,7 @@
         args,
         collective,
         in_specs=[ANY] * len(args),
+        out_specs=out_specs,
     )
 
 
@@ -1215,9 +1236,8 @@
     )
 
 
-def to_owners(weight, matrix, cols):
-    moved = product(weight, matrix, NN).astype(bf16)
-    return moved.reshape(moved.shape[0], cols, -1).transpose(1, 0, 2)
+def to_owners(weight, matrix):
+    return product(weight, matrix, NN).astype(bf16)
 
 
 def from_owners(blocks, matrix):
@@ -1238,8 +1258,8 @@
     dma = pltpu.SemaphoreType.DMA
 
     qkv_split, out_split = split_matrix(ch, slots, cols), split_matrix(och, slots, cols)
-    wq = to_owners(weight_qkv, qkv_split, cols)
-    wo = to_owners(weight_out, out_split, cols)
+    wq = to_owners(weight_qkv, qkv_split)
+    wo = to_owners(weight_out, out_split)
     bias = jnp.pad(bias_qkv.reshape(ch, H), ((0, 0), (0, slots * cols - H)))
     bias = bias.reshape(ch, slots, cols).transpose(2, 1, 0).reshape(cols, 1, slots * ch)
     terms = []
@@ -1286,22 +1306,24 @@
     vm = pltpu.VMEM
     lead = slots * 4 // 7 * CHANNELS
     (
-        grad_up_two, gq, go, gb, grad_bias_up, feat, res_out, res_tok
+        grad_weight_up, gq, go, gb, grad_bias_up, feat, res_out, res_tok
     ) = call_staged(
         back_two_kernel,
         rows,
         cols,
         [
-            ((feats, ffc - half), f32),
+            ((feats, ffc), f32),
             ((cols, feats, slots * ch), bf16),
             ((cols, feats, slots * och), bf16),
             ((cols, 1, slots * ch), f32),
             ((1, ffc), f32),
             ((8, feats), f32),
             ((feats, rows * width), bf16),
-            ((feats, rows * width), bf16),
+            ((feats, rows * width), f32),
         ],
         [
+            vm((feats, ffc - half), f32),
+            vm((feats, rows * width), bf16),
             vm((rows, feats, width), bf16),
             vm((qn, L), bf16),
             vm((on, L), bf16),
@@ -1325,26 +1347,26 @@
         + [dma((3, cols)), dma((3, cols))]
         + [dma((rows,))] * 4
         + [dma((cols,))] * 2
-        + [dma((3,))]
+        + [dma((5,))]
         + share_scratch(rows, cols, feats, width)
         + reduce_scratch(rows, feats, ffc - half)
         + reduce_scratch(rows, feats, on)
         + reduce_scratch(rows, feats, lead)
         + reduce_scratch(rows, feats, qn - lead),
         (
-            output, normed_mid, grad_pre, w_out, branch, att, qkv, logs,
+            output, grad_up_one, normed_mid, grad_pre, w_out, branch, att, qkv, logs,
             vec, normed_in, w_qkv, tok_own, grad_mid, parts,
         ),
         4,
-    )
-    grad_weight_up = jnp.concatenate([grad_up_one, grad_up_two], axis=1)
+        [ANY] + [VMEM] * 5 + [ANY, VMEM],
+    )
     grad_weight_qkv = from_owners(gq, qkv_split)
     grad_weight_out = from_owners(go, out_split)
     grad_bias_qkv = gb.reshape(cols, slots, ch).transpose(2, 1, 0)
     grad_bias_qkv = grad_bias_qkv.reshape(ch, slots * cols)[:, :H].reshape(-1)
     return (
         res_out,
-        res_tok.astype(f32),
+        res_tok,
         feat[0],
         feat[1],
         grad_weight_qkv,

time: 521 us -> 490 us (0.940)
  Pallas kernels: 491 us -> 461 us
    pallas_call x3, Pallas kernels: 491 us -> 461 us  [call(): pl.pallas_call(kernel, out_shape=[jax.ShapeDtypeStruct(s, t) for s, t in...]
where the time goes in v5:
time: 490 us; the launch traced here: 487 us
  Pallas kernels  461 us (94%)
  local copies, waits for them, and re-layouts  13.2 us (3%)
  matrix products  8 us (2%)
    pallas_call x3, Pallas kernels, call(): pl.pallas_call(kernel, out_shape=[jax.ShapeDtypeStruct(s, t) for s, t in...  461 us

profile of v5, /device:TPU:9, one launch (start us, length us, event | category | flops | bytes accessed | tf_op | source)
XLA Modules:
  0.0 486.6 jit_solution(16597664423163104802)
XLA Ops:
  0.6 0.0 copy-start
  0.7 0.1 pad.8.clone
  0.8 1.4 stack.31.vec
  2.2 0.8 reshape.194
  3.0 0.1 copy.47
  3.2 0.1 reshape.196
  3.3 0.7 maximum_maximum_fusion.bias
  4.0 2.0 fusion.6.wo
  6.0 0.0 copy-done
  6.0 0.0 copy-start.6
  6.0 2.3 fusion.5.wq
  8.3 0.0 copy-done.6
  8.3 1.2 broadcast_in_dim.3.bias_up
  9.5 224.6 %shard_map.245 = (bf16[8,200,1344]{2,1,0:T(8,128)(2,1)}, bf16[8,200,448]{2,1,0:T(8,128)(2,1)}, bf16[8,200,1600]{2,1,0:T(8,128)(2,1)}, bf16[8,200,1600]{2,1,0:T(8...) custom-call(bf16[200,2048]{1,0:T(8,128)(2,1)} %tok.1, ...), custom_call_target="tpu_custom_call" | custom-call | tf_op jit(solution)/shard_map/pallas_call | solution.py:1175
  234.1 91.9 %shard_map.246 = (f32[200,1600]{1,0:T(8,128)}, f32[200,768]{1,0:T(8,128)}, f32[8,200,256]{2,1,0:T(8,128)}, bf16[8,200,1024]{2,1,0:T(8,128)(2,1)}, bf16[8,200,256]{2,1,0:T(8,128)(2,1)}, /*index=5*/f32[8,200,8]{2,1,0:T(8,128)}) custom-call(bf16[8,200,1024]{2,1,0:T(8,128)(2,1)} %get-tuple-element.44.refs_0_, bf16[1600,1024]{1,0:T(8,128)(2,1)} %get-tuple-element.45.refs_1_, ...), custom_call_target="tpu_custom_call" | custom-call | tf_op jit(solution)/shard_map/pallas_call | solution.py:1175
  326.1 144.9 %shard_map.247 = (f32[200,1600]{1,0:T(8,128)}, bf16[4,200,336]{2,1,0:T(8,128)(2,1)}, bf16[4,200,112]{2,1,0:T(8,128)(2,1)}, f32[4,1,336]{2,1,0:T(1,128)}, f32[1,1...) custom-call(bf16[8,200,256]{2,1,0:T(8,128)(2,1)} %get-tuple-element.53.refs_0_, ...), custom_call_target="tpu_custom_call" | custom-call | tf_op jit(solution)/shard_map/pallas_call | solution.py:1175
  471.0 0.7 reduce
  471.7 1.3 reduce.1
  473.0 1.5 fusion.43
  474.5 0.1 reshape.198
  474.6 0.1 copy.45
  474.7 0.7 reshape.200
  475.4 1.0 copy.46
  476.5 0.2 reshape.201
  476.6 1.2 fusion.7
  477.8 1.3 copy.43
  479.1 0.0 copy-start.5
  479.2 0.4 reshape.197
  479.6 0.0 copy-start.2
  479.6 2.5 fusion
  482.1 0.0 copy-done.5
  482.1 0.0 copy-start.4
  482.1 0.9 copy.58
  483.0 0.0 copy-done.2
  483.0 0.0 copy-start.3
  483.0 0.0 copy-start.1
  483.0 1.2 copy.59
  484.2 0.0 copy-done.4
  484.2 1.1 copy.60
  485.2 0.0 copy-done.3
  485.2 1.1 copy.61
  486.3 0.0 copy-done.1
  (13 shorter events, 0.1 us)
Async XLA Ops:
  0.6 5.3 %copy-start = (bf16[200,1200]{1,0:T(8,128)(2,1)S(1)}, bf16[200,1200]{1,0:T(8,128)(2,1)}, u32[]{:S(2)}) copy-start(bf16[200,1200]{1,0:T(8,128)(2,1)} %param.17) | copy-start | bytes 1440004
  6.0 2.3 copy-start.6
  479.1 3.0 copy-start.5
  479.6 3.4 copy-start.2
  482.1 2.1 copy-start.4
  483.0 2.2 copy-start.3
  483.0 3.3 copy-start.1

commit v6 on v5

--- a/solution.py
+++ b/solution.py
@@ -230,12 +230,19 @@
 
 
 def middle(size, extra):
-    return min((size // 256 + extra) * 128, (size - 1) // 128 * 128)
+    return min(max((size // 256 + extra) * 128, 128), (size - 1) // 128 * 128)
+
+
+def where(condition, act):
+    if condition is None:
+        act()
+    else:
+        pl.when(condition)(act)
 
 
 class Reduce:
-    def __init__(self, p, left, right, scratch, cut):
-        self.p, self.left, self.right = p, left, right
+    def __init__(self, p, left, right, scratch, cut, only=None):
+        self.p, self.left, self.right, self.only = p, left, right, only
         self.slots, self.send, self.recv = scratch
         self.parts = (slice(0, cut), slice(cut, self.slots.shape[-1]))
 
@@ -251,6 +258,9 @@
         )
 
     def step(self, t):
+        where(self.only, lambda: self.run(t))
+
+    def run(self, t):
         p = self.p
         for way in range(2):
             part = self.parts[way]
@@ -270,6 +280,9 @@
         return self
 
     def finish(self):
+        where(self.only, self.end)
+
+    def end(self):
         for way in range(2):
             for t in range(self.p.R - 1):
                 self.copy(way, t).wait_send()
@@ -455,10 +468,12 @@
 
 
 class Ring:
-    def __init__(self, p, own, full, sems, cut):
-        self.p, self.own, self.full = p, own, full
+    def __init__(self, p, own, full, sems, cut, first=0, last=None, only=None):
+        self.p, self.own, self.full, self.only = p, own, full, only
         self.send, self.recv = sems
-        self.parts = (slice(0, cut), slice(cut, own.shape[1]))
+        last = own.shape[1] if last is None else last
+        self.span = slice(first, last)
+        self.parts = (slice(first, cut), slice(cut, last))
 
     def copy(self, way, t):
         p = self.p
@@ -475,10 +490,15 @@
 
     def local(self):
         return pltpu.make_async_copy(
-            self.own, self.full.at[self.p.r], self.send.at[self.p.R - 1]
+            self.own.at[:, self.span],
+            self.full.at[self.p.r, :, self.span],
+            self.send.at[self.p.R - 1],
         )
 
     def step(self, t):
+        where(self.only, lambda: self.run(t))
+
+    def run(self, t):
         if t == 0:
             self.local().start()
         for way in range(2):
@@ -490,6 +510,9 @@
             self.local().wait()
 
     def finish(self):
+        where(self.only, self.end)
+
+    def end(self):
         for way in range(2):
             for t in range(self.p.R - 1):
                 self.copy(way, t).wait_send()
@@ -603,7 +626,7 @@
     qfull, ofull, ufull, dfull, qown, oown, qout, oout, qin, oin, bin_, qbias, vin, vecs,
     xfull, n1, qkv, att, logs, resid, normed, n2, hidden, gp, cfull, tok_own, cot_own,
     part, core_in, side_out, side_in, share_s, share_r,
-    qs, qr, os_, or_, us, ur, ds0, dr0, ts, tr, cs, cr,
+    qs, qr, zs, zr, os_, or_, us, ur, ds0, dr0, ts, tr, cs, cr,
     xs, xr, ys, yr, ns, nr, es, er, vs, vr, loc,
 ):
     p = Place(rows, cols)
@@ -654,11 +677,23 @@
             qbias[:, base : base + ch] = bin_[j, :, s * ch : (s + 1) * ch]
             base = s * HD + j * och
             oown[:, base : base + och] = oin[j, :, s * och : (s + 1) * och]
-    ring_q = Ring(p, qown, qfull, (qs, qr), middle(slots * CHANNELS, 0))
+    tail = (slots - 1) * CHANNELS // 128 * 128
+    filled = (slots - 1) * cols + p.c < H
+    exact = tail == (slots - 1) * CHANNELS
+    ring_q = Ring(p, qown, qfull, (qs, qr), middle(tail, 0), 0, tail)
+    ring_t = Ring(
+        p, qown, qfull, (zs, zr), tail + 128, tail, None, filled if exact else None
+    )
+    if exact:
+
+        @pl.when(jnp.logical_not(filled))
+        def _():
+            qfull[:, :, tail:] = jnp.zeros((rows, qfull.shape[1], CHANNELS), bf16)
+
     ring_o = Ring(p, oown, ofull, (os_, or_), middle(slots * HD, 1))
     ring_u = Ring(p, wu, ufull, (us, ur), middle(ffc, 0))
     ring_d = Ring(p, wd, dfull, (ds0, dr0), middle(ffc, 1))
-    early = steps(rows, ring_q, ring_o)
+    early = steps(rows, ring_q, ring_t, ring_o)
     late = steps(rows, ring_u, ring_d)
     serve(early, 0)
     red_tok.arrive()
@@ -806,7 +841,7 @@
             copy.wait_send()
     for copy in vec_copies:
         copy.wait_send()
-    for ring in (ring_q, ring_o, ring_u, ring_d):
+    for ring in (ring_q, ring_t, ring_o, ring_u, ring_d):
         ring.finish()
     red_tok.finish()
     red_cot.finish()
@@ -857,7 +892,7 @@
         big(L), big(width), big(width),
     ]
     scratch += share_scratch(rows, cols, feats, width)
-    scratch += [dma((2 * rows,))] * 8
+    scratch += [dma((2 * rows,))] * 10
     scratch += [dma((rows + 1,)), dma((rows,))] * 2
     scratch += spread_sems(cols) * 3
     scratch += [dma((3, cols)), dma((3, cols)), dma((rows,)), dma((rows,)), dma((24,))]
@@ -953,7 +988,7 @@
     rows, cols, ready, output, up_one, normed_mid, grad_pre, w_out, branch, att, qkv, logs,
     vec, normed_in, w_qkv, own, grad_mid, parts,
     grad_up_all, wq_o, wo_o, bias_o, units_o, feat_o, res_out, res_f32,
-    grad_up, res_tok, grad_tok, grad_qkv, grad_att, dkey, dval, lead_sum, rest_sum, out_sum, gq, go, gb,
+    grad_up, res_tok, grad_tok, grad_qkv, grad_att, dkey, dval, lead_sum, rest_sum, last_sum, out_sum, gq, go, gb,
     units, units_in, qkv_in, feat, feat_in, feat_sum, feat_cols,
     bs, br, ts, tr, es, er, fs, fr, us, ur, ws, wr, loc, *scratch,
 ):
@@ -970,6 +1005,7 @@
         p, normed_mid, grad_pre.at[pl.ds(ffc - half, half)], scratch[6:9], middle(half, 0)
     ).into(grad_up)
     out = Reduce(p, branch, att, scratch[9:12], middle(slots * HD, 1)).into(out_sum)
+    filled = (slots - 1) * cols + p.c < H
     wide = [
         Reduce(
             p,
@@ -977,12 +1013,15 @@
             grad_qkv.at[pl.ds(first * CHANNELS, count * CHANNELS)],
             scratch[i : i + 3],
             middle(count * CHANNELS, 0),
+            only,
         ).into(total)
-        for first, count, i, total in (
-            (0, lead, 12, lead_sum),
-            (lead, slots - lead, 15, rest_sum),
+        for first, count, i, total, only in (
+            (0, lead, 12, lead_sum, None),
+            (lead, slots - 1 - lead, 15, rest_sum, None),
+            (slots - 1, 1, 18, last_sum, filled),
         )
     ]
+    last_sum[...] = jnp.zeros_like(last_sum)
     early = steps(rows, up, out)
     late = steps(rows, *wide)
     at = lambda t: rows * t // 8
@@ -1033,7 +1072,7 @@
     serve(early, at(3))
     lax.fori_loop(most, slots, head, 0)
     serve(early, at(4))
-    take(late, 1)
+    take(late, 2)
     ready("w_qkv", "own", "parts", "vec", "grad_mid")
     fill_partial(
         share.part, w_qkv, grad_qkv, cols, rows, width, lambda: serve(early, at(5))
@@ -1043,7 +1082,7 @@
     take(late, 1)
     share.middle()
     serve(early, rows)
-    take(late, 1)
+    take(late, 2)
     ones = jnp.ones((8, L), bf16)
     units[:, :ffc] = product(ones, grad_pre[...], NT)[0:1]
     units[:, ffc:] = product(ones, grad_qkv[...], NT)[0:1]
@@ -1123,8 +1162,10 @@
     serve(late, rows)
     for j in range(cols):
         for s in range(slots):
-            base = (s if s < lead else s - lead) * CHANNELS + j * ch
-            source = lead_sum if s < lead else rest_sum
+            source, first = lead_sum, 0
+            if s >= lead:
+                source, first = (rest_sum, lead) if s < slots - 1 else (last_sum, slots - 1)
+            base = (s - first) * CHANNELS + j * ch
             gq[j, :, s * ch : (s + 1) * ch] = source[:, base : base + ch]
     for ring in [up, out] + wide:
         ring.finish()
@@ -1330,7 +1371,8 @@
             vm((HD, L), f32),
             vm((HD, L), f32),
             vm((feats, lead), bf16),
-            vm((feats, qn - lead), bf16),
+            vm((feats, qn - CHANNELS - lead), bf16),
+            vm((feats, CHANNELS), bf16),
             vm((feats, on), bf16),
             vm((cols, feats, slots * ch), bf16),
             vm((cols, feats, slots * och), bf16),
@@ -1352,7 +1394,8 @@
         + reduce_scratch(rows, feats, ffc - half)
         + reduce_scratch(rows, feats, on)
         + reduce_scratch(rows, feats, lead)
-        + reduce_scratch(rows, feats, qn - lead),
+        + reduce_scratch(rows, feats, qn - CHANNELS - lead)
+        + reduce_scratch(rows, feats, CHANNELS),
         (
             output, grad_up_one, normed_mid, grad_pre, w_out, branch, att, qkv, logs,
             vec, normed_in, w_qkv, tok_own, grad_mid, parts,

time: 490 us -> 482 us (0.984)
  Pallas kernels: 461 us -> 453 us
    pallas_call x3, Pallas kernels: 461 us -> 453 us  [call(): pl.pallas_call(kernel, out_shape=[jax.ShapeDtypeStruct(s, t) for s, t in...]
where the time goes in v6:
time: 482 us; the launch traced here: 478 us
  Pallas kernels  453 us (94%)
  local copies, waits for them, and re-layouts  13.2 us (3%)
  matrix products  8 us (2%)
    pallas_call x3, Pallas kernels, call(): pl.pallas_call(kernel, out_shape=[jax.ShapeDtypeStruct(s, t) for s, t in...  453 us

profile of v6, /device:TPU:9, one launch (start us, length us, event | category | flops | bytes accessed | tf_op | source)
XLA Modules:
  0.0 478.2 jit_solution(16998108171544032332)
XLA Ops:
  0.6 0.0 copy-start
  0.7 0.1 pad.8.clone
  0.8 1.4 stack.31.vec
  2.2 0.8 reshape.194
  3.0 0.1 copy.47
  3.2 0.1 reshape.196
  3.3 0.7 maximum_maximum_fusion.bias
  4.0 2.0 fusion.6.wo
  6.0 0.0 copy-done
  6.0 0.0 copy-start.6
  6.0 2.3 fusion.5.wq
  8.3 0.0 copy-done.6
  8.3 1.2 broadcast_in_dim.3.bias_up
  9.5 219.9 %shard_map.245 = (bf16[8,200,1344]{2,1,0:T(8,128)(2,1)}, bf16[8,200,448]{2,1,0:T(8,128)(2,1)}, bf16[8,200,1600]{2,1,0:T(8,128)(2,1)}, bf16[8,200,1600]{2,1,0:T(8...) custom-call(bf16[200,2048]{1,0:T(8,128)(2,1)} %tok.1, ...), custom_call_target="tpu_custom_call" | custom-call | tf_op jit(solution)/shard_map/pallas_call | solution.py:1216
  229.4 91.6 %shard_map.246 = (f32[200,1600]{1,0:T(8,128)}, f32[200,768]{1,0:T(8,128)}, f32[8,200,256]{2,1,0:T(8,128)}, bf16[8,200,1024]{2,1,0:T(8,128)(2,1)}, bf16[8,200,256]{2,1,0:T(8,128)(2,1)}, /*index=5*/f32[8,200,8]{2,1,0:T(8,128)}) custom-call(bf16[8,200,1024]{2,1,0:T(8,128)(2,1)} %get-tuple-element.44.refs_0_, bf16[1600,1024]{1,0:T(8,128)(2,1)} %get-tuple-element.45.refs_1_, ...), custom_call_target="tpu_custom_call" | custom-call | tf_op jit(solution)/shard_map/pallas_call | solution.py:1216
  320.9 141.8 %shard_map.247 = (f32[200,1600]{1,0:T(8,128)}, bf16[4,200,336]{2,1,0:T(8,128)(2,1)}, bf16[4,200,112]{2,1,0:T(8,128)(2,1)}, f32[4,1,336]{2,1,0:T(1,128)}, f32[1,1...) custom-call(bf16[8,200,256]{2,1,0:T(8,128)(2,1)} %get-tuple-element.53.refs_0_, ...), custom_call_target="tpu_custom_call" | custom-call | tf_op jit(solution)/shard_map/pallas_call | solution.py:1216
  462.8 0.7 reduce
  463.5 1.3 reduce.1
  464.8 1.5 fusion.43
  466.3 0.1 reshape.198
  466.4 0.1 copy.45
  466.5 0.7 reshape.200
  467.2 1.0 copy.46
  468.2 0.2 reshape.201
  468.4 1.2 fusion.7
  469.6 1.3 copy.43
  470.9 0.0 copy-start.5
  470.9 0.4 reshape.197
  471.4 0.0 copy-start.2
  471.4 2.5 fusion
  473.9 0.0 copy-done.5
  473.9 0.0 copy-start.4
  473.9 0.9 copy.58
  474.8 0.0 copy-done.2
  474.8 0.0 copy-start.3
  474.8 0.0 copy-start.1
  474.8 1.2 copy.59
  475.9 0.0 copy-done.4
  475.9 1.1 copy.60
  477.0 0.0 copy-done.3
  477.0 1.1 copy.61
  478.1 0.0 copy-done.1
  (13 shorter events, 0.1 us)
Async XLA Ops:
  0.6 5.3 %copy-start = (bf16[200,1200]{1,0:T(8,128)(2,1)S(1)}, bf16[200,1200]{1,0:T(8,128)(2,1)}, u32[]{:S(2)}) copy-start(bf16[200,1200]{1,0:T(8,128)(2,1)} %param.17) | copy-start | bytes 1440004
  6.0 2.3 copy-start.6
  470.9 3.0 copy-start.5
  471.4 3.4 copy-start.2
  473.9 2.1 copy-start.4
  474.8 2.2 copy-start.3
  474.8 3.3 copy-start.1
